TPU v7x, 32 devices: a whole 2x2x4 slice. The times are simulated.
32 devices in a mesh: section: 2 (over core), row: 4 (over z), col: 4 (over y, x).
Axes of the slice: x: 2, y: 2, z: 4, core: 2. Of those that a mesh axis runs over, the one named last changes fastest.
Arguments:
- layer_input: bfloat16 [2, 4, 512, 1536], P(None, 'row', None, 'col'), may hold values from -36 to 36
- g_out: float32 [2, 4, 512, 1536], P(None, 'row', None, 'col'), may hold values from -6 to 6
- attn_gain: float32 [2, 1536], P('section', 'col'), may hold values from 0.25 to 1.75
- w_query: bfloat16 [2, 1536, 1536], P('section', 'row', 'col'), may hold values from -0.15625 to 0.15625
- w_keyval: bfloat16 [2, 1536, 512], P('section', 'row', 'col'), may hold values from -0.15625 to 0.15625
- w_out: bfloat16 [2, 1536, 1536], P('section', 'col', 'row'), may hold values from -0.875 to 0.875
- ffn_gain: float32 [2, 1536], P('section', 'col'), may hold values from 0.25 to 1.75
- w_gate: bfloat16 [2, 1536, 8960], P('section', 'row', 'col'), may hold values from -0.15625 to 0.15625
- w_up: bfloat16 [2, 1536, 8960], P('section', 'row', 'col'), may hold values from -0.15625 to 0.15625
- w_down: bfloat16 [2, 8960, 1536], P('section', 'col', 'row'), may hold values from -0.0625 to 0.0625
Outputs:
- acts: bfloat16 [2, 2, 4, 512, 1536], P('section', None, 'row', None, 'col')
- grads_in: bfloat16 [2, 2, 4, 512, 1536], P('section', None, 'row', None, 'col')
- d_attn_gain: float32 [2, 1536], P('section', 'col')
- d_query: float32 [2, 1536, 1536], P('section', 'row', 'col')
- d_keyval: float32 [2, 1536, 512], P('section', 'row', 'col')
- d_out: float32 [2, 1536, 1536], P('section', 'col', 'row')
- d_ffn_gain: float32 [2, 1536], P('section', 'col')
- d_gate: float32 [2, 1536, 8960], P('section', 'row', 'col')
- d_up: float32 [2, 1536, 8960], P('section', 'row', 'col')
- d_down: float32 [2, 8960, 1536], P('section', 'col', 'row')
All inputs are finite; a program needn't handle non-finite values.
Results may differ from a plain program's by a relative error of at most 0.028.
Values may be sent and summed in bfloat16 or wider, within the bound.
No kernel may reach another device: no remote copies, remote signals or barrier semaphores. Data moves between devices by JAX's collectives and lax.ppermute only.
A program may use at most 320 MiB of HBM per device.

v0:
```python
import math

import jax
import jax.numpy as jnp
from jax import lax
from jax.sharding import PartitionSpec as P

D = 1536
HD = 128
SPAN = 4


EPS = 1e-06
THETA = 1000000.0


def partner_2(block, axis, stride):
    count = lax.axis_size(axis)
    route = []
    for low in range(count):
        high = low | 1 << stride
        if high != low and high < count:
            route += [(low, high), (high, low)]
    return lax.ppermute(block, axis, route)


def from_behind(value, axis, steps):
    count = lax.axis_size(axis)
    leading, last = (max(0, -steps), min(count, count - steps))
    return lax.ppermute(value, axis, [(source, source + steps) for source in range(leading, last)])


def rotate_half(values):
    half = values.shape[-1] // 2
    return jnp.concatenate([-values[..., half:], values[..., :half]], axis=-1)


def rope_tables(positions, head_size):
    half = head_size // 2
    freqs = THETA ** (-(jnp.arange(half, dtype=jnp.float32) * 2.0) / head_size)
    angles = positions.astype(jnp.float32)[:, None] * freqs[None, :]
    angles = jnp.concatenate([angles, angles], axis=-1)
    return (jnp.cos(angles), jnp.sin(angles))


def rotate(values, cosine, sine):
    return values * cosine + rotate_half(values) * sine


def rotate_back(values, cosine, sine):
    return values * cosine - rotate_half(values * sine)


def feature_total(values):
    return lax.psum(values, "col")


def gather_features(values):
    return lax.all_gather(values, "col", axis=1, tiled=True)


def sum_partials(values):
    return lax.psum_scatter(
        values.astype(jnp.bfloat16), "col", scatter_dimension=1, tiled=True
    ).astype(jnp.float32)


def norm_forward(resid, gain):
    squares = feature_total(jnp.sum(resid * resid, axis=1))
    inverse = lax.rsqrt(squares / D + EPS)
    normed = (resid * inverse[:, None] * gain[None, :]).astype(jnp.bfloat16)
    return (gather_features(normed), inverse)


def norm_backward(grad_normed, resid, inverse, gain):
    scaled = resid * inverse[:, None]
    grad_gain = jnp.sum(grad_normed * scaled, axis=0)
    grad_scaled = grad_normed * gain[None, :]
    mean_term = feature_total(jnp.sum(grad_scaled * scaled, axis=1)) / D
    return (inverse[:, None] * (grad_scaled - scaled * mean_term[:, None]), grad_gain)


def layer_forward(resid, gains, weights, setting):
    w_query, w_keyval, w_gate, w_up, w_out, w_down = weights
    cosine, sine, allowed, is_key, peer = setting
    rows = resid.shape[0]
    local_heads = w_query.shape[1] // HD
    scale = 1.0 / math.sqrt(HD)
    normed_attn, inverse_attn = norm_forward(resid, gains[0])
    query_raw = jnp.dot(normed_attn, w_query, preferred_element_type=jnp.float32).reshape(
        rows, local_heads, HD
    )
    queries = rotate(query_raw, cosine[:, None, :], sine[:, None, :]).astype(jnp.bfloat16)
    own_cols = jnp.dot(normed_attn, w_keyval, preferred_element_type=jnp.float32)
    own_cols = jnp.where(is_key, rotate(own_cols, cosine, sine), own_cols).astype(jnp.bfloat16)
    partner = partner_2(own_cols, "col", 0)
    key_value = jnp.stack(
        [jnp.where(is_key, own_cols, partner), jnp.where(is_key, partner, own_cols)]
    )[:, None]
    for level in range(SPAN.bit_length() - 1):
        other = partner_2(key_value, "row", level)
        upper = peer >> level & 1 == 1
        key_value = jnp.where(
            upper,
            jnp.concatenate([other, key_value], axis=1),
            jnp.concatenate([key_value, other], axis=1),
        )
    keys = key_value[0].reshape(-1, HD)
    values = key_value[1].reshape(-1, HD)
    scores = jnp.einsum("qhd,kd->hqk", queries, keys, preferred_element_type=jnp.float32) * scale
    unnormed = jnp.where(allowed[None], jnp.exp(scores), 0.0)
    total = jnp.sum(unnormed, axis=-1)
    probs = unnormed / total[..., None]
    attended = jnp.einsum(
        "hqk,kd->qhd", probs.astype(jnp.bfloat16), values, preferred_element_type=jnp.float32
    )
    attended = attended.reshape(rows, local_heads * HD).astype(jnp.bfloat16)
    middle = resid + sum_partials(jnp.dot(attended, w_out, preferred_element_type=jnp.float32))
    normed_ffn, inverse_ffn = norm_forward(middle, gains[1])
    gate = jnp.dot(normed_ffn, w_gate, preferred_element_type=jnp.float32)
    up = jnp.dot(normed_ffn, w_up, preferred_element_type=jnp.float32)
    hidden = (jax.nn.silu(gate) * up).astype(jnp.bfloat16)
    result = middle + sum_partials(jnp.dot(hidden, w_down, preferred_element_type=jnp.float32))
    kept = (
        resid,
        inverse_attn,
        normed_attn,
        queries,
        keys,
        values,
        jnp.log(total),
        attended,
        middle,
        inverse_ffn,
        normed_ffn,
        gate,
        up,
        hidden,
    )
    return (result, kept)


def layer_backward(grad_out, kept, gains, weights, setting):
    w_query, w_keyval, w_gate, w_up, w_out, w_down = weights
    cosine, sine, allowed, is_key, peer = setting
    (
        resid,
        inverse_attn,
        normed_attn,
        queries,
        keys,
        values,
        log_total,
        attended,
        middle,
        inverse_ffn,
        normed_ffn,
        gate,
        up,
        hidden,
    ) = kept
    rows = resid.shape[0]
    local_heads = w_query.shape[1] // HD
    scale = 1.0 / math.sqrt(HD)
    grad_branch = gather_features(grad_out.astype(jnp.bfloat16))
    grad_down = jnp.einsum("tf,td->fd", hidden, grad_branch, preferred_element_type=jnp.float32)
    grad_hidden = jnp.einsum("td,fd->tf", grad_branch, w_down, preferred_element_type=jnp.float32)
    sigma = jax.nn.sigmoid(gate)
    grad_gate_act = (grad_hidden * up * sigma * (1.0 + gate * (1.0 - sigma))).astype(jnp.bfloat16)
    grad_up_act = (grad_hidden * gate * sigma).astype(jnp.bfloat16)
    grad_gate = jnp.einsum(
        "td,tf->df", normed_ffn, grad_gate_act, preferred_element_type=jnp.float32
    )
    grad_up = jnp.einsum("td,tf->df", normed_ffn, grad_up_act, preferred_element_type=jnp.float32)
    grad_normed_ffn = sum_partials(
        jnp.einsum("tf,df->td", grad_gate_act, w_gate, preferred_element_type=jnp.float32)
        + jnp.einsum("tf,df->td", grad_up_act, w_up, preferred_element_type=jnp.float32)
    )
    grad_middle_norm, grad_gain_ffn = norm_backward(grad_normed_ffn, middle, inverse_ffn, gains[1])
    grad_middle = grad_out + grad_middle_norm
    grad_attn_out = gather_features(grad_middle.astype(jnp.bfloat16))
    grad_wout = jnp.einsum("tq,td->qd", attended, grad_attn_out, preferred_element_type=jnp.float32)
    grad_attended = (
        jnp.einsum("td,qd->tq", grad_attn_out, w_out, preferred_element_type=jnp.float32)
        .astype(jnp.bfloat16)
        .reshape(rows, local_heads, HD)
    )
    scores = jnp.einsum("qhd,kd->hqk", queries, keys, preferred_element_type=jnp.float32) * scale
    probs = jnp.where(allowed[None], jnp.exp(scores - log_total[..., None]), 0.0)
    grad_probs = jnp.einsum(
        "qhd,kd->hqk", grad_attended, values, preferred_element_type=jnp.float32
    )
    grad_scores = (
        probs * (grad_probs - jnp.sum(probs * grad_probs, axis=-1, keepdims=True))
    ).astype(jnp.bfloat16)
    grad_queries = (
        jnp.einsum("hqk,kd->qhd", grad_scores, keys, preferred_element_type=jnp.float32) * scale
    )
    grad_keys = (
        jnp.einsum("hqk,qhd->kd", grad_scores, queries, preferred_element_type=jnp.float32) * scale
    )
    grad_values = jnp.einsum(
        "hqk,qhd->kd", probs.astype(jnp.bfloat16), grad_attended, preferred_element_type=jnp.float32
    )
    grad_kv = jnp.stack([grad_keys, grad_values]).reshape(2, SPAN, rows, HD)
    grad_mine = lax.dynamic_index_in_dim(grad_kv, peer, 1, keepdims=False)
    for offset in range(1, SPAN):
        target = jnp.maximum(peer - offset, 0)
        outgoing = lax.dynamic_index_in_dim(grad_kv, target, 1, keepdims=False)
        outgoing = jnp.where(peer >= offset, outgoing, jnp.zeros_like(outgoing))
        grad_mine = grad_mine + from_behind(outgoing.astype(jnp.bfloat16), "row", -offset).astype(
            outgoing.dtype
        )
    grad_key_own = grad_mine[0]
    grad_value_own = grad_mine[1]
    received = partner_2(
        jnp.where(is_key, grad_value_own, grad_key_own).astype(jnp.bfloat16), "col", 0
    ).astype(jnp.float32)
    grad_own = jnp.where(is_key, grad_key_own, grad_value_own) + received
    grad_own = jnp.where(is_key, rotate_back(grad_own, cosine, sine), grad_own).astype(jnp.bfloat16)
    grad_query_raw = (
        rotate_back(grad_queries, cosine[:, None, :], sine[:, None, :])
        .astype(jnp.bfloat16)
        .reshape(rows, local_heads * HD)
    )
    grad_wquery = jnp.einsum(
        "td,tq->dq", normed_attn, grad_query_raw, preferred_element_type=jnp.float32
    )
    grad_wkeyval = jnp.einsum(
        "td,tc->dc", normed_attn, grad_own, preferred_element_type=jnp.float32
    )
    grad_normed_attn = sum_partials(
        jnp.einsum("tq,dq->td", grad_query_raw, w_query, preferred_element_type=jnp.float32)
        + jnp.einsum("tc,dc->td", grad_own, w_keyval, preferred_element_type=jnp.float32)
    )
    grad_resid_norm, grad_gain_attn = norm_backward(grad_normed_attn, resid, inverse_attn, gains[0])
    weight_grads = (grad_wquery, grad_wkeyval, grad_gate, grad_up, grad_wout, grad_down)
    return (grad_middle + grad_resid_norm, weight_grads, (grad_gain_attn, grad_gain_ffn))


def local(layer_input, g_out, attn_gain, w_query, w_keyval, w_out, ffn_gain, w_gate, w_up, w_down):
    section = lax.axis_index("section")
    peer = lax.axis_index("row") % SPAN
    is_key = lax.axis_index("col") % 2 == 0
    micro = layer_input.shape[0]
    rows = layer_input.shape[2]
    width = layer_input.shape[3]
    weights = (
        lax.all_gather(w_query[0], "row", axis=0, tiled=True),
        lax.all_gather(w_keyval[0], "row", axis=0, tiled=True),
        lax.all_gather(w_gate[0], "row", axis=0, tiled=True),
        lax.all_gather(w_up[0], "row", axis=0, tiled=True),
        lax.all_gather(w_out[0], "row", axis=1, tiled=True),
        lax.all_gather(w_down[0], "row", axis=1, tiled=True),
    )
    gains = (attn_gain[0], ffn_gain[0])
    positions = peer * rows + jnp.arange(rows, dtype=jnp.int32)
    cosine, sine = rope_tables(positions, HD)
    key_positions = jnp.arange(rows * SPAN, dtype=jnp.int32)
    allowed = key_positions[None, :] <= positions[:, None]
    setting = (cosine, sine, allowed, is_key, peer)
    received = jnp.zeros((rows, width), jnp.bfloat16)
    kept_list = []
    sent_list = []
    for tick in range(micro + 1):
        first = layer_input[min(tick, micro - 1), 0]
        resid = jnp.where(section == 0, first, received).astype(jnp.float32)
        result, kept = layer_forward(resid, gains, weights, setting)
        sent = result.astype(jnp.bfloat16)
        sent_list.append(sent)
        kept_list.append(kept)
        if tick < micro:
            received = from_behind(sent, "section", 1)
    acts = jnp.where(section == 0, jnp.stack(sent_list[:micro]), jnp.stack(sent_list[1:]))
    arrived = jnp.zeros((rows, width), jnp.bfloat16)
    grad_list = []
    totals = None
    gain_totals = None
    for tick in range(micro + 1):
        if tick < micro:
            top = g_out[tick, 0]
        else:
            top = jnp.zeros((rows, width), jnp.float32)
        grad_out = jnp.where(section == 1, top, arrived.astype(jnp.float32))
        kept = jax.tree.map(
            lambda early, late: jnp.where(section == 0, early, late),
            kept_list[max(tick - 1, 0)],
            kept_list[min(tick + 1, micro)],
        )
        grad_resid, weight_grads, gain_grads = layer_backward(
            grad_out, kept, gains, weights, setting
        )
        back = grad_resid.astype(jnp.bfloat16)
        grad_list.append(back)
        if tick < micro:
            arrived = from_behind(back, "section", -1)
        if totals is None:
            totals = tuple(weight_grads)
            gain_totals = tuple(gain_grads)
        else:
            totals = tuple((left + right for left, right in zip(totals, weight_grads)))
            gain_totals = tuple((left + right for left, right in zip(gain_totals, gain_grads)))
    sum_query, sum_keyval, sum_gate, sum_up, sum_out, sum_down = totals
    totals = (
        lax.psum_scatter(
            sum_query.astype(jnp.bfloat16), "row", scatter_dimension=0, tiled=True
        ).astype(jnp.float32),
        lax.psum_scatter(
            sum_keyval.astype(jnp.bfloat16), "row", scatter_dimension=0, tiled=True
        ).astype(jnp.float32),
        lax.psum_scatter(
            sum_gate.astype(jnp.bfloat16), "row", scatter_dimension=0, tiled=True
        ).astype(jnp.float32),
        lax.psum_scatter(
            sum_up.astype(jnp.bfloat16), "row", scatter_dimension=0, tiled=True
        ).astype(jnp.float32),
        lax.psum_scatter(
            sum_out.astype(jnp.bfloat16), "row", scatter_dimension=1, tiled=True
        ).astype(jnp.float32),
        lax.psum_scatter(
            sum_down.astype(jnp.bfloat16), "row", scatter_dimension=1, tiled=True
        ).astype(jnp.float32),
    )
    gain_attn, gain_ffn = lax.psum((gain_totals[0], gain_totals[1]), "row")
    grads_in = jnp.where(section == 0, jnp.stack(grad_list[1:]), jnp.stack(grad_list[:micro]))
    acts = acts.reshape(1, micro, 1, rows, width)
    grads_in = grads_in.reshape(1, micro, 1, rows, width)
    final_query, final_keyval, final_gate, final_up, final_out, final_down = totals
    return (
        acts,
        grads_in,
        gain_attn[None],
        final_query[None],
        final_keyval[None],
        final_out[None],
        gain_ffn[None],
        final_gate[None],
        final_up[None],
        final_down[None],
    )


def solution(mesh):
    placed = (
        P(None, "row", None, "col"),
        P(None, "row", None, "col"),
        P("section", "col"),
        P("section", "row", "col"),
        P("section", "row", "col"),
        P("section", "col", "row"),
        P("section", "col"),
        P("section", "row", "col"),
        P("section", "row", "col"),
        P("section", "col", "row"),
    )
    return jax.shard_map(
        local,
        mesh=mesh,
        in_specs=placed,
        out_specs=(
            P("section", None, "row", None, "col"),
            P("section", None, "row", None, "col"),
            P("section", "col"),
            P("section", "row", "col"),
            P("section", "row", "col"),
            P("section", "col", "row"),
            P("section", "col"),
            P("section", "row", "col"),
            P("section", "row", "col"),
            P("section", "col", "row"),
        ),
        check_vma=False,
    )
```

profile of v0, /device:TPU:0, one launch (start us, length us, event | category | flops | bytes accessed | tf_op | source)
XLA Modules:
  0.0 2234.9 jit_solution(9128519053788460988)
XLA Ops:
  63.0 24.9 %all-gather.48.cloned.1.call-done = bf16[1,1536,384]{2,1,0:T(8,128)(2,1)} async-done(((bf16[1,384,384]{2,1,0:T(8,128)(2,1)}), bf16[1,1536,384]{2,1,0:T(8,128)(2,1)}) %all-gather.48.cloned.1.call-update) | async-done | bytes 1179664 | tf_op jit(solution)/shard_map/all_gather | solution.py:249
  106.0 35.0 %collective-permute-done.2 = bf16[2,2,512,128]{3,2,0,1:T(8,128)(2,1)} collective-permute-done((bf16[2,2,512,128]{3,2,0,1:T(8,128)(2,1)}, bf16[2,2,512,128]{3,2,0,1:T(8,128)(2,1)}, u32[]{:S(2)}, u32[]{:S(2)}) %collective-permute-start.2) | collective-permute-done | bytes 524320 | tf_op jit(solution)/shard_map/ppermute | solution.py:24
  154.8 31.2 %reduce-scatter.27.cloned.1.call-done = bf16[512,384]{0,1:T(8,128)(2,1)} async-done(((bf16[512,1536]{0,1:T(8,128)(2,1)}), bf16[512,384]{0,1:T(8,128)(2,1)}) %reduce-scatter.27.cloned.1.call-update) | async-done | bytes 393232 | tf_op jit(solution)/shard_map/reduce_scatter | solution.py:63
  200.4 28.7 %all-gather.26.cloned.1.call-done = bf16[512,1536]{0,1:T(8,128)(2,1)} async-done(((bf16[512,384]{0,1:T(8,128)(2,1)}), bf16[512,1536]{0,1:T(8,128)(2,1)}) %all-gather.26.cloned.1.call-update) | async-done | bytes 1572880 | tf_op jit(solution)/shard_map/all_gather | solution.py:59
  229.1 126.5 %all-gather.52.cloned.1.call-done = bf16[1,1536,2240]{1,2,0:T(8,128)(2,1)} async-done(((bf16[1,384,2240]{1,2,0:T(8,128)(2,1)}), bf16[1,1536,2240]{1,2,0:T(8,128)(2,1)}) %all-gather.52.cloned.1.call-update) | async-done | bytes 6881296 | tf_op jit(solution)/shard_map/all_gather | solution.py:251
  364.8 115.5 %all-gather.54.cloned.1.call-done = bf16[1,1536,2240]{1,2,0:T(8,128)(2,1)} async-done(((bf16[1,384,2240]{1,2,0:T(8,128)(2,1)}), bf16[1,1536,2240]{1,2,0:T(8,128)(2,1)}) %all-gather.54.cloned.1.call-update) | async-done | bytes 6881296 | tf_op jit(solution)/shard_map/all_gather | solution.py:252
  492.2 112.9 %all-gather.56.cloned.1.call-done = bf16[1,2240,1536]{2,1,0:T(8,128)(2,1)} async-done(((bf16[1,2240,384]{2,1,0:T(8,128)(2,1)}), bf16[1,2240,1536]{2,1,0:T(8,128)(2,1)}) %all-gather.56.cloned.1.call-update) | async-done | bytes 6881296 | tf_op jit(solution)/shard_map/all_gather | solution.py:254
  613.9 29.4 %reduce-scatter.29.cloned.1.call-done = bf16[512,384]{0,1:T(8,128)(2,1)} async-done(((bf16[512,1536]{0,1:T(8,128)(2,1)}), bf16[512,384]{0,1:T(8,128)(2,1)}) %reduce-scatter.29.cloned.1.call-update) | async-done | bytes 393232 | tf_op jit(solution)/shard_map/reduce_scatter | solution.py:63
  660.0 30.5 %all-gather.28.cloned.1.call-done = bf16[512,1536]{0,1:T(8,128)(2,1)} async-done(((bf16[512,384]{0,1:T(8,128)(2,1)}), bf16[512,1536]{0,1:T(8,128)(2,1)}) %all-gather.28.cloned.1.call-update) | async-done | bytes 1572880 | tf_op jit(solution)/shard_map/all_gather | solution.py:59
  746.7 31.2 %reduce-scatter.31.cloned.1.call-done = bf16[512,384]{0,1:T(8,128)(2,1)} async-done(((bf16[512,1536]{0,1:T(8,128)(2,1)}), bf16[512,384]{0,1:T(8,128)(2,1)}) %reduce-scatter.31.cloned.1.call-update) | async-done | bytes 393232 | tf_op jit(solution)/shard_map/reduce_scatter | solution.py:63
  796.0 24.9 %all-gather.30.cloned.1.call-done = bf16[512,1536]{0,1:T(8,128)(2,1)} async-done(((bf16[512,384]{0,1:T(8,128)(2,1)}), bf16[512,1536]{0,1:T(8,128)(2,1)}) %all-gather.30.cloned.1.call-update) | async-done | bytes 1572880 | tf_op jit(solution)/shard_map/all_gather | solution.py:59
  838.8 15.4 all-gather.36.cloned.1.call-done
  893.8 22.2 reduce-scatter.39.cloned.1.call-done
  916.0 34.0 %reduce-scatter.33.cloned.1.call-done = bf16[512,384]{0,1:T(8,128)(2,1)} async-done(((bf16[512,1536]{0,1:T(8,128)(2,1)}), bf16[512,384]{0,1:T(8,128)(2,1)}) %reduce-scatter.33.cloned.1.call-update) | async-done | bytes 393232 | tf_op jit(solution)/shard_map/reduce_scatter | solution.py:63
  970.8 26.9 %all-gather.32.cloned.1.call-done = bf16[512,1536]{0,1:T(8,128)(2,1)} async-done(((bf16[512,384]{0,1:T(8,128)(2,1)}), bf16[512,1536]{0,1:T(8,128)(2,1)}) %all-gather.32.cloned.1.call-update) | async-done | bytes 1572880 | tf_op jit(solution)/shard_map/all_gather | solution.py:59
  1083.8 20.4 fusion.2
  1163.2 33.5 %reduce-scatter.41.cloned.1.call-done = bf16[512,384]{0,1:T(8,128)(2,1)} async-done(((bf16[512,1536]{0,1:T(8,128)(2,1)}), bf16[512,384]{0,1:T(8,128)(2,1)}) %reduce-scatter.41.cloned.1.call-update) | async-done | bytes 393232 | tf_op jit(solution)/shard_map/reduce_scatter | solution.py:63
  1216.7 24.8 %all-gather.34.cloned.1.call-done = bf16[512,1536]{0,1:T(8,128)(2,1)} async-done(((bf16[512,384]{0,1:T(8,128)(2,1)}), bf16[512,1536]{0,1:T(8,128)(2,1)}) %all-gather.34.cloned.1.call-update) | async-done | bytes 1572880 | tf_op jit(solution)/shard_map/all_gather | solution.py:59
  1304.1 31.1 %reduce-scatter.43.cloned.1.call-done = bf16[512,384]{0,1:T(8,128)(2,1)} async-done(((bf16[512,1536]{0,1:T(8,128)(2,1)}), bf16[512,384]{0,1:T(8,128)(2,1)}) %reduce-scatter.43.cloned.1.call-update) | async-done | bytes 393232 | tf_op jit(solution)/shard_map/reduce_scatter | solution.py:63
  1350.1 30.9 %all-gather.42.cloned.1.call-done = bf16[512,1536]{0,1:T(8,128)(2,1)} async-done(((bf16[512,384]{0,1:T(8,128)(2,1)}), bf16[512,1536]{0,1:T(8,128)(2,1)}) %all-gather.42.cloned.1.call-update) | async-done | bytes 1572880 | tf_op jit(solution)/shard_map/all_gather | solution.py:59
  1443.4 34.1 %reduce-scatter.45.cloned.1.call-done = bf16[512,384]{0,1:T(8,128)(2,1)} async-done(((bf16[512,1536]{0,1:T(8,128)(2,1)}), bf16[512,384]{0,1:T(8,128)(2,1)}) %reduce-scatter.45.cloned.1.call-update) | async-done | bytes 393232 | tf_op jit(solution)/shard_map/reduce_scatter | solution.py:63
  1494.6 30.5 %all-gather.44.cloned.1.call-done = bf16[512,1536]{0,1:T(8,128)(2,1)} async-done(((bf16[512,384]{0,1:T(8,128)(2,1)}), bf16[512,1536]{0,1:T(8,128)(2,1)}) %all-gather.44.cloned.1.call-update) | async-done | bytes 1572880 | tf_op jit(solution)/shard_map/all_gather | solution.py:59
  1564.5 22.5 %reduce-scatter.47.cloned.1.call-done = bf16[512,384]{0,1:T(8,128)(2,1)} async-done(((bf16[512,1536]{0,1:T(8,128)(2,1)}), bf16[512,384]{0,1:T(8,128)(2,1)}) %reduce-scatter.47.cloned.1.call-update) | async-done | bytes 393232 | tf_op jit(solution)/shard_map/reduce_scatter | solution.py:63
  1586.9 34.0 %reduce-scatter.37.cloned.1.call-done = bf16[512,384]{0,1:T(8,128)(2,1)} async-done(((bf16[512,1536]{0,1:T(8,128)(2,1)}), bf16[512,384]{0,1:T(8,128)(2,1)}) %reduce-scatter.37.cloned.1.call-update) | async-done | bytes 393232 | tf_op jit(solution)/shard_map/reduce_scatter | solution.py:63
  1635.3 30.9 %all-gather.46.cloned.1.call-done = bf16[512,1536]{0,1:T(8,128)(2,1)} async-done(((bf16[512,384]{0,1:T(8,128)(2,1)}), bf16[512,1536]{0,1:T(8,128)(2,1)}) %all-gather.46.cloned.1.call-update) | async-done | bytes 1572880 | tf_op jit(solution)/shard_map/all_gather | solution.py:59
  1769.7 16.3 add_convert_fusion.2
  1814.5 16.5 add_convert_fusion.1
  1861.1 17.0 add_convert_fusion
  1911.8 15.9 all-reduce.2
  1927.7 42.9 %reduce-scatter.57.cloned.1.call-done = bf16[384,2240]{1,0:T(8,128)(2,1)} async-done(((bf16[1536,2240]{1,0:T(8,128)(2,1)}), bf16[384,2240]{1,0:T(8,128)(2,1)}) %reduce-scatter.57.cloned.1.call-update) | async-done | bytes 1720336
  1973.3 123.6 %reduce-scatter.59.cloned.1.call-done = bf16[384,2240]{1,0:T(8,128)(2,1)} async-done(((bf16[1536,2240]{1,0:T(8,128)(2,1)}), bf16[384,2240]{1,0:T(8,128)(2,1)}) %reduce-scatter.59.cloned.1.call-update) | async-done | bytes 1720336
  2104.9 118.4 %reduce-scatter.61.cloned.1.call-done = bf16[384,2240]{1,0:T(8,128)(2,1)} async-done(((bf16[1536,2240]{1,0:T(8,128)(2,1)}), bf16[384,2240]{1,0:T(8,128)(2,1)}) %reduce-scatter.61.cloned.1.call-update) | async-done | bytes 1720336
  (667 shorter events, 885.6 us)
Async XLA Ops:
  22.5 65.4 %all-gather.48.cloned.1.call-start = ((), (), s32[]{:S(2)}) async-start(), calls=%async_computation.44 | async-start | bytes 1474560 | tf_op jit(solution)/shard_map/all_gather | solution.py:249
  23.3 127.8 %all-gather.50.cloned.1.call-start = ((), (), s32[]{:S(2)}) async-start(), calls=%async_computation.45 | async-start | bytes 1474560 | tf_op jit(solution)/shard_map/all_gather | solution.py:253
  24.0 162.0 %reduce-scatter.27.cloned.1.call-start = ((), (), s32[]{:S(2)}) async-start(), calls=%async_computation.19 | async-start | bytes 1966080 | tf_op jit(solution)/shard_map/reduce_scatter | solution.py:63
  154.7 74.4 %all-gather.26.cloned.1.call-start = ((), (), s32[]{:S(2)}) async-start(), calls=%async_computation.20 | async-start | bytes 1966080 | tf_op jit(solution)/shard_map/all_gather | solution.py:59
  198.1 157.5 %all-gather.52.cloned.1.call-start = ((), (), s32[]{:S(2)}) async-start(), calls=%async_computation.46 | async-start | bytes 8601600 | tf_op jit(solution)/shard_map/all_gather | solution.py:251
  198.6 281.7 %all-gather.54.cloned.1.call-start = ((), (), s32[]{:S(2)}) async-start(), calls=%async_computation.47 | async-start | bytes 8601600 | tf_op jit(solution)/shard_map/all_gather | solution.py:252
  199.4 405.7 %all-gather.56.cloned.1.call-start = ((), (), s32[]{:S(2)}) async-start(), calls=%async_computation.48 | async-start | bytes 8601600 | tf_op jit(solution)/shard_map/all_gather | solution.py:254
  200.1 443.1 %reduce-scatter.29.cloned.1.call-start = ((), (), s32[]{:S(2)}) async-start(), calls=%async_computation.21 | async-start | bytes 1966080 | tf_op jit(solution)/shard_map/reduce_scatter | solution.py:63
  613.8 76.7 %all-gather.28.cloned.1.call-start = ((), (), s32[]{:S(2)}) async-start(), calls=%async_computation.22 | async-start | bytes 1966080 | tf_op jit(solution)/shard_map/all_gather | solution.py:59
  659.5 118.4 %reduce-scatter.31.cloned.1.call-start = ((), (), s32[]{:S(2)}) async-start(), calls=%async_computation.23 | async-start | bytes 1966080 | tf_op jit(solution)/shard_map/reduce_scatter | solution.py:63
  746.7 74.3 %all-gather.30.cloned.1.call-start = ((), (), s32[]{:S(2)}) async-start(), calls=%async_computation.24 | async-start | bytes 1966080 | tf_op jit(solution)/shard_map/all_gather | solution.py:59
  795.8 120.2 %reduce-scatter.39.cloned.1.call-start = ((), (), s32[]{:S(2)}) async-start(), calls=%async_computation.31 | async-start | bytes 1966080 | tf_op jit(solution)/shard_map/reduce_scatter | solution.py:63
  884.7 65.3 %reduce-scatter.33.cloned.1.call-start = ((), (), s32[]{:S(2)}) async-start(), calls=%async_computation.25 | async-start | bytes 1966080 | tf_op jit(solution)/shard_map/reduce_scatter | solution.py:63
  893.7 103.9 %all-gather.32.cloned.1.call-start = ((), (), s32[]{:S(2)}) async-start(), calls=%async_computation.26 | async-start | bytes 1966080 | tf_op jit(solution)/shard_map/all_gather | solution.py:59
  970.7 191.3 %reduce-scatter.35.cloned.1.call-start = ((), (), s32[]{:S(2)}) async-start(), calls=%async_computation.27 | async-start | bytes 1966080 | tf_op jit(solution)/shard_map/reduce_scatter | solution.py:63
  1125.5 71.2 %reduce-scatter.41.cloned.1.call-start = ((), (), s32[]{:S(2)}) async-start(), calls=%async_computation.33 | async-start | bytes 1966080 | tf_op jit(solution)/shard_map/reduce_scatter | solution.py:63
  1157.6 83.9 %all-gather.34.cloned.1.call-start = ((), (), s32[]{:S(2)}) async-start(), calls=%async_computation.28 | async-start | bytes 1966080 | tf_op jit(solution)/shard_map/all_gather | solution.py:59
  1210.5 64.3 %all-gather.40.cloned.1.call-start = ((), (), s32[]{:S(2)}) async-start(), calls=%async_computation.34 | async-start | bytes 1966080 | tf_op jit(solution)/shard_map/all_gather | solution.py:59
  1216.7 118.5 %reduce-scatter.43.cloned.1.call-start = ((), (), s32[]{:S(2)}) async-start(), calls=%async_computation.35 | async-start | bytes 1966080 | tf_op jit(solution)/shard_map/reduce_scatter | solution.py:63
  1303.9 77.1 %all-gather.42.cloned.1.call-start = ((), (), s32[]{:S(2)}) async-start(), calls=%async_computation.36 | async-start | bytes 1966080 | tf_op jit(solution)/shard_map/all_gather | solution.py:59
  1350.0 127.4 %reduce-scatter.45.cloned.1.call-start = ((), (), s32[]{:S(2)}) async-start(), calls=%async_computation.37 | async-start | bytes 1966080 | tf_op jit(solution)/shard_map/reduce_scatter | solution.py:63
  1443.3 81.8 %all-gather.44.cloned.1.call-start = ((), (), s32[]{:S(2)}) async-start(), calls=%async_computation.38 | async-start | bytes 1966080 | tf_op jit(solution)/shard_map/all_gather | solution.py:59
  1494.1 92.8 %reduce-scatter.47.cloned.1.call-start = ((), (), s32[]{:S(2)}) async-start(), calls=%async_computation.39 | async-start | bytes 1966080 | tf_op jit(solution)/shard_map/reduce_scatter | solution.py:63
  1555.6 65.3 %reduce-scatter.37.cloned.1.call-start = ((), (), s32[]{:S(2)}) async-start(), calls=%async_computation.29 | async-start | bytes 1966080 | tf_op jit(solution)/shard_map/reduce_scatter | solution.py:63
  1564.4 101.8 %all-gather.46.cloned.1.call-start = ((), (), s32[]{:S(2)}) async-start(), calls=%async_computation.40 | async-start | bytes 1966080 | tf_op jit(solution)/shard_map/all_gather | solution.py:59
  1635.2 256.5 %reduce-scatter.53.cloned.1.call-start = ((), (), s32[]{:S(2)}) async-start(), calls=%async_computation.43 | async-start | bytes 491520 | tf_op jit(solution)/shard_map/reduce_scatter | solution.py:308
  1728.1 165.3 %reduce-scatter.55.cloned.1.call-start = ((), (), s32[]{:S(2)}) async-start(), calls=%async_computation.49 | async-start | bytes 1474560
  1736.4 160.6 %reduce-scatter.51.cloned.1.call-start = ((), (), s32[]{:S(2)}) async-start(), calls=%async_computation.42 | async-start | bytes 1474560 | tf_op jit(solution)/shard_map/reduce_scatter | solution.py:305
  1744.7 154.1 %reduce-scatter.49.cloned.1.call-start = ((), (), s32[]{:S(2)}) async-start(), calls=%async_computation.41 | async-start | bytes 1966080 | tf_op jit(solution)/shard_map/reduce_scatter | solution.py:63
  1758.4 212.2 %reduce-scatter.57.cloned.1.call-start = ((), (), s32[]{:S(2)}) async-start(), calls=%async_computation.50 | async-start | bytes 8847360
  1796.3 300.7 %reduce-scatter.59.cloned.1.call-start = ((), (), s32[]{:S(2)}) async-start(), calls=%async_computation.51 | async-start | bytes 8847360
  1841.3 382.0 %reduce-scatter.61.cloned.1.call-start = ((), (), s32[]{:S(2)}) async-start(), calls=%async_computation.52 | async-start | bytes 8847360
  (183 other events, 10806.2 us)
Sparse Core Ops, SparseCore 0:
  22.6 30.1 all-gather.23
  54.4 33.4 all-gather.47
  89.5 50.7 all-gather.49
  154.8 31.1 reduce-scatter.26
  198.2 30.8 all-gather.25
  230.5 124.9 all-gather.51
  357.1 123.1 all-gather.53
  481.9 123.1 all-gather.55
  613.9 29.2 reduce-scatter.28
  659.7 30.8 all-gather.27
  746.8 31.0 reduce-scatter.30
  790.1 30.8 all-gather.29
  823.4 30.8 all-gather.35
  884.8 31.1 reduce-scatter.38
  918.8 31.1 reduce-scatter.32
  966.8 30.8 all-gather.31
  999.9 30.8 all-gather.37
  1125.6 36.3 reduce-scatter.34
  1165.6 31.0 reduce-scatter.40
  1210.7 30.8 all-gather.33
  1243.9 30.8 all-gather.39
  1304.0 31.1 reduce-scatter.42
  1350.1 30.8 all-gather.41
  1443.4 33.9 reduce-scatter.44
  1494.2 30.8 all-gather.43
  1555.7 31.1 reduce-scatter.46
  1589.7 31.1 reduce-scatter.36
  1635.3 30.8 all-gather.45
  1814.9 29.7 reduce-scatter.48
  1846.8 123.7 reduce-scatter.56
  1972.9 124.0 reduce-scatter.58
  2099.3 124.0 reduce-scatter.60
  (3 shorter events, 78.9 us)
where the time goes:
time: 2250 us; the launch traced here: 2230 us
  waiting for transfers between devices  1390 us (62%)
  matrix products  447 us (20%)
  other arithmetic  133 us (6%)
  blocking collectives  123 us (5%)
  local copies, waits for them, and re-layouts  85.8 us (4%)
  starting transfers between devices  43.5 us (2%)
    reduce_scatter x12, waiting for transfers between devices, sum_partials(): lax.psum_scatter(values.astype(jnp.bfloat16), 'col', scatter_dimension=1,...  308 us
    unnamed x39, waiting for transfers between devices  289 us
    all_gather x12, waiting for transfers between devices, gather_features(): return lax.all_gather(values, 'col', axis=1, tiled=True)  282 us
    all_gather x1, waiting for transfers between devices, local(): lax.all_gather(w_gate[0], 'row', axis=0, tiled=True)  126 us
    all_gather x1, waiting for transfers between devices, local(): lax.all_gather(w_up[0], 'row', axis=0, tiled=True)  116 us
    all_gather x1, waiting for transfers between devices, local(): lax.all_gather(w_down[0], 'row', axis=1, tiled=True)  113 us
    psum x10, blocking collectives, feature_total(): return lax.psum(values, 'col')  91.5 us
    ppermute x12, waiting for transfers between devices, partner_2(): return lax.ppermute(block, axis, route)  78.4 us
  transfers between devices with their start and end apart: 60, of which 49 were waited for; matrix products, arithmetic and copies ran while one was open for 16% of the time, Pallas kernels for 0%

commit v1 on v0

v1 whole, which is shorter than its diff:
```python
import math

import jax
import jax.numpy as jnp
from jax import lax
from jax.sharding import PartitionSpec as P

HD = 128
SPAN = 4
EPS = 1e-06
THETA = 1000000.0
BF = jnp.bfloat16
F32 = jnp.float32


def dot(left, right, left_dim, right_dim):
    return lax.dot_general(
        left, right, (((left_dim,), (right_dim,)), ((), ())), preferred_element_type=F32
    )


def rotate_half(values):
    half = values.shape[-1] // 2
    return jnp.concatenate([-values[..., half:], values[..., :half]], axis=-1)


def rope_tables(positions, head_size):
    half = head_size // 2
    freqs = THETA ** (-(jnp.arange(half, dtype=F32) * 2.0) / head_size)
    angles = positions.astype(F32)[:, None] * freqs[None, :]
    angles = jnp.concatenate([angles, angles], axis=-1)
    return (jnp.cos(angles), jnp.sin(angles))


def rotate(values, cosine, sine):
    return values * cosine + rotate_half(values) * sine


def rotate_back(values, cosine, sine):
    return values * cosine - rotate_half(values * sine)


def over_col(block, step):
    count = lax.axis_size("col")
    return lax.ppermute(block, "col", [(i, i ^ step) for i in range(count)])


def over_section(block):
    return lax.ppermute(block, "section", [(0, 1), (1, 0)])


def along_row(block, steps):
    count = lax.axis_size("row")
    route = [(i, i + steps) for i in range(count) if 0 <= i % SPAN + steps < SPAN]
    return lax.ppermute(block, "row", route)


def gather_blocks(own):
    half = own.shape[0] // 2
    first = over_col(own, 1)
    second = over_col(own, 2)
    third_low = over_col(first[:half], 2)
    third_high = over_col(second[half:], 1)
    return own, first, second, jnp.concatenate([third_low, third_high], axis=0)


def gather_tokens(own):
    return jnp.concatenate(gather_blocks(own), axis=0)


def scatter_tokens(partial):
    blocks = jnp.split(partial, 4, axis=0)
    half = blocks[0].shape[0] // 2
    low = over_col(blocks[3][:half], 1)
    high = over_col(blocks[3][half:], 2)
    second_low = (blocks[2][:half].astype(F32) + low.astype(F32)).astype(BF)
    first_high = (blocks[1][half:].astype(F32) + high.astype(F32)).astype(BF)
    from_first = over_col(jnp.concatenate([blocks[1][:half], first_high], axis=0), 1)
    from_second = over_col(jnp.concatenate([second_low, blocks[2][half:]], axis=0), 2)
    return blocks[0].astype(F32) + from_first.astype(F32) + from_second.astype(F32)


def norm(resid, gain):
    inverse = lax.rsqrt(jnp.mean(resid * resid, axis=1, keepdims=True) + EPS)
    return (resid * inverse * gain[None, :]).astype(BF), inverse


def norm_backward(grad_normed, resid, inverse, gain):
    scaled = resid * inverse
    grad_gain = jnp.sum(grad_normed * scaled, axis=0)
    grad_scaled = grad_normed * gain[None, :]
    mean_term = jnp.mean(grad_scaled * scaled, axis=1, keepdims=True)
    return inverse * (grad_scaled - scaled * mean_term), grad_gain


def local(layer_input, g_out, attn_gain, w_query, w_keyval, w_out, ffn_gain, w_gate, w_up, w_down):
    section = lax.axis_index("section")
    col = lax.axis_index("col")
    peer = lax.axis_index("row") % SPAN
    cols = lax.axis_size("col")
    is_first = section == 0
    is_key = col % 2 == 0
    rows = layer_input.shape[2]
    width = layer_input.shape[3]
    own_rows = rows // cols
    full = width * cols
    heads = w_query.shape[2] // HD
    query_cols = w_query.shape[2]
    key_cols = w_keyval.shape[2]
    units = w_gate.shape[2]
    padded = -(-units // 256) * 256
    scale = 1.0 / math.sqrt(HD)

    def by_section(first, second):
        return jnp.where(is_first, first, second)

    def xor_rows(block):
        return jnp.concatenate(
            [lax.dynamic_slice_in_dim(block, (col ^ k) * own_rows, own_rows, 0) for k in range(cols)],
            axis=0,
        )

    def reorder(block, k):
        parts = jnp.split(block, cols, axis=0)
        return jnp.concatenate([parts[m ^ k] for m in range(cols)], axis=0)

    def gather_width(block):
        parts = [reorder(part, k) for k, part in enumerate(gather_blocks(xor_rows(block)))]
        total = jnp.zeros((block.shape[0], full), block.dtype)
        for k, part in enumerate(parts):
            total = lax.dynamic_update_slice_in_dim(total, part, (col ^ k) * width, 1)
        return total

    def tokens_from_width(block):
        total = jnp.zeros((own_rows, full), block.dtype)
        for k in range(cols):
            part = lax.dynamic_slice_in_dim(block, (col ^ k) * own_rows, own_rows, 0)
            if k:
                part = over_col(part, k)
            total = lax.dynamic_update_slice_in_dim(total, part, (col ^ k) * width, 1)
        return total

    def width_from_tokens(block):
        total = jnp.zeros((rows, width), block.dtype)
        for k in range(cols):
            part = lax.dynamic_slice_in_dim(block, (col ^ k) * width, width, 1)
            if k:
                part = over_col(part, k)
            total = lax.dynamic_update_slice_in_dim(total, part, (col ^ k) * own_rows, 0)
        return total

    gains_own = jnp.stack([attn_gain[0], ffn_gain[0]])
    gains_other = over_section(gains_own)
    gains_part = jnp.stack([by_section(gains_own, gains_other), by_section(gains_other, gains_own)])
    gains = jnp.zeros((2, 2, full), F32)
    for k in range(cols):
        part = over_col(gains_part, k) if k else gains_part
        gains = lax.dynamic_update_slice_in_dim(gains, part, (col ^ k) * width, 2)

    pad = ((0, 0), (0, padded - units))
    gate_own = jnp.pad(w_gate[0], pad)
    up_own = jnp.pad(w_up[0], pad)
    down_own = jnp.pad(w_down[0].T, pad)
    attn_own = jnp.concatenate([w_query[0], w_keyval[0], w_out[0].T], axis=1)
    shard = attn_own.shape[0]
    half_rows = shard // 2
    half_units = padded // 2

    def both_layers(low, high):
        got = over_section(by_section(high, low))
        return by_section(low, got), by_section(got, high)

    attn_parts = both_layers(attn_own[:half_rows], attn_own[half_rows:])
    gate_up_parts = both_layers(gate_own, up_own)
    down_parts = both_layers(down_own[:, :half_units], down_own[:, half_units:])
    weights = []
    for layer in range(2):
        attn_w = lax.all_gather(attn_parts[layer], ("row", "section"), axis=0, tiled=True)
        gate_up_w = lax.all_gather(gate_up_parts[layer], ("section", "row"), axis=0, tiled=True)
        down_w = lax.all_gather(down_parts[layer], ("section", "row"), axis=0, tiled=True)
        weights.append(
            (
                attn_w[:, :query_cols],
                attn_w[:, query_cols : query_cols + key_cols],
                attn_w[:, query_cols + key_cols :],
                gate_up_w[:full],
                gate_up_w[full:],
                down_w[:full],
                down_w[full:],
            )
        )

    order = jnp.concatenate(
        [(col ^ k) * own_rows + jnp.arange(own_rows, dtype=jnp.int32) for k in range(cols)]
    )
    positions = peer * rows + order
    cosine, sine = rope_tables(positions, HD)
    key_positions = jnp.concatenate([(peer - k) * rows + order for k in range(SPAN)])
    allowed = (key_positions[None, :] <= positions[:, None]) & (key_positions[None, :] >= 0)

    def swap_pairs(keys):
        parts = keys.reshape(SPAN, cols // 2, 2, own_rows, HD)
        return jnp.concatenate([parts[:, :, 1:], parts[:, :, :1]], axis=2).reshape(keys.shape)

    def layer_forward(resid, normed, inverse_attn, layer):
        w_q, w_kv, w_o, w_g, w_u, w_d0, w_d1 = weights[layer]
        query_raw = dot(normed, w_q, 1, 0).reshape(rows, heads, HD)
        queries = rotate(query_raw, cosine[:, None, :], sine[:, None, :]).astype(BF)
        own_cols = dot(normed, w_kv, 1, 0)
        own_cols = jnp.where(is_key, rotate(own_cols, cosine, sine), own_cols).astype(BF)
        mine = jnp.concatenate(
            [own_cols] + [along_row(own_cols, k) for k in range(1, SPAN)], axis=0
        )
        partner = swap_pairs(over_col(mine, 1))
        keys = jnp.where(is_key, mine, partner)
        values = jnp.where(is_key, partner, mine)
        scores = jnp.einsum("qhd,kd->hqk", queries, keys, preferred_element_type=F32) * scale
        unnormed = jnp.where(allowed[None], jnp.exp(scores), 0.0)
        total = jnp.sum(unnormed, axis=-1)
        probs = unnormed / total[..., None]
        attended = jnp.einsum("hqk,kd->qhd", probs.astype(BF), values, preferred_element_type=F32)
        attended = attended.reshape(rows, heads * HD).astype(BF)
        middle = resid + scatter_tokens(dot(attended, w_o, 1, 1).astype(BF))
        normed_own, inverse_ffn = norm(middle, gains[layer, 1])
        normed_ffn = gather_tokens(normed_own)
        gate = dot(normed_ffn, w_g, 1, 0)
        up = dot(normed_ffn, w_u, 1, 0)
        hidden = (jax.nn.silu(gate) * up).astype(BF)
        down = dot(hidden[:, :half_units], w_d0, 1, 1) + dot(hidden[:, half_units:], w_d1, 1, 1)
        result = middle + scatter_tokens(down.astype(BF))
        kept = (
            resid,
            inverse_attn,
            normed,
            queries,
            keys,
            values,
            jnp.log(total),
            attended,
            middle,
            inverse_ffn,
            normed_ffn,
            gate,
            up,
            hidden,
        )
        return result, kept

    def swap_add(left, keep, send):
        got = over_section(dot(left, send, 0, 0).astype(BF))
        return (dot(left, keep, 0, 0) + got.astype(F32)).astype(BF)

    def scatter_rows(total):
        return lax.psum_scatter(total, "row", scatter_dimension=0, tiled=True)

    def layer_backward(grad_own, grad_branch, kept, layer):
        w_q, w_kv, w_o, w_g, w_u, w_d0, w_d1 = weights[layer]
        (
            resid,
            inverse_attn,
            normed,
            queries,
            keys,
            values,
            log_total,
            attended,
            middle,
            inverse_ffn,
            normed_ffn,
            gate,
            up,
            hidden,
        ) = kept
        low, high = hidden[:, :half_units], hidden[:, half_units:]
        down_sum = scatter_rows(swap_add(grad_branch, by_section(low, high), by_section(high, low)))
        grad_hidden = jnp.concatenate(
            [dot(grad_branch, w_d0, 1, 0), dot(grad_branch, w_d1, 1, 0)], axis=1
        )
        sigma = jax.nn.sigmoid(gate)
        grad_gate_act = (grad_hidden * up * sigma * (1.0 + gate * (1.0 - sigma))).astype(BF)
        grad_up_act = (grad_hidden * gate * sigma).astype(BF)
        grad_normed_ffn = scatter_tokens(
            (dot(grad_gate_act, w_g, 1, 1) + dot(grad_up_act, w_u, 1, 1)).astype(BF)
        )
        gate_up_sum = scatter_rows(
            swap_add(
                normed_ffn,
                by_section(grad_gate_act, grad_up_act),
                by_section(grad_up_act, grad_gate_act),
            )
        )
        grad_middle, grad_gain_ffn = norm_backward(
            grad_normed_ffn, middle, inverse_ffn, gains[layer, 1]
        )
        grad_middle = grad_own + grad_middle
        grad_attn_out = gather_tokens(grad_middle.astype(BF))
        grad_wout = dot(grad_attn_out, attended, 0, 0)
        grad_attended = dot(grad_attn_out, w_o, 1, 0).astype(BF).reshape(rows, heads, HD)
        scores = jnp.einsum("qhd,kd->hqk", queries, keys, preferred_element_type=F32) * scale
        probs = jnp.where(allowed[None], jnp.exp(scores - log_total[..., None]), 0.0)
        grad_probs = jnp.einsum("qhd,kd->hqk", grad_attended, values, preferred_element_type=F32)
        grad_scores = (
            probs * (grad_probs - jnp.sum(probs * grad_probs, axis=-1, keepdims=True))
        ).astype(BF)
        grad_queries = (
            jnp.einsum("hqk,kd->qhd", grad_scores, keys, preferred_element_type=F32) * scale
        )
        grad_keys = (
            jnp.einsum("hqk,qhd->kd", grad_scores, queries, preferred_element_type=F32) * scale
        )
        grad_values = jnp.einsum(
            "hqk,qhd->kd", probs.astype(BF), grad_attended, preferred_element_type=F32
        )
        partner = swap_pairs(
            over_col(jnp.where(is_key, grad_values, grad_keys).astype(BF), 1)
        ).astype(F32)
        grad_cols = jnp.where(is_key, grad_keys, grad_values) + partner
        pieces = jnp.split(grad_cols, SPAN, axis=0)
        grad_mine = pieces[0]
        for k in range(1, SPAN):
            grad_mine = grad_mine + along_row(pieces[k].astype(BF), -k).astype(F32)
        grad_mine = jnp.where(is_key, rotate_back(grad_mine, cosine, sine), grad_mine).astype(BF)
        grad_query_raw = (
            rotate_back(grad_queries, cosine[:, None, :], sine[:, None, :])
            .astype(BF)
            .reshape(rows, heads * HD)
        )
        grad_normed = scatter_tokens(
            (dot(grad_query_raw, w_q, 1, 1) + dot(grad_mine, w_kv, 1, 1)).astype(BF)
        )
        attn_grads = jnp.concatenate(
            [
                dot(normed, grad_query_raw, 0, 0).astype(BF),
                dot(normed, grad_mine, 0, 0).astype(BF),
                grad_wout.astype(BF),
            ],
            axis=1,
        ).reshape(-1, 2, half_rows, attn_own.shape[1])
        got = over_section(by_section(attn_grads[:, 1], attn_grads[:, 0])).astype(F32)
        attn_grads = (by_section(attn_grads[:, 0], attn_grads[:, 1]).astype(F32) + got).astype(BF)
        attn_sum = scatter_rows(attn_grads.reshape(-1, attn_own.shape[1]))
        grad_resid, grad_gain_attn = norm_backward(
            grad_normed, resid, inverse_attn, gains[layer, 0]
        )
        return (
            grad_middle + grad_resid,
            (attn_sum, gate_up_sum, down_sum),
            jnp.stack([grad_gain_attn, grad_gain_ffn]),
        )

    x_full = gather_width(lax.dynamic_index_in_dim(layer_input[:, 0], section, 0, keepdims=False))
    top = lax.dynamic_index_in_dim(g_out[:, 0], section, 0, keepdims=False)
    normed, inverse = norm(x_full.astype(F32), gains[0, 0])
    result, kept_0 = layer_forward(x_full[:own_rows].astype(F32), normed, inverse[:own_rows], 0)
    act_0 = result.astype(BF)
    resid = act_0.astype(F32)
    normed_own, inverse = norm(resid, gains[1, 0])
    result, kept_1 = layer_forward(resid, gather_tokens(normed_own), inverse, 1)
    act_1 = result.astype(BF)

    top_branch = gather_width(top.astype(BF))
    top_own = tokens_from_width(top)
    grad_1, sums_1, gain_grads_1 = layer_backward(top_own, top_branch, kept_1, 1)
    grad_1 = grad_1.astype(BF)
    grad_0, sums_0, gain_grads_0 = layer_backward(
        grad_1.astype(F32), gather_tokens(grad_1), kept_0, 0
    )
    grad_0 = grad_0.astype(BF)

    def by_layer(first, second):
        first, second = width_from_tokens(first), width_from_tokens(second)
        got = over_section(by_section(second, first))
        return jnp.stack([by_section(first, got), by_section(got, second)])

    acts = by_layer(act_0, act_1)
    grads_in = by_layer(grad_0, grad_1)

    def to_layer(zero, one):
        one_low = lax.ppermute(one, "section", [(0, 1)])
        zero_high = lax.ppermute(zero, "section", [(1, 0)])
        return by_section(zero, one_low), by_section(zero_high, one)

    attn_final = jnp.concatenate(to_layer(sums_0[0], sums_1[0]), axis=0).astype(F32)
    final_gate, final_up = to_layer(sums_0[1], sums_1[1])
    down_final = jnp.concatenate(to_layer(sums_0[2], sums_1[2]), axis=1)[:, :units]
    gain_sums = lax.psum(jnp.stack([gain_grads_0, gain_grads_1]), ("section", "row", "col"))
    gain_sums = lax.dynamic_index_in_dim(gain_sums, section, 0, keepdims=False)
    gain_sums = lax.dynamic_slice_in_dim(gain_sums, col * width, width, 1)

    return (
        acts.reshape(1, 2, 1, rows, width),
        grads_in.reshape(1, 2, 1, rows, width),
        gain_sums[:1],
        attn_final[None, :, :query_cols],
        attn_final[None, :, query_cols : query_cols + key_cols],
        attn_final[:, query_cols + key_cols :].T[None],
        gain_sums[1:],
        final_gate[None, :, :units].astype(F32),
        final_up[None, :, :units].astype(F32),
        down_final.astype(F32).T[None],
    )


def solution(mesh):
    placed = (
        P(None, "row", None, "col"),
        P(None, "row", None, "col"),
        P("section", "col"),
        P("section", "row", "col"),
        P("section", "row", "col"),
        P("section", "col", "row"),
        P("section", "col"),
        P("section", "row", "col"),
        P("section", "row", "col"),
        P("section", "col", "row"),
    )
    return jax.shard_map(
        local,
        mesh=mesh,
        in_specs=placed,
        out_specs=(
            P("section", None, "row", None, "col"),
            P("section", None, "row", None, "col"),
            P("section", "col"),
            P("section", "row", "col"),
            P("section", "row", "col"),
            P("section", "col", "row"),
            P("section", "col"),
            P("section", "row", "col"),
            P("section", "row", "col"),
            P("section", "col", "row"),
        ),
        check_vma=False,
    )
```

time: 2250 us -> 1310 us (0.58)
  waiting for transfers between devices: 1390 us -> 674 us
  matrix products: 447 us -> 231 us
  starting transfers between devices: 43.5 us -> 133 us
  blocking collectives: 123 us -> 41.6 us
  other arithmetic: 133 us -> 95.3 us
    all_gather x17 -> x6, waiting for transfers between devices: 662 us -> 188 us  [the longest x2 126 us: local(): lax.all_gather(gate_up_parts[layer], ('section', 'row'), axis=0, tiled=True)]
    unnamed x39 -> x12, waiting for transfers between devices: 289 us -> 1.2 us
    dot_general x75 -> x54, matrix products: 447 us -> 231 us  [the longest x42 175 us: dot(): lax.dot_general(left, right, (((left_dim,), (right_dim,)), ((), ())), pre...]
    ppermute x25 -> x116, waiting for transfers between devices: 128 us -> 254 us  [the longest x86 186 us: over_col(): return lax.ppermute(block, 'col', [(i, i ^ step) for i in range(count)])]
    ppermute x25 -> x116, starting transfers between devices: 39.3 us -> 132 us  [the longest x86 94.4 us: over_col(): return lax.ppermute(block, 'col', [(i, i ^ step) for i in range(count)])]
    reduce_scatter x14 -> x6, waiting for transfers between devices: 308 us -> 231 us  [scatter_rows(): return lax.psum_scatter(total, 'row', scatter_dimension=0, tiled=True)]
    psum x11 -> x1, blocking collectives: 107 us -> 41.6 us  [local(): lax.psum(jnp.stack([gain_grads_0, gain_grads_1]), ('section', 'row', 'col'))]
    unnamed x325 -> x318, local copies, waits for them, and re-layouts: 67.8 us -> 44.7 us
  transfers between devices with their start and end apart: 60 -> 128, of which waited for: 49 -> 81; matrix products, arithmetic and copies ran while one was open for 16% -> 26% of each run, Pallas kernels for 0% -> 0%
where the time goes in v1:
time: 1310 us; the launch traced here: 1300 us
  waiting for transfers between devices  674 us (51%)
  matrix products  231 us (18%)
  starting transfers between devices  133 us (10%)
  local copies, waits for them, and re-layouts  103 us (8%)
  other arithmetic  95.3 us (7%)
  blocking collectives  41.6 us (3%)
  between operations  17.6 us (1%)
    reduce_scatter x6, waiting for transfers between devices, scatter_rows(): return lax.psum_scatter(total, 'row', scatter_dimension=0, tiled=True)  231 us
    ppermute x86, waiting for transfers between devices, over_col(): return lax.ppermute(block, 'col', [(i, i ^ step) for i in range(count)])  186 us
    dot_general x42, matrix products, dot(): lax.dot_general(left, right, (((left_dim,), (right_dim,)), ((), ())), pre...  175 us
    all_gather x2, waiting for transfers between devices, local(): lax.all_gather(gate_up_parts[layer], ('section', 'row'), axis=0, tiled=True)  126 us
    ppermute x86, starting transfers between devices, over_col(): return lax.ppermute(block, 'col', [(i, i ^ step) for i in range(count)])  94.4 us
    all_gather x2, waiting for transfers between devices, local(): lax.all_gather(down_parts[layer], ('section', 'row'), axis=0, tiled=True)  62 us
    unnamed x318, local copies, waits for them, and re-layouts  44.7 us
    psum x1, blocking collectives, local(): lax.psum(jnp.stack([gain_grads_0, gain_grads_1]), ('section', 'row', 'col'))  41.6 us
  transfers between devices with their start and end apart: 128, of which 81 were waited for; matrix products, arithmetic and copies ran while one was open for 26% of the time, Pallas kernels for 0%

profile of v1, /device:TPU:0, one launch (start us, length us, event | category | flops | bytes accessed | tf_op | source)
XLA Modules:
  0.0 1295.9 jit_solution(16315841469923638162)
XLA Ops:
  123.0 7.9 collective-permute-done.14
  150.7 32.2 %all-gather.9.cloned.1.call-done = bf16[3072,2304]{1,0:T(8,128)(2,1)} async-done(((bf16[384,2304]{1,0:T(8,128)(2,1)}), bf16[3072,2304]{1,0:T(8,128)(2,1)}) %all-gather.9.cloned.1.call-update) | async-done | bytes 14155792 | tf_op jit(solution)/shard_map/all_gather | solution.py:179
  182.9 7.3 fusion.40
  192.4 7.4 multiply_convert_fusion.5
  199.9 62.0 %all-gather.11.cloned.1.call-done = bf16[3072,1152]{1,0:T(8,128)(2,1)} async-done(((bf16[384,1152]{1,0:T(8,128)(2,1)}), bf16[3072,1152]{1,0:T(8,128)(2,1)}) %all-gather.11.cloned.1.call-update) | async-done | bytes 7077904 | tf_op jit(solution)/shard_map/all_gather | solution.py:180
  299.2 12.1 collective-permute-done.30
  387.0 6.9 fusion.51
  415.0 94.2 %all-gather.15.cloned.1.call-done = bf16[3072,2304]{1,0:T(8,128)(2,1)} async-done(((bf16[384,2304]{1,0:T(8,128)(2,1)}), bf16[3072,2304]{1,0:T(8,128)(2,1)}) %all-gather.15.cloned.1.call-update) | async-done | bytes 14155792 | tf_op jit(solution)/shard_map/all_gather | solution.py:179
  509.3 9.6 fusion.28
  518.9 11.2 multiply_convert_fusion.3
  569.3 13.7 %collective-permute-done.56 = f32[128,384]{1,0:T(8,128)S(1)} collective-permute-done((f32[128,384]{1,0:T(8,128)S(1)}, f32[128,384]{1,0:T(8,128)S(1)}, u32[]{:S(2)}, u32[]{:S(2)}) %collective-permute-start.56) | collective-permute-done | bytes 196640 | tf_op jit(solution)/shard_map/ppermute | solution.py:45
  589.3 7.0 collective-permute-done.65
  607.8 10.9 fusion.3
  620.4 7.0 fusion.5
  634.6 9.4 collective-permute-done.69
  686.6 7.4 collective-permute-done.74
  699.2 6.8 collective-permute-done.77
  719.5 7.8 fusion.34
  727.3 6.9 fusion.76
  780.0 11.1 fusion
  792.8 7.1 fusion.2
  857.3 7.3 fusion.15
  870.3 7.9 convolution_convert_fusion
  882.9 7.1 collective-permute-done.109
  890.0 10.4 add_convert_fusion
  902.0 9.1 convolution_convert_fusion.1
  911.5 11.2 collective-permute-done.108
  922.6 8.0 add_convert_fusion.1
  965.3 7.9 collective-permute-done.94
  983.4 41.6 %psum.7 = f32[2,2,1536]{2,1,0:T(2,128)S(1)} all-reduce(f32[2,2,1536]{2,1,0:T(2,128)S(1)} %pad_maximum_fusion.29), channel_id=1, replica_groups=mesh['section'=2,'row'=4,'col'=4] {'section','row','col'}, use_global_device_ids=true, to_apply=%region_16.17 | all-reduce | flops 6144 | bytes 49152 | tf_op jit(solution)/shard_map/psum | solution.py:386
  1036.0 110.4 %reduce-scatter.13.cloned.1.call-done = bf16[384,2304]{1,0:T(8,128)(2,1)} async-done(((bf16[1536,2304]{1,0:T(8,128)(2,1)}), bf16[384,2304]{1,0:T(8,128)(2,1)}) %reduce-scatter.13.cloned.1.call-update) | async-done | bytes 1769488 | tf_op jit(solution)/shard_map/reduce_scatter | solution.py:254
  1152.1 120.4 %reduce-scatter.11.cloned.1.call-done = bf16[384,2304]{1,0:T(8,128)(2,1)} async-done(((bf16[1536,2304]{1,0:T(8,128)(2,1)}), bf16[384,2304]{1,0:T(8,128)(2,1)}) %reduce-scatter.11.cloned.1.call-update) | async-done | bytes 1769488 | tf_op jit(solution)/shard_map/reduce_scatter | solution.py:254
  (849 shorter events, 591.3 us)
Async XLA Ops:
  7.2 47.0 %all-gather.7.cloned.1.call-start = ((), (), s32[]{:S(2)}) async-start(), calls=%async_computation.6 | async-start | bytes 3096576 | tf_op jit(solution)/shard_map/all_gather | solution.py:178
  12.4 170.5 %all-gather.9.cloned.1.call-start = ((), (), s32[]{:S(2)}) async-start(), calls=%async_computation.7 | async-start | bytes 15925248 | tf_op jit(solution)/shard_map/all_gather | solution.py:179
  23.0 238.9 %all-gather.11.cloned.1.call-start = ((), (), s32[]{:S(2)}) async-start(), calls=%async_computation.8 | async-start | bytes 7962624 | tf_op jit(solution)/shard_map/all_gather | solution.py:180
  30.0 287.8 %all-gather.13.cloned.1.call-start = ((), (), s32[]{:S(2)}) async-start(), calls=%async_computation.9 | async-start | bytes 3096576 | tf_op jit(solution)/shard_map/all_gather | solution.py:178
  30.6 356.4 %all-gather.17.cloned.1.call-start = ((), (), s32[]{:S(2)}) async-start(), calls=%async_computation.11 | async-start | bytes 7962624 | tf_op jit(solution)/shard_map/all_gather | solution.py:180
  31.2 478.0 %all-gather.15.cloned.1.call-start = ((), (), s32[]{:S(2)}) async-start(), calls=%async_computation.10 | async-start | bytes 15925248 | tf_op jit(solution)/shard_map/all_gather | solution.py:179
  31.7 15.9 %collective-permute-start = (bf16[512,384]{1,0:T(8,128)(2,1)S(1)}, bf16[512,384]{1,0:T(8,128)(2,1)S(1)}, u32[]{:S(2)}, u32[]{:S(2)}) collective-permute-start(bf16[512,384]{1,0:T(8,128)(2,1)S(1)} %get-tuple-element.199), channel_id=1, source_target_pairs={{0,1},{1,0},{2,3},{3,2},{4,5},{5,4},{6,7},{7,6},{8,9},{9,8},{10,11... | collective-permute-start | bytes 1179656 | tf_op jit(solution)/shard_map/ppermute | solution.py:45
  68.0 957.6 %reduce-scatter.9.cloned.1.call-start = ((), (), s32[]{:S(2)}) async-start(), calls=%async_computation.13 | async-start | bytes 1720320 | tf_op jit(solution)/shard_map/reduce_scatter | solution.py:254
  272.6 15.2 %collective-permute-start.57 = (bf16[512,384]{1,0:T(8,128)(2,1)S(1)}, bf16[512,384]{1,0:T(8,128)(2,1)S(1)}, u32[]{:S(2)}, u32[]{:S(2)}) collective-permute-start(bf16[512,384]{1,0:T(8,128)(2,1)S(1)} %get-tuple-element.177), channel_id=1, source_target_pairs={{0,1},{1,0},{2,3},{3,2},{4,5},{5,4},{6,7},{7,6},{8,9},{9,8},{10,11... | collective-permute-start | bytes 1179656 | tf_op jit(solution)/shard_map/ppermute | solution.py:45
  278.7 16.7 %collective-permute-start.24 = (bf16[128,1536]{1,0:T(8,128)(2,1)S(1)}, bf16[128,1536]{1,0:T(8,128)(2,1)S(1)}, u32[]{:S(2)}, u32[]{:S(2)}) collective-permute-start(bf16[128,1536]{1,0:T(8,128)(2,1)S(1)} %pad_maximum_fusion.13), channel_id=1, source_target_pairs={{0,1},{1,0},{2,3},{3,2},{4,5},{5,4},{6,7},{7,6},{8,9},{9,8},{10,11... | collective-permute-start | bytes 1179656 | tf_op jit(solution)/shard_map/ppermute | solution.py:45
  280.3 15.2 %collective-permute-start.26 = (bf16[128,1536]{1,0:T(8,128)(2,1)S(1)}, bf16[128,1536]{1,0:T(8,128)(2,1)S(1)}, u32[]{:S(2)}, u32[]{:S(2)}) collective-permute-start(bf16[128,1536]{1,0:T(8,128)(2,1)S(1)} %pad_maximum_fusion.14), channel_id=1, source_target_pairs={{0,2},{1,3},{2,0},{3,1},{4,6},{5,7},{6,4},{7,5},{8,10},{9,11},{10,... | collective-permute-start | bytes 1179656 | tf_op jit(solution)/shard_map/ppermute | solution.py:45
  282.9 280.4 %collective-permute-start.54 = (f32[128,384]{1,0:T(8,128)}, f32[128,384]{1,0:T(8,128)}, u32[]{:S(2)}, u32[]{:S(2)}) collective-permute-start(f32[128,384]{1,0:T(8,128)} %get-tuple-element.107), channel_id=1, source_target_pairs={{0,1},{1,0},{2,3},{3,2},{4,5},{5,4},{6,7},{7,6},{8,9},{9,8},{10,11... | collective-permute-start | bytes 589832 | tf_op jit(solution)/shard_map/ppermute | solution.py:45
  285.6 280.3 %collective-permute-start.55 = (f32[128,384]{1,0:T(8,128)}, f32[128,384]{1,0:T(8,128)}, u32[]{:S(2)}, u32[]{:S(2)}) collective-permute-start(f32[128,384]{1,0:T(8,128)} %get-tuple-element.106), channel_id=1, source_target_pairs={{0,2},{1,3},{2,0},{3,1},{4,6},{5,7},{6,4},{7,5},{8,10},{9,11},{10,... | collective-permute-start | bytes 589832 | tf_op jit(solution)/shard_map/ppermute | solution.py:45
  287.8 38.1 %collective-permute-start.59 = (bf16[256,384]{1,0:T(8,128)(2,1)}, bf16[256,384]{1,0:T(8,128)(2,1)}, u32[]{:S(2)}, u32[]{:S(2)}) collective-permute-start(bf16[256,384]{1,0:T(8,128)(2,1)} %get-tuple-element.171), channel_id=1, source_target_pairs={{0,1},{1,0},{2,3},{3,2},{4,5},{5,4},{6,7},{7,6},{8,9},{9,8},{10,11... | collective-permute-start | bytes 589832 | tf_op jit(solution)/shard_map/ppermute | solution.py:45
  296.0 15.3 %collective-permute-start.30 = (bf16[128,1536]{1,0:T(8,128)(2,1)S(1)}, bf16[128,1536]{1,0:T(8,128)(2,1)S(1)}, u32[]{:S(2)}, u32[]{:S(2)}) collective-permute-start(bf16[128,1536]{1,0:T(8,128)(2,1)S(1)} %get-tuple-element.63), channel_id=1, source_target_pairs={{0,1},{1,0},{2,3},{3,2},{4,5},{5,4},{6,7},{7,6},{8,9},{9,8},{10,11... | collective-permute-start | bytes 1179656 | tf_op jit(solution)/shard_map/ppermute | solution.py:45
  328.8 49.5 %collective-permute-start.60 = (bf16[256,384]{1,0:T(8,128)(2,1)}, bf16[256,384]{1,0:T(8,128)(2,1)}, u32[]{:S(2)}, u32[]{:S(2)}) collective-permute-start(bf16[256,384]{1,0:T(8,128)(2,1)} %slice.649), channel_id=1, source_target_pairs={{0,2},{1,3},{2,0},{3,1},{4,6},{5,7},{6,4},{7,5},{8,10},{9,11},{10,... | collective-permute-start | bytes 589832 | tf_op jit(solution)/shard_map/ppermute | solution.py:45
  539.3 15.5 %collective-permute-start.46 = (bf16[64,1536]{1,0:T(8,128)(2,1)S(1)}, bf16[64,1536]{1,0:T(8,128)(2,1)S(1)}, u32[]{:S(2)}, u32[]{:S(2)}) collective-permute-start(bf16[64,1536]{1,0:T(8,128)(2,1)S(1)} %get-tuple-element.111), channel_id=1, source_target_pairs={{0,2},{1,3},{2,0},{3,1},{4,6},{5,7},{6,4},{7,5},{8,10},{9,11},{10,... | collective-permute-start | bytes 589832 | tf_op jit(solution)/shard_map/ppermute | solution.py:45
  555.4 27.6 %collective-permute-start.47 = (bf16[128,1536]{1,0:T(8,128)(2,1)S(1)}, bf16[128,1536]{1,0:T(8,128)(2,1)S(1)}, u32[]{:S(2)}, u32[]{:S(2)}) collective-permute-start(bf16[128,1536]{1,0:T(8,128)(2,1)S(1)} %pad_maximum_fusion.17), channel_id=1, source_target_pairs={{0,1},{1,0},{2,3},{3,2},{4,5},{5,4},{6,7},{7,6},{8,9},{9,8},{10,11... | collective-permute-start | bytes 1179656 | tf_op jit(solution)/shard_map/ppermute | solution.py:45
  560.7 22.4 %collective-permute-start.49 = (bf16[128,1536]{1,0:T(8,128)(2,1)S(1)}, bf16[128,1536]{1,0:T(8,128)(2,1)S(1)}, u32[]{:S(2)}, u32[]{:S(2)}) collective-permute-start(bf16[128,1536]{1,0:T(8,128)(2,1)S(1)} %pad_maximum_fusion.18), channel_id=1, source_target_pairs={{0,2},{1,3},{2,0},{3,1},{4,6},{5,7},{6,4},{7,5},{8,10},{9,11},{10,... | collective-permute-start | bytes 1179656 | tf_op jit(solution)/shard_map/ppermute | solution.py:45
  562.7 20.4 %collective-permute-start.62 = (bf16[128,1536]{1,0:T(8,128)(2,1)S(1)}, bf16[128,1536]{1,0:T(8,128)(2,1)S(1)}, u32[]{:S(2)}, u32[]{:S(2)}) collective-permute-start(bf16[128,1536]{1,0:T(8,128)(2,1)S(1)} %pad_maximum_fusion.20), channel_id=1, source_target_pairs={{0,1},{1,0},{2,3},{3,2},{4,5},{5,4},{6,7},{7,6},{8,9},{9,8},{10,11... | collective-permute-start | bytes 1179656 | tf_op jit(solution)/shard_map/ppermute | solution.py:45
  563.3 19.8 %collective-permute-start.64 = (bf16[128,1536]{1,0:T(8,128)(2,1)S(1)}, bf16[128,1536]{1,0:T(8,128)(2,1)S(1)}, u32[]{:S(2)}, u32[]{:S(2)}) collective-permute-start(bf16[128,1536]{1,0:T(8,128)(2,1)S(1)} %pad_maximum_fusion.21), channel_id=1, source_target_pairs={{0,2},{1,3},{2,0},{3,1},{4,6},{5,7},{6,4},{7,5},{8,10},{9,11},{10,... | collective-permute-start | bytes 1179656 | tf_op jit(solution)/shard_map/ppermute | solution.py:45
  565.9 17.1 %collective-permute-start.56 = (f32[128,384]{1,0:T(8,128)S(1)}, f32[128,384]{1,0:T(8,128)S(1)}, u32[]{:S(2)}, u32[]{:S(2)}) collective-permute-start(f32[128,384]{1,0:T(8,128)S(1)} %copy-done.89), channel_id=1, source_target_pairs={{0,3},{1,2},{2,1},{3,0},{4,7},{5,6},{6,5},{7,4},{8,11},{9,10},{10,... | collective-permute-start | bytes 589832 | tf_op jit(solution)/shard_map/ppermute | solution.py:45
  765.4 261.8 %reduce-scatter.7.cloned.1.call-start = ((), (), s32[]{:S(2)}) async-start(), calls=%async_computation.12 | async-start | bytes 1720320 | tf_op jit(solution)/shard_map/reduce_scatter | solution.py:254
  852.4 178.2 %reduce-scatter.17.cloned.1.call-start = ((), (), s32[]{:S(2)}) async-start(), calls=%async_computation.17 | async-start | bytes 4423680 | tf_op jit(solution)/shard_map/reduce_scatter | solution.py:254
  864.6 169.0 %reduce-scatter.15.cloned.1.call-start = ((), (), s32[]{:S(2)}) async-start(), calls=%async_computation.16 | async-start | bytes 4423680 | tf_op jit(solution)/shard_map/reduce_scatter | solution.py:254
  882.8 263.5 %reduce-scatter.13.cloned.1.call-start = ((), (), s32[]{:S(2)}) async-start(), calls=%async_computation.15 | async-start | bytes 8847360 | tf_op jit(solution)/shard_map/reduce_scatter | solution.py:254
  900.4 372.2 %reduce-scatter.11.cloned.1.call-start = ((), (), s32[]{:S(2)}) async-start(), calls=%async_computation.14 | async-start | bytes 8847360 | tf_op jit(solution)/shard_map/reduce_scatter | solution.py:254
  958.4 17.4 %collective-permute-start.102 = (bf16[128,384]{1,0:T(8,128)(2,1)S(1)}, bf16[128,384]{1,0:T(8,128)(2,1)S(1)}, u32[]{:S(2)}, u32[]{:S(2)}) collective-permute-start(bf16[128,384]{1,0:T(8,128)(2,1)S(1)} %get-tuple-element.167), channel_id=1, source_target_pairs={{0,3},{1,2},{2,1},{3,0},{4,7},{5,6},{6,5},{7,4},{8,11},{9,10},{10,... | collective-permute-start | bytes 294920 | tf_op jit(solution)/shard_map/ppermute | solution.py:45
  983.2 43.8 %collective-permute-start.103 = (bf16[512,384]{1,0:T(8,128)(2,1)S(1)}, bf16[512,384]{1,0:T(8,128)(2,1)S(1)}, u32[]{:S(2)}, u32[]{:S(2)}) collective-permute-start(bf16[512,384]{1,0:T(8,128)(2,1)S(1)} %broadcast_select_fusion.12), channel_id=1, source_target_pairs={{0,16},{16,0},{1,17},{17,1},{2,18},{18,2},{3,19},{19,3},{4,20},{20... | collective-permute-start | bytes 1179656 | tf_op jit(solution)/shard_map/ppermute | solution.py:49
  1030.5 120.6 %collective-permute-start.114 = (bf16[384,1152]{1,0:T(8,128)(2,1)}, bf16[384,1152]{1,0:T(8,128)(2,1)}, u32[]{:S(2)}, u32[]{:S(2)}) collective-permute-start(bf16[384,1152]{1,0:T(8,128)(2,1)} %reduce-scatter.17.cloned.1.call-done), channel_id=1, source_target_pairs={{0,16},{1,17},{2,18},{3,19},{4,20},{5,21},{6,22},{7,23},{8,24},{9,... | collective-permute-start | bytes 2654216 | tf_op jit(solution)/shard_map/ppermute | solution.py:379
  1033.7 240.3 %collective-permute-start.115 = (bf16[384,1152]{1,0:T(8,128)(2,1)}, bf16[384,1152]{1,0:T(8,128)(2,1)}, u32[]{:S(2)}, u32[]{:S(2)}) collective-permute-start(bf16[384,1152]{1,0:T(8,128)(2,1)} %reduce-scatter.15.cloned.1.call-done), channel_id=1, source_target_pairs={{16,0},{17,1},{18,2},{19,3},{20,4},{21,5},{22,6},{23,7},{24,8},{25... | collective-permute-start | bytes 2654216 | tf_op jit(solution)/shard_map/ppermute | solution.py:380
  1146.4 132.1 %collective-permute-start.110 = (bf16[384,2304]{1,0:T(8,128)(2,1)}, bf16[384,2304]{1,0:T(8,128)(2,1)}, u32[]{:S(2)}, u32[]{:S(2)}) collective-permute-start(bf16[384,2304]{1,0:T(8,128)(2,1)} %reduce-scatter.13.cloned.1.call-done), channel_id=1, source_target_pairs={{0,16},{1,17},{2,18},{3,19},{4,20},{5,21},{6,22},{7,23},{8,24},{9,... | collective-permute-start | bytes 5308424 | tf_op jit(solution)/shard_map/ppermute | solution.py:379
  (242 other events, 2344.1 us)
Sparse Core Ops, SparseCore 0:
  12.6 37.4 all-gather.6
  52.2 130.6 all-gather.8
  185.1 76.7 all-gather.10
  263.4 33.4 all-gather.12
  298.3 73.4 all-gather.16
  373.3 135.8 all-gather.14
  765.5 29.5 reduce-scatter.8
  852.5 30.3 reduce-scatter.6
  885.2 65.2 reduce-scatter.16
  952.6 67.6 reduce-scatter.14
  1022.7 123.6 reduce-scatter.12
  1148.5 124.0 reduce-scatter.10

commit v2 on v1

v2 whole, which is shorter than its diff:
```python
import functools
import math

import jax
import jax.numpy as jnp
from jax import lax
from jax.experimental import pallas as pl
from jax.experimental.pallas import tpu as pltpu
from jax.sharding import PartitionSpec as P


HD = 128
SPAN = 4
EPS = 1e-06
THETA = 1000000.0
BF = jnp.bfloat16
F32 = jnp.float32


def dot(left, right, left_dim, right_dim):
    return lax.dot_general(
        left, right, (((left_dim,), (right_dim,)), ((), ())), preferred_element_type=F32
    )


def rope_tables(positions, head_size):
    half = head_size // 2
    freqs = THETA ** (-(jnp.arange(half, dtype=F32) * 2.0) / head_size)
    angles = positions.astype(F32)[:, None] * freqs[None, :]
    angles = jnp.concatenate([angles, angles], axis=-1)
    return (jnp.cos(angles), jnp.sin(angles))


ROW = "row"


def after(value, *others):
    return lax.optimization_barrier((value, *others))


def over_col(block, step):
    count = lax.axis_size("col")
    return lax.ppermute(block, "col", [(i, i ^ step) for i in range(count)])


def over_section(block):
    return lax.ppermute(block, "section", [(0, 1), (1, 0)])


def along_row(block, steps):
    count = lax.axis_size(ROW)
    route = [(i, i + steps) for i in range(count) if 0 <= i % SPAN + steps < SPAN]
    return lax.ppermute(block, ROW, route)


def gather_blocks(own):
    half = own.shape[0] // 2
    first = over_col(own, 1)
    second = over_col(own, 2)
    third_low = over_col(first[:half], 2)
    third_high = over_col(second[half:], 1)
    return own, first, second, jnp.concatenate([third_low, third_high], axis=0)


def gather_tokens(own):
    return jnp.concatenate(gather_blocks(own), axis=0)


def scatter_tokens(partial):
    blocks = jnp.split(partial, 4, axis=0)
    got = [over_col(blocks[k], k).astype(F32) for k in (3, 1, 2)]
    return blocks[0].astype(F32) + got[0] + got[1] + got[2]


def norm(resid, gain):
    inverse = lax.rsqrt(jnp.mean(resid * resid, axis=1, keepdims=True) + EPS)
    return (resid * inverse * gain[None, :]).astype(BF), inverse


def norm_backward(grad_normed, resid, inverse, gain):
    scaled = resid * inverse
    grad_gain = jnp.sum(grad_normed * scaled, axis=0)
    grad_scaled = grad_normed * gain[None, :]
    mean_term = jnp.mean(grad_scaled * scaled, axis=1, keepdims=True)
    return inverse * (grad_scaled - scaled * mean_term), grad_gain


def qkv_kernel(heads, x_ref, w_ref, cos_ref, sign_ref, q_ref, kv_ref):
    raw = jnp.dot(x_ref[...], w_ref[...], preferred_element_type=F32)
    cosine, signed = cos_ref[...], sign_ref[...]
    for h in range(heads + 1):
        z = raw[:, h * HD : (h + 1) * HD]
        z = (z * cosine + pltpu.roll(z, HD // 2, 1) * signed).astype(BF)
        if h < heads:
            q_ref[:, h * HD : (h + 1) * HD] = z
        else:
            kv_ref[:, :HD] = z
    kv_ref[:, HD:] = raw[:, (heads + 1) * HD :].astype(BF)


def project_turn(normed, weight, cosine, signed, heads):
    rows, depth = normed.shape
    step = rows // 2
    cols = (heads + 2) * HD
    return pl.pallas_call(
        functools.partial(qkv_kernel, heads),
        grid=(2,),
        in_specs=[
            pl.BlockSpec((step, depth), lambda i: (i, 0)),
            pl.BlockSpec((depth, cols), lambda i: (0, 0)),
            pl.BlockSpec((step, HD), lambda i: (i, 0)),
            pl.BlockSpec((step, HD), lambda i: (i, 0)),
        ],
        out_specs=[
            pl.BlockSpec((step, heads * HD), lambda i: (i, 0)),
            pl.BlockSpec((step, 2 * HD), lambda i: (i, 0)),
        ],
        out_shape=[
            jax.ShapeDtypeStruct((rows, heads * HD), BF),
            jax.ShapeDtypeStruct((rows, 2 * HD), BF),
        ],
        cost_estimate=pl.CostEstimate(
            flops=2 * rows * depth * cols,
            bytes_accessed=2 * (rows * depth + depth * cols + rows * cols),
            transcendentals=0,
        ),
        name="project_turn",
    )(normed, weight, cosine, signed)


def attend_kernel(scale, peer_ref, col_ref, row_ref, q_ref, *refs):
    pieces, (o_ref, lse_ref, e_ref, total_ref, acc_ref) = refs[:SPAN], refs[SPAN:]
    peer = peer_ref[0]
    q = q_ref[...]

    def exps(k):
        s = lax.dot_general(
            pieces[k][:, :HD], q, (((1,), (1,)), ((), ())), preferred_element_type=F32
        )
        return jnp.exp(s * scale)

    e = jnp.where(col_ref[...] <= row_ref[...], exps(0), 0.0)
    e_ref[0] = e
    total_ref[...] = jnp.sum(e, axis=0, keepdims=True)
    for k in range(1, SPAN):

        @pl.when(peer >= k)
        def _():
            e = exps(k)
            e_ref[k] = e
            total_ref[...] += jnp.sum(e, axis=0, keepdims=True)

    total = total_ref[...]
    lse_ref[0] = jnp.log(total)
    shrink = jnp.where(total > 1.0, 2.0**-64, 1.0)
    inverse = 1.0 / (total * shrink)

    def term(k):
        p = ((e_ref[k] * shrink) * inverse).astype(BF)
        return lax.dot_general(
            pieces[k][:, HD:], p, (((0,), (0,)), ((), ())), preferred_element_type=F32
        )

    acc_ref[...] = term(0)
    for k in range(1, SPAN):

        @pl.when(peer >= k)
        def _():
            acc_ref[...] += term(k)

    o_ref[...] = acc_ref[...].T.astype(BF)


def attend(queries, pieces, peer, order, heads, scale):
    rows = queries.shape[0]
    full = SPAN * rows
    return pl.pallas_call(
        functools.partial(attend_kernel, scale),
        grid=(heads,),
        in_specs=[
            pl.BlockSpec(memory_space=pltpu.SMEM),
            pl.BlockSpec((rows, 1), lambda h: (0, 0)),
            pl.BlockSpec((1, rows), lambda h: (0, 0)),
            pl.BlockSpec((rows, HD), lambda h: (0, h)),
            *[pl.BlockSpec((rows, 2 * HD), lambda h: (0, 0))] * SPAN,
        ],
        out_specs=[
            pl.BlockSpec((rows, HD), lambda h: (0, h)),
            pl.BlockSpec((1, 1, rows), lambda h: (h, 0, 0)),
        ],
        out_shape=[
            jax.ShapeDtypeStruct((rows, heads * HD), BF),
            jax.ShapeDtypeStruct((heads, 1, rows), F32),
        ],
        scratch_shapes=[
            pltpu.VMEM((SPAN, rows, rows), F32),
            pltpu.VMEM((1, rows), F32),
            pltpu.VMEM((HD, rows), F32),
        ],
        cost_estimate=pl.CostEstimate(
            flops=4 * heads * rows * full * HD,
            bytes_accessed=4 * rows * HD * (heads + SPAN),
            transcendentals=heads * rows * full,
        ),
        name="attend",
    )(peer, order[:, None], order[None, :], queries, *pieces)


def attend_back_kernel(scale, peer_ref, col_ref, row_ref, cos_ref, sign_ref, q_ref, do_ref, lse_ref, *refs):
    pieces = refs[:SPAN]
    dq_ref, outs = refs[SPAN], refs[SPAN + 1 : 2 * SPAN + 1]
    p_ref, dp_ref, sum_ref, turn_ref, acc_ref = refs[2 * SPAN + 1 :]
    h = pl.program_id(0)
    last = pl.num_programs(0) - 1
    peer = peer_ref[0]
    q, do = q_ref[...], do_ref[...]
    lse = lse_ref[0]

    def first(k):
        nt = (((1,), (1,)), ((), ()))
        s = lax.dot_general(pieces[k][:, :HD], q, nt, preferred_element_type=F32)
        p = jnp.exp(s * scale - lse)
        if k == 0:
            p = jnp.where(col_ref[...] <= row_ref[...], p, 0.0)
        dp = lax.dot_general(pieces[k][:, HD:], do, nt, preferred_element_type=F32)
        p_ref[k] = p
        dp_ref[k] = dp
        return jnp.sum(p * dp, axis=0, keepdims=True)

    def second(k):
        p = p_ref[k]
        ds = (p * (dp_ref[k] - sum_ref[...])).astype(BF)
        dk = jnp.dot(ds, q, preferred_element_type=F32)
        dv = jnp.dot(p.astype(BF), do, preferred_element_type=F32)

        @pl.when(h == 0)
        def _():
            acc_ref[k, :, :HD] = dk
            acc_ref[k, :, HD:] = dv

        @pl.when(h > 0)
        def _():
            acc_ref[k, :, :HD] += dk
            acc_ref[k, :, HD:] += dv

        return lax.dot_general(
            pieces[k][:, :HD], ds, (((0,), (0,)), ((), ())), preferred_element_type=F32
        )

    sum_ref[...] = first(0)
    for k in range(1, SPAN):

        @pl.when(peer >= k)
        def _():
            sum_ref[...] += first(k)

    turn_ref[...] = second(0)
    for k in range(1, SPAN):

        @pl.when(peer >= k)
        def _():
            turn_ref[...] += second(k)

    dq = turn_ref[...].T * scale
    dq = dq * cos_ref[...] - pltpu.roll(dq, HD // 2, 1) * sign_ref[...]
    dq_ref[...] = dq.astype(BF)

    @pl.when(h == last)
    def _():
        for k in range(SPAN):

            @pl.when(peer >= k)
            def _():
                outs[k][:, :HD] = (acc_ref[k, :, :HD] * scale).astype(outs[k].dtype)
                outs[k][:, HD:] = acc_ref[k, :, HD:].astype(outs[k].dtype)

            @pl.when(peer < k)
            def _():
                outs[k][...] = jnp.zeros(outs[k].shape, outs[k].dtype)


def attend_back(queries, grads, lse, pieces, peer, order, cosine, signed, heads, scale):
    rows = queries.shape[0]
    full = SPAN * rows
    whole = pl.BlockSpec((rows, 2 * HD), lambda h: (0, 0))
    table = pl.BlockSpec((rows, HD), lambda h: (0, 0))
    one_head = pl.BlockSpec((rows, HD), lambda h: (0, h))
    return pl.pallas_call(
        functools.partial(attend_back_kernel, scale),
        grid=(heads,),
        in_specs=[
            pl.BlockSpec(memory_space=pltpu.SMEM),
            pl.BlockSpec((rows, 1), lambda h: (0, 0)),
            pl.BlockSpec((1, rows), lambda h: (0, 0)),
            table,
            table,
            one_head,
            one_head,
            pl.BlockSpec((1, 1, rows), lambda h: (h, 0, 0)),
            *[whole] * SPAN,
        ],
        out_specs=[one_head, *[whole] * SPAN],
        out_shape=[
            jax.ShapeDtypeStruct((rows, heads * HD), BF),
            jax.ShapeDtypeStruct((rows, 2 * HD), F32),
            *[jax.ShapeDtypeStruct((rows, 2 * HD), BF)] * (SPAN - 1),
        ],
        scratch_shapes=[
            pltpu.VMEM((SPAN, rows, rows), F32),
            pltpu.VMEM((SPAN, rows, rows), F32),
            pltpu.VMEM((1, rows), F32),
            pltpu.VMEM((HD, rows), F32),
            pltpu.VMEM((SPAN, rows, 2 * HD), F32),
        ],
        cost_estimate=pl.CostEstimate(
            flops=10 * heads * rows * full * HD,
            bytes_accessed=4 * rows * HD * (2 * heads + 2 * SPAN),
            transcendentals=heads * rows * full,
        ),
        name="attend_back",
    )(peer, order[:, None], order[None, :], cosine, signed, queries, grads, lse, *pieces)


def step(layer_input, g_out, attn_gain, w_query, w_keyval, w_out, ffn_gain, w_gate, w_up, w_down):
    section = lax.axis_index("section")
    col = lax.axis_index("col")
    peer = lax.axis_index(ROW) % SPAN
    cols = lax.axis_size("col")
    is_first = section == 0
    is_key = col % 2 == 0
    rows = layer_input.shape[2]
    width = layer_input.shape[3]
    own_rows = rows // cols
    full = width * cols
    heads = w_query.shape[2] // HD
    query_cols = w_query.shape[2]
    qkv_cols = query_cols + 2 * HD
    units = w_gate.shape[2]
    scale = 1.0 / math.sqrt(HD)

    def by_section(first, second):
        return jnp.where(is_first, first, second)

    def by_key(first, second):
        return jnp.where(is_key, first, second)

    def xor_rows(block):
        return jnp.concatenate(
            [lax.dynamic_slice_in_dim(block, (col ^ k) * own_rows, own_rows, 0) for k in range(cols)],
            axis=0,
        )

    def reorder(block, k):
        parts = jnp.split(block, cols, axis=0)
        return jnp.concatenate([parts[m ^ k] for m in range(cols)], axis=0)

    def gather_width(block):
        parts = [reorder(part, k) for k, part in enumerate(gather_blocks(xor_rows(block)))]
        total = jnp.zeros((block.shape[0], full), block.dtype)
        for k, part in enumerate(parts):
            total = lax.dynamic_update_slice_in_dim(total, part, (col ^ k) * width, 1)
        return total

    def tokens_from_width(block):
        total = jnp.zeros((own_rows, full), block.dtype)
        for k in range(cols):
            part = lax.dynamic_slice_in_dim(block, (col ^ k) * own_rows, own_rows, 0)
            if k:
                part = over_col(part, k)
            total = lax.dynamic_update_slice_in_dim(total, part, (col ^ k) * width, 1)
        return total

    def width_from_tokens(block):
        total = jnp.zeros((rows, width), block.dtype)
        for k in range(cols):
            part = lax.dynamic_slice_in_dim(block, (col ^ k) * width, width, 1)
            if k:
                part = over_col(part, k)
            total = lax.dynamic_update_slice_in_dim(total, part, (col ^ k) * own_rows, 0)
        return total

    gains_own = jnp.stack([attn_gain[0], ffn_gain[0]])
    gains_other = over_section(gains_own)
    gains_part = jnp.stack([by_section(gains_own, gains_other), by_section(gains_other, gains_own)])
    gains = jnp.zeros((2, 2, full), F32)
    for k in range(cols):
        part = over_col(gains_part, k) if k else gains_part
        gains = lax.dynamic_update_slice_in_dim(gains, part, (col ^ k) * width, 2)

    shard = w_query.shape[1]
    keyval_other = over_col(w_keyval[0], 1)
    attn_own = jnp.concatenate(
        [
            w_query[0],
            by_key(w_keyval[0], keyval_other),
            by_key(keyval_other, w_keyval[0]),
            w_out[0].T,
        ],
        axis=1,
    )
    half_rows = shard // 2
    wide = -(-units // 256) * 256
    half_units = wide // 2

    def both_layers(low, high):
        got = over_section(by_section(high, low))
        return by_section(low, got), by_section(got, high)

    def widen(array):
        return jnp.pad(array, ((0, 0), (0, wide - units)))

    down_own = widen(w_down[0].T)
    attn_parts = both_layers(attn_own[:half_rows], attn_own[half_rows:])
    gate_up_parts = both_layers(widen(w_gate[0]), widen(w_up[0]))
    down_parts = both_layers(down_own[:, :half_units], down_own[:, half_units:])

    def gather_layers(part):
        both = lax.all_gather(part, ("section", ROW), axis=0, tiled=True)
        return both[:full], both[full:]

    def gather_attn(part):
        return lax.all_gather(part, (ROW, "section"), axis=0, tiled=True)

    order = jnp.concatenate(
        [(col ^ k) * own_rows + jnp.arange(own_rows, dtype=jnp.int32) for k in range(cols)]
    )
    positions = peer * rows + order
    cosine, sine = rope_tables(positions, HD)
    signed = jnp.where(jnp.arange(HD) < HD // 2, -sine, sine)

    def swap_halves(values):
        return jnp.concatenate([values[:, HD // 2 :], values[:, : HD // 2]], axis=1)

    peers = jnp.reshape(peer, (1,)).astype(jnp.int32)

    def attn_forward(normed, attn_w):
        queries, key_value = project_turn(normed, attn_w, cosine, signed, heads)
        pieces = [key_value] + [along_row(key_value, k) for k in range(1, SPAN)]
        attended, lse = attend(queries, pieces, peers, order, heads, scale)
        return attended, (normed, queries, pieces, lse, attended)

    def attn_out(resid, attended, attn_w):
        return resid + scatter_tokens(dot(attended, attn_w[:, qkv_cols:], 1, 1).astype(BF))

    def ffn_gather(middle, ffn_gain):
        normed_own, inverse_ffn = norm(middle, ffn_gain)
        return gather_tokens(normed_own), inverse_ffn

    def ffn_in(normed_ffn, gate_up_w):
        gate = dot(normed_ffn, gate_up_w[0], 1, 0)
        up = dot(normed_ffn, gate_up_w[1], 1, 0)
        return gate.astype(BF), up.astype(BF), (jax.nn.silu(gate) * up).astype(BF)

    def ffn_out(hidden, down_w):
        out = dot(hidden[:, :half_units], down_w[0], 1, 1)
        return scatter_tokens((out + dot(hidden[:, half_units:], down_w[1], 1, 1)).astype(BF))

    def swap_add(left, first, second):
        got = over_section(dot(left, by_section(second, first), 0, 0).astype(BF))
        return (dot(left, by_section(first, second), 0, 0) + got.astype(F32)).astype(BF)

    def scatter_rows(total):
        return lax.psum_scatter(total, ROW, scatter_dimension=0, tiled=True)

    def ffn_backward(grad_own, grad_branch, kept, ffn_gain, gate_up_w, down_w):
        middle, inverse_ffn, normed_ffn, gate, up, hidden = kept
        down_total = swap_add(grad_branch, hidden[:, :half_units], hidden[:, half_units:])
        grad_branch, down_total = after(grad_branch, down_total)
        down_sum = scatter_rows(down_total)
        grad_hidden = jnp.concatenate(
            [dot(grad_branch, down_w[0], 1, 0), dot(grad_branch, down_w[1], 1, 0)], axis=1
        )
        gate, up = gate.astype(F32), up.astype(F32)
        sigma = jax.nn.sigmoid(gate)
        dgate = (grad_hidden * up * sigma * (1.0 + gate * (1.0 - sigma))).astype(BF)
        dup = (grad_hidden * gate * sigma).astype(BF)
        grad_normed_ffn = scatter_tokens(
            (dot(dgate, gate_up_w[0], 1, 1) + dot(dup, gate_up_w[1], 1, 1)).astype(BF)
        )
        gate_up_total = swap_add(normed_ffn, dgate, dup)
        grad_normed_ffn, gate_up_total = after(grad_normed_ffn, gate_up_total)
        gate_up_sum = scatter_rows(gate_up_total)
        grad_middle, grad_gain_ffn = norm_backward(grad_normed_ffn, middle, inverse_ffn, ffn_gain)
        return grad_own + grad_middle, gate_up_sum, down_sum, grad_gain_ffn

    def attn_backward(grad_middle, resid, inverse_attn, kept, attn_gain, attn_w, *others):
        normed, queries, pieces, lse, attended = kept
        w_qkv, w_o = attn_w[:, :qkv_cols], attn_w[:, qkv_cols:]
        grad_attn_out = gather_tokens(grad_middle.astype(BF))
        grad_attended = dot(grad_attn_out, w_o, 1, 0).astype(BF)
        grad_query_raw, grad_mine, *grad_sent = attend_back(
            queries, grad_attended, lse, pieces, peers, order, cosine, signed, heads, scale
        )
        for k in range(1, SPAN):
            grad_mine = grad_mine + along_row(grad_sent[k - 1], -k).astype(F32)
        grad_wout = dot(grad_attn_out, attended, 0, 0).astype(BF)
        grad_wquery = dot(normed, grad_query_raw, 0, 0).astype(BF)
        got = over_section(by_section(grad_wout, grad_wquery))
        early = by_section(grad_wquery, grad_wout).astype(F32) + got.astype(F32)
        grad_mine, early, *others = after(grad_mine, early.astype(BF), *others)
        early = scatter_rows(early)
        grad_key = grad_mine[:, :HD]
        grad_keyval = jnp.concatenate(
            [
                (grad_key * cosine - swap_halves(grad_key) * signed).astype(BF),
                grad_mine[:, HD:].astype(BF),
            ],
            axis=1,
        )
        grad_wkeyval = dot(normed, grad_keyval, 0, 0).astype(BF)
        grad_wkey, grad_wvalue = grad_wkeyval[:, :HD], grad_wkeyval[:, HD:]
        got = over_section(by_section(grad_wvalue, grad_wkey))
        late = by_section(grad_wkey, grad_wvalue).astype(F32) + got.astype(F32)
        late = late.astype(BF)
        grad_normed = (
            dot(grad_query_raw, w_qkv[:, :query_cols], 1, 1)
            + dot(grad_keyval, w_qkv[:, query_cols:], 1, 1)
        ).astype(BF)
        grad_normed = scatter_tokens(grad_normed)
        grad_resid, grad_gain_attn = norm_backward(grad_normed, resid, inverse_attn, attn_gain)
        return grad_middle + grad_resid, early, late, grad_gain_attn, others

    def own_width(block):
        block = lax.dynamic_slice_in_dim(block, col * width, width, 1)
        return xor_rows(block)

    def core_swap(layer, block):
        return block, lax.ppermute(block, "section", [(1 - layer, layer)])

    def by_layer(first, second):
        first, first_got = first
        second, second_got = second
        return jnp.stack([by_section(first, second_got), by_section(first_got, second)])

    def to_core(layer, block):
        got = lax.ppermute(block, "section", [(1 - layer, layer)])
        return (block, got) if layer == 0 else (got, block)

    attn_w = [gather_attn(attn_parts[0])]
    x_full = gather_width(lax.dynamic_index_in_dim(layer_input[:, 0], section, 0, keepdims=False))
    gate_up_w = [gather_layers(gate_up_parts[0])]
    normed, inverse = norm(x_full.astype(F32), gains[0, 0])
    resid_0, inverse_0 = x_full[:own_rows].astype(F32), inverse[:own_rows]
    _, down_part = after(normed, down_parts[0])
    down_w = [gather_layers(down_part)]
    attended, kept_attn_0 = attn_forward(normed, attn_w[0])
    _, attn_part = after(attended, attn_parts[1])
    attn_w.append(gather_attn(attn_part))
    middle = attn_out(resid_0, attended, attn_w[0])
    _, gate_up_part = after(middle, gate_up_parts[1])
    gate_up_w.append(gather_layers(gate_up_part))
    normed_ffn, inverse_ffn = ffn_gather(middle, gains[0, 1])
    gate, up, hidden = ffn_in(normed_ffn, gate_up_w[0])
    _, down_part = after(hidden, down_parts[1])
    down_w.append(gather_layers(down_part))
    result = middle + ffn_out(hidden, down_w[0])
    kept_ffn_0 = (middle, inverse_ffn, normed_ffn, gate, up, hidden)
    x_full = gather_tokens(result.astype(BF))
    act_0 = core_swap(0, own_width(x_full))
    normed, inverse = norm(x_full.astype(F32), gains[1, 0])
    resid_1, inverse_1 = x_full[:own_rows].astype(F32), inverse[:own_rows]
    attended, kept_attn_1 = attn_forward(normed, attn_w[1])
    _, g_out = after(attended, g_out)
    middle = attn_out(resid_1, attended, attn_w[1])
    normed_ffn, inverse_ffn = ffn_gather(middle, gains[1, 1])
    top = lax.dynamic_index_in_dim(g_out[:, 0], section, 0, keepdims=False)
    top_branch = gather_width(top.astype(BF))
    top_own = tokens_from_width(top)
    gate, up, hidden = ffn_in(normed_ffn, gate_up_w[1])
    result = middle + ffn_out(hidden, down_w[1])
    kept_ffn_1 = (middle, inverse_ffn, normed_ffn, gate, up, hidden)
    act_1 = core_swap(1, width_from_tokens(result.astype(BF)))
    acts = by_layer(act_0, act_1)

    grad_middle, gate_up_1, down_1, gain_ffn_1 = ffn_backward(
        top_own, top_branch, kept_ffn_1, gains[1, 1], gate_up_w[1], down_w[1]
    )
    grad_1, early_1, late_1, gain_attn_1, (acts,) = attn_backward(
        grad_middle, resid_1, inverse_1, kept_attn_1, gains[1, 0], attn_w[1], acts
    )
    grad_1 = grad_1.astype(BF)
    branch, late_1 = after(gather_tokens(grad_1), late_1)
    late_1 = scatter_rows(late_1)
    grads_1 = core_swap(1, own_width(branch))
    grad_middle, gate_up_0, down_0, gain_ffn_0 = ffn_backward(
        grad_1.astype(F32), branch, kept_ffn_0, gains[0, 1], gate_up_w[0], down_w[0]
    )
    grad_0, early_0, late_0, gain_attn_0, _ = attn_backward(
        grad_middle, resid_0, inverse_0, kept_attn_0, gains[0, 0], attn_w[0]
    )
    grads_in = by_layer(core_swap(0, width_from_tokens(grad_0.astype(BF))), grads_1)
    late_0 = scatter_rows(late_0)

    def own_layer(first, second):
        return jax.tree.map(by_section, tuple(first), tuple(second))

    def final(zero, one):
        return own_layer(to_core(0, zero), to_core(1, one))

    final_query, final_out = final(early_0, early_1)
    final_key, final_value = final(late_0, late_1)
    final_keyval = by_key(final_key, final_value).astype(F32) + over_col(
        by_key(final_value, final_key), 1
    ).astype(F32)
    final_gate, final_up = final(gate_up_0, gate_up_1)
    final_down = jnp.concatenate(final(down_0, down_1), axis=1)[:, :units]

    gain_grads_0 = jnp.stack([gain_attn_0, gain_ffn_0])
    gain_grads_1 = jnp.stack([gain_attn_1, gain_ffn_1])
    gain_sums = by_section(gain_grads_0, gain_grads_1) + over_section(
        by_section(gain_grads_1, gain_grads_0)
    )
    gain_parts = [
        lax.dynamic_slice_in_dim(gain_sums, (col ^ k) * width, width, 1) for k in range(cols)
    ]
    gain_sums = gain_parts[0] + sum(over_col(gain_parts[k], k) for k in range(1, cols))
    row_count = lax.axis_size(ROW)
    step = 1
    while step < row_count:
        gain_sums = gain_sums + lax.ppermute(
            gain_sums, ROW, [(i, i ^ step) for i in range(row_count)]
        )
        step *= 2

    return (
        acts.reshape(1, 2, 1, rows, width),
        grads_in.reshape(1, 2, 1, rows, width),
        gain_sums[:1],
        final_query[None].astype(F32),
        final_keyval[None],
        final_out.T[None].astype(F32),
        gain_sums[1:],
        final_gate[None, :, :units].astype(F32),
        final_up[None, :, :units].astype(F32),
        final_down.astype(F32).T[None],
    )


def solution(mesh):
    tokens = P(None, ROW, None, "col")
    gain = P("section", "col")
    rows_cols = P("section", ROW, "col")
    cols_rows = P("section", "col", ROW)
    layers = P("section", None, ROW, None, "col")
    return jax.shard_map(
        step,
        mesh=mesh,
        in_specs=(
            tokens,
            tokens,
            gain,
            rows_cols,
            rows_cols,
            cols_rows,
            gain,
            rows_cols,
            rows_cols,
            cols_rows,
        ),
        out_specs=(
            layers,
            layers,
            gain,
            rows_cols,
            rows_cols,
            cols_rows,
            gain,
            rows_cols,
            rows_cols,
            cols_rows,
        ),
        check_vma=False,
    )
```

time: 1310 us -> 1240 us (0.947)
  matrix products: 231 us -> 163 us
  waiting for transfers between devices: 674 us -> 737 us
  local copies, waits for them, and re-layouts: 103 us -> 57.7 us
  blocking collectives: 41.6 us -> 0 us
  Pallas kernels: 0 us -> 33.4 us
  other arithmetic: 95.3 us -> 68.9 us
  starting transfers between devices: 133 us -> 154 us
    ppermute x18 -> x26, waiting for transfers between devices: 35 us -> 135 us  [the longest x12 134 us: along_row(): return lax.ppermute(block, ROW, route)]
    dot_general x12 -> x0, matrix products: 55.9 us -> none  [the longest x2 22 us: layer_backward(): jnp.einsum('qhd,kd->hqk', grad_attended, values, preferred_element_type=F32)]
    reduce_scatter x6 -> x8, waiting for transfers between devices: 231 us -> 181 us  [scatter_rows(): return lax.psum_scatter(total, ROW, scatter_dimension=0, tiled=True)]
    psum x1 -> x0, blocking collectives: 41.6 us -> none  [local(): lax.psum(jnp.stack([gain_grads_0, gain_grads_1]), ('section', 'row', 'col'))]
    pallas_call x0 -> x6, Pallas kernels: none -> 33.4 us  [the longest x2 15.2 us: attend_back(): pl.pallas_call(functools.partial(attend_back_kernel, scale), grid=(heads,...]
    ppermute x86 -> x73, waiting for transfers between devices: 186 us -> 207 us  [over_col(): return lax.ppermute(block, 'col', [(i, i ^ step) for i in range(count)])]
    ppermute x18 -> x26, starting transfers between devices: 34.8 us -> 52 us  [the longest x12 23.5 us: along_row(): return lax.ppermute(block, ROW, route)]
    unnamed x318 -> x224, local copies, waits for them, and re-layouts: 44.7 us -> 28.5 us
  transfers between devices with their start and end apart: 128 -> 126, of which waited for: 81 -> 71; matrix products, arithmetic and copies ran while one was open for 26% -> 20% of each run, Pallas kernels for 0% -> 3%
where the time goes in v2:
time: 1240 us; the launch traced here: 1230 us
  waiting for transfers between devices  737 us (59%)
  matrix products  163 us (13%)
  starting transfers between devices  154 us (12%)
  other arithmetic  68.9 us (6%)
  local copies, waits for them, and re-layouts  57.7 us (5%)
  Pallas kernels  33.4 us (3%)
  between operations  16.3 us (1%)
    ppermute x73, waiting for transfers between devices, over_col(): return lax.ppermute(block, 'col', [(i, i ^ step) for i in range(count)])  207 us
    all_gather x4, waiting for transfers between devices, gather_layers(): both = lax.all_gather(part, ('section', ROW), axis=0, tiled=True)  193 us
    reduce_scatter x8, waiting for transfers between devices, scatter_rows(): return lax.psum_scatter(total, ROW, scatter_dimension=0, tiled=True)  181 us
    dot_general x38, matrix products, dot(): lax.dot_general(left, right, (((left_dim,), (right_dim,)), ((), ())), pre...  163 us
    ppermute x12, waiting for transfers between devices, along_row(): return lax.ppermute(block, ROW, route)  134 us
    ppermute x73, starting transfers between devices, over_col(): return lax.ppermute(block, 'col', [(i, i ^ step) for i in range(count)])  88.1 us
    unnamed x224, local copies, waits for them, and re-layouts  28.5 us
  transfers between devices with their start and end apart: 126, of which 71 were waited for; matrix products, arithmetic and copies ran while one was open for 20% of the time, Pallas kernels for 3%

profile of v2, /device:TPU:0, one launch (start us, length us, event | category | flops | bytes accessed | tf_op | source)
XLA Modules:
  0.0 1230.5 jit_solution(11450846349998799705)
XLA Ops:
  85.1 11.2 collective-permute-done.11.refs_2_
  96.4 9.8 collective-permute-done.12.refs_3_
  117.6 8.6 collective-permute-done.13
  130.7 11.0 all-gather.17.cloned.1.call-start
  158.7 41.1 %all-gather.9.cloned.1.call-done = bf16[3072,2304]{1,0:T(8,128)(2,1)} async-done(((bf16[384,2304]{1,0:T(8,128)(2,1)}), bf16[3072,2304]{1,0:T(8,128)(2,1)}) %all-gather.9.cloned.1.call-update) | async-done | bytes 14155792 | tf_op jit(solution)/shard_map/all_gather | solution.py:418
  214.9 67.1 %all-gather.11.cloned.1.call-done = bf16[3072,1152]{1,0:T(8,128)(2,1)} async-done(((bf16[384,1152]{1,0:T(8,128)(2,1)}), bf16[3072,1152]{1,0:T(8,128)(2,1)}) %all-gather.11.cloned.1.call-update) | async-done | bytes 7077904 | tf_op jit(solution)/shard_map/all_gather | solution.py:418
  292.9 9.4 collective-permute-done.22
  302.4 7.7 collective-permute-done.23
  313.4 8.1 collective-permute-done.25
  349.4 11.2 collective-permute-done.30.refs_2_
  360.7 10.4 collective-permute-done.31.refs_3_
  391.8 8.0 collective-permute-done.36
  427.3 35.3 %all-gather.15.cloned.1.call-done = bf16[3072,2304]{1,0:T(8,128)(2,1)} async-done(((bf16[384,2304]{1,0:T(8,128)(2,1)}), bf16[3072,2304]{1,0:T(8,128)(2,1)}) %all-gather.15.cloned.1.call-update) | async-done | bytes 14155792 | tf_op jit(solution)/shard_map/all_gather | solution.py:418
  470.2 8.2 multiply_convert_fusion
  495.1 49.4 %all-gather.17.cloned.1.call-done = bf16[3072,1152]{1,0:T(8,128)(2,1)} async-done(((bf16[384,1152]{1,0:T(8,128)(2,1)}), bf16[3072,1152]{1,0:T(8,128)(2,1)}) %all-gather.17.cloned.1.call-update) | async-done | bytes 7077904 | tf_op jit(solution)/shard_map/all_gather | solution.py:418
  555.5 8.0 convolution_convert_fusion.1
  604.7 7.9 collective-permute-done.48
  613.4 8.8 add_convert_fusion.1
  637.6 11.4 collective-permute-done.63
  662.3 7.6 attend_back.2
  686.5 32.5 %collective-permute-done.56 = bf16[512,256]{1,0:T(8,128)(2,1)} collective-permute-done((bf16[512,256]{1,0:T(8,128)(2,1)}, bf16[512,256]{1,0:T(8,128)(2,1)}, u32[]{:S(2)}, u32[]{:S(2)}) %collective-permute-start.56) | collective-permute-done | bytes 262176 | tf_op jit(solution)/shard_map/ppermute | solution.py:53
  736.8 8.6 collective-permute-done.67
  755.7 8.9 collective-permute-done.70
  824.5 9.4 collective-permute-done.76
  834.0 8.0 collective-permute-done.77
  842.2 8.2 add_convert_fusion
  854.6 9.1 collective-permute-done.80
  875.0 7.6 attend_back.3
  896.8 33.3 %collective-permute-done.85 = bf16[512,256]{1,0:T(8,128)(2,1)S(1)} collective-permute-done((bf16[512,256]{1,0:T(8,128)(2,1)S(1)}, bf16[512,256]{1,0:T(8,128)(2,1)S(1)}, u32[]{:S(2)}, u32[]{:S(2)}) %collective-permute-start.85) | collective-permute-done | bytes 262176 | tf_op jit(solution)/shard_map/ppermute | solution.py:53
  989.6 37.3 %reduce-scatter.19.cloned.1.call-done = bf16[384,2304]{1,0:T(8,128)(2,1)} async-done(((bf16[1536,2304]{1,0:T(8,128)(2,1)}), bf16[384,2304]{1,0:T(8,128)(2,1)}) %reduce-scatter.19.cloned.1.call-update) | async-done | bytes 1769488 | tf_op jit(solution)/shard_map/reduce_scatter | solution.py:463
  1062.5 113.3 %reduce-scatter.17.cloned.1.call-done = bf16[384,2304]{1,0:T(8,128)(2,1)} async-done(((bf16[1536,2304]{1,0:T(8,128)(2,1)}), bf16[384,2304]{1,0:T(8,128)(2,1)}) %reduce-scatter.17.cloned.1.call-update) | async-done | bytes 1769488 | tf_op jit(solution)/shard_map/reduce_scatter | solution.py:463
  1178.1 30.3 %reduce-scatter.9.cloned.1.call-done = bf16[384,384]{1,0:T(8,128)(2,1)} async-done(((bf16[1536,384]{1,0:T(8,128)(2,1)}), bf16[384,384]{1,0:T(8,128)(2,1)}) %reduce-scatter.9.cloned.1.call-update) | async-done | bytes 294928 | tf_op jit(solution)/shard_map/reduce_scatter | solution.py:463
  (667 shorter events, 567.2 us)
Async XLA Ops:
  7.2 57.3 %all-gather.7.cloned.1.call-start = ((), (), s32[]{:S(2)}) async-start(), calls=%async_computation.8 | async-start | bytes 3538944 | tf_op jit(solution)/shard_map/all_gather | solution.py:422
  18.1 181.8 %all-gather.9.cloned.1.call-start = ((), (), s32[]{:S(2)}) async-start(), calls=%async_computation.9 | async-start | bytes 15925248 | tf_op jit(solution)/shard_map/all_gather | solution.py:418
  28.6 253.3 %all-gather.11.cloned.1.call-start = ((), (), s32[]{:S(2)}) async-start(), calls=%async_computation.10 | async-start | bytes 7962624 | tf_op jit(solution)/shard_map/all_gather | solution.py:418
  61.7 269.2 %all-gather.13.cloned.1.call-start = ((), (), s32[]{:S(2)}) async-start(), calls=%async_computation.11 | async-start | bytes 3538944 | tf_op jit(solution)/shard_map/all_gather | solution.py:422
  111.5 351.1 %all-gather.15.cloned.1.call-start = ((), (), s32[]{:S(2)}) async-start(), calls=%async_computation.12 | async-start | bytes 15925248 | tf_op jit(solution)/shard_map/all_gather | solution.py:418
  130.7 413.8 %all-gather.17.cloned.1.call-start = ((), (), s32[]{:S(2)}) async-start(), calls=%async_computation.13 | async-start | bytes 7962624 | tf_op jit(solution)/shard_map/all_gather | solution.py:418
  313.3 628.9 %reduce-scatter.23.cloned.1.call-start = ((), (), s32[]{:S(2)}) async-start(), calls=%async_computation.21 | async-start | bytes 4423680 | tf_op jit(solution)/shard_map/reduce_scatter | solution.py:463
  340.8 30.3 %collective-permute-start.31 = (bf16[512,256]{1,0:T(8,128)(2,1)}, bf16[512,256]{1,0:T(8,128)(2,1)S(1)}, u32[]{:S(2)}, u32[]{:S(2)}) collective-permute-start(bf16[512,256]{1,0:T(8,128)(2,1)} %get-tuple-element.54.refs_0_), channel_id=1, source_target_pairs={{0,12},{1,13},{2,14},{3,15},{16,28},{17,29},{18,30},{19,31}} | collective-permute-start | bytes 786440 | tf_op jit(solution)/shard_map/ppermute | solution.py:53
  563.4 49.9 %collective-permute-start.50 = (bf16[1536,2304]{1,0:T(8,128)(2,1)}, bf16[1536,2304]{1,0:T(8,128)(2,1)}, u32[]{:S(2)}, u32[]{:S(2)}) collective-permute-start(bf16[1536,2304]{1,0:T(8,128)(2,1)} %convolution_convert_fusion.1), channel_id=1, source_target_pairs={{0,16},{16,0},{1,17},{17,1},{2,18},{18,2},{3,19},{19,3},{4,20},{20... | collective-permute-start | bytes 21233672 | tf_op jit(solution)/shard_map/ppermute | solution.py:47
  674.6 47.4 %collective-permute-start.58 = (bf16[1536,384]{1,0:T(8,128)(2,1)}, bf16[1536,384]{1,0:T(8,128)(2,1)S(1)}, u32[]{:S(2)}, u32[]{:S(2)}) collective-permute-start(bf16[1536,384]{1,0:T(8,128)(2,1)} %get-tuple-element.248), channel_id=1, source_target_pairs={{0,16},{16,0},{1,17},{17,1},{2,18},{18,2},{3,19},{19,3},{4,20},{20... | collective-permute-start | bytes 3538952 | tf_op jit(solution)/shard_map/ppermute | solution.py:47
  676.1 42.9 %collective-permute-start.56 = (bf16[512,256]{1,0:T(8,128)(2,1)}, bf16[512,256]{1,0:T(8,128)(2,1)}, u32[]{:S(2)}, u32[]{:S(2)}) collective-permute-start(bf16[512,256]{1,0:T(8,128)(2,1)} %get-tuple-element.64), channel_id=1, source_target_pairs={{8,0},{12,4},{9,1},{13,5},{10,2},{14,6},{11,3},{15,7},{24,16},{28,... | collective-permute-start | bytes 786440 | tf_op jit(solution)/shard_map/ppermute | solution.py:53
  677.4 41.6 %collective-permute-start.57 = (bf16[512,256]{1,0:T(8,128)(2,1)}, bf16[512,256]{1,0:T(8,128)(2,1)}, u32[]{:S(2)}, u32[]{:S(2)}) collective-permute-start(bf16[512,256]{1,0:T(8,128)(2,1)} %get-tuple-element.65), channel_id=1, source_target_pairs={{12,0},{13,1},{14,2},{15,3},{28,16},{29,17},{30,18},{31,19}} | collective-permute-start | bytes 786440 | tf_op jit(solution)/shard_map/ppermute | solution.py:53
  678.9 42.1 %collective-permute-start.66 = (bf16[512,384]{1,0:T(8,128)(2,1)S(1)}, bf16[512,384]{1,0:T(8,128)(2,1)S(1)}, u32[]{:S(2)}, u32[]{:S(2)}) collective-permute-start(bf16[512,384]{1,0:T(8,128)(2,1)S(1)} %get-tuple-element.196), channel_id=1, source_target_pairs={{16,0},{17,1},{18,2},{19,3},{20,4},{21,5},{22,6},{23,7},{24,8},{25... | collective-permute-start | bytes 1179656 | tf_op jit(solution)/shard_map/ppermute | solution.py:528
  681.4 266.2 %reduce-scatter.15.cloned.1.call-start = ((), (), s32[]{:S(2)}) async-start(), calls=%async_computation.17 | async-start | bytes 491520 | tf_op jit(solution)/shard_map/reduce_scatter | solution.py:463
  775.1 175.0 %reduce-scatter.21.cloned.1.call-start = ((), (), s32[]{:S(2)}) async-start(), calls=%async_computation.20 | async-start | bytes 4423680 | tf_op jit(solution)/shard_map/reduce_scatter | solution.py:463
  788.4 199.1 %reduce-scatter.11.cloned.1.call-start = ((), (), s32[]{:S(2)}) async-start(), calls=%async_computation.15 | async-start | bytes 1474560 | tf_op jit(solution)/shard_map/reduce_scatter | solution.py:463
  789.0 237.9 %reduce-scatter.19.cloned.1.call-start = ((), (), s32[]{:S(2)}) async-start(), calls=%async_computation.19 | async-start | bytes 8847360 | tf_op jit(solution)/shard_map/reduce_scatter | solution.py:463
  806.5 35.7 %collective-permute-start.79 = (bf16[1536,2304]{1,0:T(8,128)(2,1)}, bf16[1536,2304]{1,0:T(8,128)(2,1)}, u32[]{:S(2)}, u32[]{:S(2)}) collective-permute-start(bf16[1536,2304]{1,0:T(8,128)(2,1)} %convolution_convert_fusion), channel_id=1, source_target_pairs={{0,16},{16,0},{1,17},{17,1},{2,18},{18,2},{3,19},{19,3},{4,20},{20... | collective-permute-start | bytes 21233672 | tf_op jit(solution)/shard_map/ppermute | solution.py:47
  806.7 249.2 %reduce-scatter.13.cloned.1.call-start = ((), (), s32[]{:S(2)}) async-start(), calls=%async_computation.16 | async-start | bytes 491520 | tf_op jit(solution)/shard_map/reduce_scatter | solution.py:463
  885.8 45.2 %collective-permute-start.87 = (bf16[1536,384]{1,0:T(8,128)(2,1)S(1)}, bf16[1536,384]{1,0:T(8,128)(2,1)S(1)}, u32[]{:S(2)}, u32[]{:S(2)}) collective-permute-start(bf16[1536,384]{1,0:T(8,128)(2,1)S(1)} %get-tuple-element.250), channel_id=1, source_target_pairs={{0,16},{16,0},{1,17},{17,1},{2,18},{18,2},{3,19},{19,3},{4,20},{20... | collective-permute-start | bytes 3538952 | tf_op jit(solution)/shard_map/ppermute | solution.py:47
  887.2 42.9 %collective-permute-start.85 = (bf16[512,256]{1,0:T(8,128)(2,1)S(1)}, bf16[512,256]{1,0:T(8,128)(2,1)S(1)}, u32[]{:S(2)}, u32[]{:S(2)}) collective-permute-start(bf16[512,256]{1,0:T(8,128)(2,1)S(1)} %copy-done.85), channel_id=1, source_target_pairs={{8,0},{12,4},{9,1},{13,5},{10,2},{14,6},{11,3},{15,7},{24,16},{28,... | collective-permute-start | bytes 786440 | tf_op jit(solution)/shard_map/ppermute | solution.py:53
  888.5 41.6 %collective-permute-start.86 = (bf16[512,256]{1,0:T(8,128)(2,1)S(1)}, bf16[512,256]{1,0:T(8,128)(2,1)S(1)}, u32[]{:S(2)}, u32[]{:S(2)}) collective-permute-start(bf16[512,256]{1,0:T(8,128)(2,1)S(1)} %copy-done.84), channel_id=1, source_target_pairs={{12,0},{13,1},{14,2},{15,3},{28,16},{29,17},{30,18},{31,19}} | collective-permute-start | bytes 786440 | tf_op jit(solution)/shard_map/ppermute | solution.py:53
  940.2 235.6 %reduce-scatter.17.cloned.1.call-start = ((), (), s32[]{:S(2)}) async-start(), calls=%async_computation.18 | async-start | bytes 8847360 | tf_op jit(solution)/shard_map/reduce_scatter | solution.py:463
  941.0 267.4 %reduce-scatter.9.cloned.1.call-start = ((), (), s32[]{:S(2)}) async-start(), calls=%async_computation.14 | async-start | bytes 1474560 | tf_op jit(solution)/shard_map/reduce_scatter | solution.py:463
  947.6 110.3 %collective-permute-start.104 = (bf16[384,128]{1,0:T(8,128)(2,1)}, bf16[384,128]{1,0:T(8,128)(2,1)}, u32[]{:S(2)}, u32[]{:S(2)}) collective-permute-start(bf16[384,128]{1,0:T(8,128)(2,1)} %reduce-scatter.15.cloned.1.call-done), channel_id=1, source_target_pairs={{0,16},{1,17},{2,18},{3,19},{4,20},{5,21},{6,22},{7,23},{8,24},{9,... | collective-permute-start | bytes 294920 | tf_op jit(solution)/shard_map/ppermute | solution.py:536
  950.1 81.1 %collective-permute-start.111 = (bf16[384,1152]{1,0:T(8,128)(2,1)}, bf16[384,1152]{1,0:T(8,128)(2,1)}, u32[]{:S(2)}, u32[]{:S(2)}) collective-permute-start(bf16[384,1152]{1,0:T(8,128)(2,1)} %reduce-scatter.21.cloned.1.call-done), channel_id=1, source_target_pairs={{16,0},{17,1},{18,2},{19,3},{20,4},{21,5},{22,6},{23,7},{24,8},{25... | collective-permute-start | bytes 2654216 | tf_op jit(solution)/shard_map/ppermute | solution.py:536
  982.9 44.0 %collective-permute-start.98 = (f32[2,384]{1,0:T(2,128)S(1)}, f32[2,384]{1,0:T(2,128)S(1)}, u32[]{:S(2)}, u32[]{:S(2)}) collective-permute-start(f32[2,384]{1,0:T(2,128)S(1)} %get-tuple-element.233), channel_id=1, source_target_pairs={{0,2},{1,3},{2,0},{3,1},{4,6},{5,7},{6,4},{7,5},{8,10},{9,11},{10,... | collective-permute-start | bytes 9224 | tf_op jit(solution)/shard_map/ppermute | solution.py:43
  984.2 45.5 %collective-permute-start.99 = (f32[2,384]{1,0:T(2,128)S(1)}, f32[2,384]{1,0:T(2,128)S(1)}, u32[]{:S(2)}, u32[]{:S(2)}) collective-permute-start(f32[2,384]{1,0:T(2,128)S(1)} %get-tuple-element.234), channel_id=1, source_target_pairs={{0,3},{1,2},{2,1},{3,0},{4,7},{5,6},{6,5},{7,4},{8,11},{9,10},{10,... | collective-permute-start | bytes 9224 | tf_op jit(solution)/shard_map/ppermute | solution.py:43
  987.5 223.0 %collective-permute-start.102 = (bf16[384,384]{1,0:T(8,128)(2,1)}, bf16[384,384]{1,0:T(8,128)(2,1)}, u32[]{:S(2)}, u32[]{:S(2)}) collective-permute-start(bf16[384,384]{1,0:T(8,128)(2,1)} %reduce-scatter.11.cloned.1.call-done), channel_id=1, source_target_pairs={{0,16},{1,17},{2,18},{3,19},{4,20},{5,21},{6,22},{7,23},{8,24},{9,... | collective-permute-start | bytes 884744 | tf_op jit(solution)/shard_map/ppermute | solution.py:536
  1026.9 186.6 %collective-permute-start.108 = (bf16[384,2304]{1,0:T(8,128)(2,1)}, bf16[384,2304]{1,0:T(8,128)(2,1)}, u32[]{:S(2)}, u32[]{:S(2)}) collective-permute-start(bf16[384,2304]{1,0:T(8,128)(2,1)} %reduce-scatter.19.cloned.1.call-done), channel_id=1, source_target_pairs={{0,16},{1,17},{2,18},{3,19},{4,20},{5,21},{6,22},{7,23},{8,24},{9,... | collective-permute-start | bytes 5308424 | tf_op jit(solution)/shard_map/ppermute | solution.py:536
  1060.4 149.3 %collective-permute-start.106 = (bf16[384,128]{1,0:T(8,128)(2,1)S(1)}, bf16[384,128]{1,0:T(8,128)(2,1)S(1)}, u32[]{:S(2)}, u32[]{:S(2)}) collective-permute-start(bf16[384,128]{1,0:T(8,128)(2,1)S(1)} %broadcast_select_fusion.17), channel_id=1, source_target_pairs={{0,1},{1,0},{2,3},{3,2},{4,5},{5,4},{6,7},{7,6},{8,9},{9,8},{10,11... | collective-permute-start | bytes 294920 | tf_op jit(solution)/shard_map/ppermute | solution.py:43
  1175.8 42.8 %collective-permute-start.109 = (bf16[384,2304]{1,0:T(8,128)(2,1)}, bf16[384,2304]{1,0:T(8,128)(2,1)}, u32[]{:S(2)}, u32[]{:S(2)}) collective-permute-start(bf16[384,2304]{1,0:T(8,128)(2,1)} %reduce-scatter.17.cloned.1.call-done), channel_id=1, source_target_pairs={{16,0},{17,1},{18,2},{19,3},{20,4},{21,5},{22,6},{23,7},{24,8},{25... | collective-permute-start | bytes 5308424 | tf_op jit(solution)/shard_map/ppermute | solution.py:536
  (193 other events, 3022.2 us)
Sparse Core Ops, SparseCore 0:
  18.2 39.7 all-gather.6
  60.2 139.6 all-gather.8
  201.5 80.4 all-gather.10
  284.0 36.7 all-gather.12
  322.9 139.6 all-gather.14
  464.1 80.3 all-gather.16
  681.5 84.6 reduce-scatter.22
  775.2 18.4 reduce-scatter.14
  796.0 64.7 reduce-scatter.20
  862.9 29.4 reduce-scatter.10
  894.8 132.0 reduce-scatter.18
  1029.0 22.5 reduce-scatter.12
  1053.9 121.8 reduce-scatter.16
  1178.6 29.8 reduce-scatter.8

commit v3 on v2

--- a/solution.py
+++ b/solution.py
@@ -85,39 +85,38 @@
     return inverse * (grad_scaled - scaled * mean_term), grad_gain
 
 
-def qkv_kernel(heads, x_ref, w_ref, cos_ref, sign_ref, q_ref, kv_ref):
+def qkv_kernel(heads, x_ref, w_ref, cos_ref, sign_ref, own_cos_ref, own_sign_ref, q_ref, own_ref):
     raw = jnp.dot(x_ref[...], w_ref[...], preferred_element_type=F32)
-    cosine, signed = cos_ref[...], sign_ref[...]
     for h in range(heads + 1):
         z = raw[:, h * HD : (h + 1) * HD]
-        z = (z * cosine + pltpu.roll(z, HD // 2, 1) * signed).astype(BF)
         if h < heads:
-            q_ref[:, h * HD : (h + 1) * HD] = z
+            z = z * cos_ref[...] + pltpu.roll(z, HD // 2, 1) * sign_ref[...]
+            q_ref[:, h * HD : (h + 1) * HD] = z.astype(BF)
         else:
-            kv_ref[:, :HD] = z
-    kv_ref[:, HD:] = raw[:, (heads + 1) * HD :].astype(BF)
-
-
-def project_turn(normed, weight, cosine, signed, heads):
+            z = z * own_cos_ref[...] + pltpu.roll(z, HD // 2, 1) * own_sign_ref[...]
+            own_ref[...] = z.astype(BF)
+
+
+def project_turn(normed, weight, tables, heads):
     rows, depth = normed.shape
     step = rows // 2
-    cols = (heads + 2) * HD
+    cols = (heads + 1) * HD
+    table = pl.BlockSpec((step, HD), lambda i: (i, 0))
     return pl.pallas_call(
         functools.partial(qkv_kernel, heads),
         grid=(2,),
         in_specs=[
             pl.BlockSpec((step, depth), lambda i: (i, 0)),
             pl.BlockSpec((depth, cols), lambda i: (0, 0)),
-            pl.BlockSpec((step, HD), lambda i: (i, 0)),
-            pl.BlockSpec((step, HD), lambda i: (i, 0)),
+            *[table] * 4,
         ],
         out_specs=[
             pl.BlockSpec((step, heads * HD), lambda i: (i, 0)),
-            pl.BlockSpec((step, 2 * HD), lambda i: (i, 0)),
+            pl.BlockSpec((step, HD), lambda i: (i, 0)),
         ],
         out_shape=[
             jax.ShapeDtypeStruct((rows, heads * HD), BF),
-            jax.ShapeDtypeStruct((rows, 2 * HD), BF),
+            jax.ShapeDtypeStruct((rows, HD), BF),
         ],
         cost_estimate=pl.CostEstimate(
             flops=2 * rows * depth * cols,
@@ -125,17 +124,43 @@
             transcendentals=0,
         ),
         name="project_turn",
-    )(normed, weight, cosine, signed)
-
-
-def attend_kernel(scale, peer_ref, col_ref, row_ref, q_ref, *refs):
-    pieces, (o_ref, lse_ref, e_ref, total_ref, acc_ref) = refs[:SPAN], refs[SPAN:]
-    peer = peer_ref[0]
+    )(normed, weight, *tables)
+
+
+def swapped(k, rows):
+    quarter = rows // 4
+    return [
+        (pl.ds(k * rows + i * quarter, quarter), pl.ds((i ^ 1) * quarter, quarter)) for i in range(4)
+    ]
+
+
+def attend_kernel(scale, flag_ref, col_ref, row_ref, q_ref, *refs):
+    mine, theirs = refs[:SPAN], refs[SPAN : 2 * SPAN]
+    o_ref, lse_ref, k_ref, v_ref, e_ref, total_ref, acc_ref = refs[2 * SPAN :]
+    rows = q_ref.shape[0]
+    peer, is_key = flag_ref[0], flag_ref[1]
     q = q_ref[...]
+
+    def place(own_ref, other_ref):
+        for k in range(SPAN):
+            own_ref[k * rows : (k + 1) * rows] = mine[k][...]
+            for here, there in swapped(k, rows):
+                other_ref[here] = theirs[k][there]
+
+    @pl.when((pl.program_id(0) == 0) & (is_key == 1))
+    def _():
+        place(k_ref, v_ref)
+
+    @pl.when((pl.program_id(0) == 0) & (is_key == 0))
+    def _():
+        place(v_ref, k_ref)
+
+    def piece(ref, k):
+        return ref[k * rows : (k + 1) * rows]
 
     def exps(k):
         s = lax.dot_general(
-            pieces[k][:, :HD], q, (((1,), (1,)), ((), ())), preferred_element_type=F32
+            piece(k_ref, k), q, (((1,), (1,)), ((), ())), preferred_element_type=F32
         )
         return jnp.exp(s * scale)
 
@@ -158,7 +183,7 @@
     def term(k):
         p = ((e_ref[k] * shrink) * inverse).astype(BF)
         return lax.dot_general(
-            pieces[k][:, HD:], p, (((0,), (0,)), ((), ())), preferred_element_type=F32
+            piece(v_ref, k), p, (((0,), (0,)), ((), ())), preferred_element_type=F32
         )
 
     acc_ref[...] = term(0)
@@ -171,9 +196,11 @@
     o_ref[...] = acc_ref[...].T.astype(BF)
 
 
-def attend(queries, pieces, peer, order, heads, scale):
+def attend(queries, mine, first, later, flags, order, heads, scale):
     rows = queries.shape[0]
     full = SPAN * rows
+    piece = pl.BlockSpec((rows, HD), lambda h: (0, 0))
+    whole = pl.BlockSpec((full, HD), lambda h: (0, 0))
     return pl.pallas_call(
         functools.partial(attend_kernel, scale),
         grid=(heads,),
@@ -182,15 +209,21 @@
             pl.BlockSpec((rows, 1), lambda h: (0, 0)),
             pl.BlockSpec((1, rows), lambda h: (0, 0)),
             pl.BlockSpec((rows, HD), lambda h: (0, h)),
-            *[pl.BlockSpec((rows, 2 * HD), lambda h: (0, 0))] * SPAN,
+            *[piece] * SPAN,
+            piece,
+            *[pl.BlockSpec((rows, HD), lambda h, k=k: (k, 0)) for k in range(SPAN - 1)],
         ],
         out_specs=[
             pl.BlockSpec((rows, HD), lambda h: (0, h)),
             pl.BlockSpec((1, 1, rows), lambda h: (h, 0, 0)),
+            whole,
+            whole,
         ],
         out_shape=[
             jax.ShapeDtypeStruct((rows, heads * HD), BF),
             jax.ShapeDtypeStruct((heads, 1, rows), F32),
+            jax.ShapeDtypeStruct((full, HD), BF),
+            jax.ShapeDtypeStruct((full, HD), BF),
         ],
         scratch_shapes=[
             pltpu.VMEM((SPAN, rows, rows), F32),
@@ -199,30 +232,34 @@
         ],
         cost_estimate=pl.CostEstimate(
             flops=4 * heads * rows * full * HD,
-            bytes_accessed=4 * rows * HD * (heads + SPAN),
+            bytes_accessed=4 * rows * HD * (heads + 2 * SPAN),
             transcendentals=heads * rows * full,
         ),
         name="attend",
-    )(peer, order[:, None], order[None, :], queries, *pieces)
-
-
-def attend_back_kernel(scale, peer_ref, col_ref, row_ref, cos_ref, sign_ref, q_ref, do_ref, lse_ref, *refs):
-    pieces = refs[:SPAN]
-    dq_ref, outs = refs[SPAN], refs[SPAN + 1 : 2 * SPAN + 1]
-    p_ref, dp_ref, sum_ref, turn_ref, acc_ref = refs[2 * SPAN + 1 :]
+    )(flags, order[:, None], order[None, :], queries, *mine, first, *[later] * (SPAN - 1))
+
+
+def attend_back_kernel(
+    scale, flag_ref, col_ref, row_ref, cos_ref, sign_ref, q_ref, do_ref, lse_ref, k_ref, v_ref,
+    dq_ref, keep_ref, send_ref, p_ref, dp_ref, sum_ref, turn_ref, dk_ref, dv_ref,
+):
     h = pl.program_id(0)
     last = pl.num_programs(0) - 1
-    peer = peer_ref[0]
+    rows = q_ref.shape[0]
+    peer, is_key = flag_ref[0], flag_ref[1]
     q, do = q_ref[...], do_ref[...]
     lse = lse_ref[0]
 
+    def piece(ref, k):
+        return ref[k * rows : (k + 1) * rows]
+
     def first(k):
         nt = (((1,), (1,)), ((), ()))
-        s = lax.dot_general(pieces[k][:, :HD], q, nt, preferred_element_type=F32)
+        s = lax.dot_general(piece(k_ref, k), q, nt, preferred_element_type=F32)
         p = jnp.exp(s * scale - lse)
         if k == 0:
             p = jnp.where(col_ref[...] <= row_ref[...], p, 0.0)
-        dp = lax.dot_general(pieces[k][:, HD:], do, nt, preferred_element_type=F32)
+        dp = lax.dot_general(piece(v_ref, k), do, nt, preferred_element_type=F32)
         p_ref[k] = p
         dp_ref[k] = dp
         return jnp.sum(p * dp, axis=0, keepdims=True)
@@ -235,16 +272,16 @@
 
         @pl.when(h == 0)
         def _():
-            acc_ref[k, :, :HD] = dk
-            acc_ref[k, :, HD:] = dv
+            dk_ref[k * rows : (k + 1) * rows] = dk
+            dv_ref[k * rows : (k + 1) * rows] = dv
 
         @pl.when(h > 0)
         def _():
-            acc_ref[k, :, :HD] += dk
-            acc_ref[k, :, HD:] += dv
+            dk_ref[k * rows : (k + 1) * rows] += dk
+            dv_ref[k * rows : (k + 1) * rows] += dv
 
         return lax.dot_general(
-            pieces[k][:, :HD], ds, (((0,), (0,)), ((), ())), preferred_element_type=F32
+            piece(k_ref, k), ds, (((0,), (0,)), ((), ())), preferred_element_type=F32
         )
 
     sum_ref[...] = first(0)
@@ -261,28 +298,36 @@
         def _():
             turn_ref[...] += second(k)
 
+        @pl.when((peer < k) & (h == 0))
+        def _():
+            dk_ref[k * rows : (k + 1) * rows] = jnp.zeros((rows, HD), F32)
+            dv_ref[k * rows : (k + 1) * rows] = jnp.zeros((rows, HD), F32)
+
     dq = turn_ref[...].T * scale
     dq = dq * cos_ref[...] - pltpu.roll(dq, HD // 2, 1) * sign_ref[...]
     dq_ref[...] = dq.astype(BF)
 
-    @pl.when(h == last)
+    @pl.when((h == last) & (is_key == 1))
     def _():
+        keep_ref[...] = dk_ref[...] * scale
         for k in range(SPAN):
-
-            @pl.when(peer >= k)
-            def _():
-                outs[k][:, :HD] = (acc_ref[k, :, :HD] * scale).astype(outs[k].dtype)
-                outs[k][:, HD:] = acc_ref[k, :, HD:].astype(outs[k].dtype)
-
-            @pl.when(peer < k)
-            def _():
-                outs[k][...] = jnp.zeros(outs[k].shape, outs[k].dtype)
-
-
-def attend_back(queries, grads, lse, pieces, peer, order, cosine, signed, heads, scale):
+            for here, there in swapped(k, rows):
+                to = pl.ds(k * rows + there.start, there.size)
+                send_ref[to] = dv_ref[here].astype(BF)
+
+    @pl.when((h == last) & (is_key == 0))
+    def _():
+        keep_ref[...] = dv_ref[...]
+        for k in range(SPAN):
+            for here, there in swapped(k, rows):
+                to = pl.ds(k * rows + there.start, there.size)
+                send_ref[to] = (dk_ref[here] * scale).astype(BF)
+
+
+def attend_back(queries, grads, lse, keys, values, flags, order, cosine, signed, heads, scale):
     rows = queries.shape[0]
     full = SPAN * rows
-    whole = pl.BlockSpec((rows, 2 * HD), lambda h: (0, 0))
+    whole = pl.BlockSpec((full, HD), lambda h: (0, 0))
     table = pl.BlockSpec((rows, HD), lambda h: (0, 0))
     one_head = pl.BlockSpec((rows, HD), lambda h: (0, h))
     return pl.pallas_call(
@@ -297,20 +342,22 @@
             one_head,
             one_head,
             pl.BlockSpec((1, 1, rows), lambda h: (h, 0, 0)),
-            *[whole] * SPAN,
-        ],
-        out_specs=[one_head, *[whole] * SPAN],
+            whole,
+            whole,
+        ],
+        out_specs=[one_head, whole, whole],
         out_shape=[
             jax.ShapeDtypeStruct((rows, heads * HD), BF),
-            jax.ShapeDtypeStruct((rows, 2 * HD), F32),
-            *[jax.ShapeDtypeStruct((rows, 2 * HD), BF)] * (SPAN - 1),
+            jax.ShapeDtypeStruct((full, HD), F32),
+            jax.ShapeDtypeStruct((full, HD), BF),
         ],
         scratch_shapes=[
             pltpu.VMEM((SPAN, rows, rows), F32),
             pltpu.VMEM((SPAN, rows, rows), F32),
             pltpu.VMEM((1, rows), F32),
             pltpu.VMEM((HD, rows), F32),
-            pltpu.VMEM((SPAN, rows, 2 * HD), F32),
+            pltpu.VMEM((full, HD), F32),
+            pltpu.VMEM((full, HD), F32),
         ],
         cost_estimate=pl.CostEstimate(
             flops=10 * heads * rows * full * HD,
@@ -318,7 +365,7 @@
             transcendentals=heads * rows * full,
         ),
         name="attend_back",
-    )(peer, order[:, None], order[None, :], cosine, signed, queries, grads, lse, *pieces)
+    )(flags, order[:, None], order[None, :], cosine, signed, queries, grads, lse, keys, values)
 
 
 def step(layer_input, g_out, attn_gain, w_query, w_keyval, w_out, ffn_gain, w_gate, w_up, w_down):
@@ -334,7 +381,7 @@
     full = width * cols
     heads = w_query.shape[2] // HD
     query_cols = w_query.shape[2]
-    qkv_cols = query_cols + 2 * HD
+    qkv_cols = query_cols + HD
     units = w_gate.shape[2]
     scale = 1.0 / math.sqrt(HD)
 
@@ -388,16 +435,7 @@
         gains = lax.dynamic_update_slice_in_dim(gains, part, (col ^ k) * width, 2)
 
     shard = w_query.shape[1]
-    keyval_other = over_col(w_keyval[0], 1)
-    attn_own = jnp.concatenate(
-        [
-            w_query[0],
-            by_key(w_keyval[0], keyval_other),
-            by_key(keyval_other, w_keyval[0]),
-            w_out[0].T,
-        ],
-        axis=1,
-    )
+    attn_own = jnp.concatenate([w_query[0], w_keyval[0], w_out[0].T], axis=1)
     half_rows = shard // 2
     wide = -(-units // 256) * 256
     half_units = wide // 2
@@ -415,7 +453,9 @@
     down_parts = both_layers(down_own[:, :half_units], down_own[:, half_units:])
 
     def gather_layers(part):
-        both = lax.all_gather(part, ("section", ROW), axis=0, tiled=True)
+        return lax.all_gather(part, ("section", ROW), axis=0, tiled=True)
+
+    def split_layers(both):
         return both[:full], both[full:]
 
     def gather_attn(part):
@@ -431,13 +471,20 @@
     def swap_halves(values):
         return jnp.concatenate([values[:, HD // 2 :], values[:, : HD // 2]], axis=1)
 
-    peers = jnp.reshape(peer, (1,)).astype(jnp.int32)
+    flags = jnp.stack([peer, jnp.where(is_key, 1, 0)]).astype(jnp.int32)
+    own_cosine = by_key(cosine, jnp.ones_like(cosine))
+    own_signed = by_key(signed, jnp.zeros_like(signed))
+    tables = (cosine, signed, own_cosine, own_signed)
 
     def attn_forward(normed, attn_w):
-        queries, key_value = project_turn(normed, attn_w, cosine, signed, heads)
-        pieces = [key_value] + [along_row(key_value, k) for k in range(1, SPAN)]
-        attended, lse = attend(queries, pieces, peers, order, heads, scale)
-        return attended, (normed, queries, pieces, lse, attended)
+        queries, own = project_turn(normed, attn_w, tables, heads)
+        first = over_col(own, 1)
+        mine = [own] + [along_row(own, k) for k in range(1, SPAN)]
+        later = over_col(jnp.concatenate(mine[1:], axis=0), 1)
+        attended, lse, keys, values = attend(
+            queries, mine, first, later, flags, order, heads, scale
+        )
+        return attended, (normed, queries, keys, values, lse, attended)
 
     def attn_out(resid, attended, attn_w):
         return resid + scatter_tokens(dot(attended, attn_w[:, qkv_cols:], 1, 1).astype(BF))
@@ -447,11 +494,13 @@
         return gather_tokens(normed_own), inverse_ffn
 
     def ffn_in(normed_ffn, gate_up_w):
+        gate_up_w = split_layers(gate_up_w)
         gate = dot(normed_ffn, gate_up_w[0], 1, 0)
         up = dot(normed_ffn, gate_up_w[1], 1, 0)
         return gate.astype(BF), up.astype(BF), (jax.nn.silu(gate) * up).astype(BF)
 
     def ffn_out(hidden, down_w):
+        down_w = split_layers(down_w)
         out = dot(hidden[:, :half_units], down_w[0], 1, 1)
         return scatter_tokens((out + dot(hidden[:, half_units:], down_w[1], 1, 1)).astype(BF))
 
@@ -462,10 +511,12 @@
     def scatter_rows(total):
         return lax.psum_scatter(total, ROW, scatter_dimension=0, tiled=True)
 
-    def ffn_backward(grad_own, grad_branch, kept, ffn_gain, gate_up_w, down_w):
-        middle, inverse_ffn, normed_ffn, gate, up, hidden = kept
-        down_total = swap_add(grad_branch, hidden[:, :half_units], hidden[:, half_units:])
-        grad_branch, down_total = after(grad_branch, down_total)
+    def down_grad(grad_branch, hidden):
+        return swap_add(grad_branch, hidden[:, :half_units], hidden[:, half_units:])
+
+    def ffn_backward(layer, grad_own, grad_branch, down_total, kept, ffn_gain, gate_up_w, down_w):
+        middle, inverse_ffn, normed_ffn, gate, up = kept
+        gate_up_w, down_w = split_layers(gate_up_w), split_layers(down_w)
         down_sum = scatter_rows(down_total)
         grad_hidden = jnp.concatenate(
             [dot(grad_branch, down_w[0], 1, 0), dot(grad_branch, down_w[1], 1, 0)], axis=1
@@ -474,51 +525,50 @@
         sigma = jax.nn.sigmoid(gate)
         dgate = (grad_hidden * up * sigma * (1.0 + gate * (1.0 - sigma))).astype(BF)
         dup = (grad_hidden * gate * sigma).astype(BF)
-        grad_normed_ffn = scatter_tokens(
-            (dot(dgate, gate_up_w[0], 1, 1) + dot(dup, gate_up_w[1], 1, 1)).astype(BF)
-        )
         gate_up_total = swap_add(normed_ffn, dgate, dup)
-        grad_normed_ffn, gate_up_total = after(grad_normed_ffn, gate_up_total)
+        if layer == 0:
+            dgate, dup, gate_up_total = after(dgate, dup, gate_up_total)
+        grad_normed_ffn = (dot(dgate, gate_up_w[0], 1, 1) + dot(dup, gate_up_w[1], 1, 1)).astype(BF)
+        grad_normed_ffn = scatter_tokens(grad_normed_ffn)
+        if layer == 1:
+            grad_normed_ffn, gate_up_total = after(grad_normed_ffn, gate_up_total)
         gate_up_sum = scatter_rows(gate_up_total)
         grad_middle, grad_gain_ffn = norm_backward(grad_normed_ffn, middle, inverse_ffn, ffn_gain)
-        return grad_own + grad_middle, gate_up_sum, down_sum, grad_gain_ffn
+        grad_middle = grad_own + grad_middle
+        return grad_middle, gate_up_sum, down_sum, grad_gain_ffn
 
     def attn_backward(grad_middle, resid, inverse_attn, kept, attn_gain, attn_w, *others):
-        normed, queries, pieces, lse, attended = kept
+        normed, queries, keys, values, lse, attended = kept
         w_qkv, w_o = attn_w[:, :qkv_cols], attn_w[:, qkv_cols:]
         grad_attn_out = gather_tokens(grad_middle.astype(BF))
         grad_attended = dot(grad_attn_out, w_o, 1, 0).astype(BF)
-        grad_query_raw, grad_mine, *grad_sent = attend_back(
-            queries, grad_attended, lse, pieces, peers, order, cosine, signed, heads, scale
+        grad_query_raw, grad_keep, grad_send = attend_back(
+            queries, grad_attended, lse, keys, values, flags, order, cosine, signed, heads, scale
         )
+        grad_keep = grad_keep + over_col(grad_send, 1).astype(F32)
+        pieces = jnp.split(grad_keep, SPAN, axis=0)
+        grad_mine = pieces[0]
         for k in range(1, SPAN):
-            grad_mine = grad_mine + along_row(grad_sent[k - 1], -k).astype(F32)
+            grad_mine = grad_mine + along_row(pieces[k].astype(BF), -k).astype(F32)
         grad_wout = dot(grad_attn_out, attended, 0, 0).astype(BF)
         grad_wquery = dot(normed, grad_query_raw, 0, 0).astype(BF)
         got = over_section(by_section(grad_wout, grad_wquery))
         early = by_section(grad_wquery, grad_wout).astype(F32) + got.astype(F32)
         grad_mine, early, *others = after(grad_mine, early.astype(BF), *others)
-        early = scatter_rows(early)
-        grad_key = grad_mine[:, :HD]
-        grad_keyval = jnp.concatenate(
-            [
-                (grad_key * cosine - swap_halves(grad_key) * signed).astype(BF),
-                grad_mine[:, HD:].astype(BF),
-            ],
-            axis=1,
-        )
-        grad_wkeyval = dot(normed, grad_keyval, 0, 0).astype(BF)
-        grad_wkey, grad_wvalue = grad_wkeyval[:, :HD], grad_wkeyval[:, HD:]
-        got = over_section(by_section(grad_wvalue, grad_wkey))
-        late = by_section(grad_wkey, grad_wvalue).astype(F32) + got.astype(F32)
-        late = late.astype(BF)
+        grad_keyval = grad_mine * own_cosine - swap_halves(grad_mine) * own_signed
+        grad_keyval = grad_keyval.astype(BF)
+        late = dot(normed, grad_keyval, 0, 0).astype(BF)
+        late = late.astype(F32) + over_section(late).astype(F32)
+        total = jnp.concatenate([early, late.astype(BF)], axis=1)
         grad_normed = (
             dot(grad_query_raw, w_qkv[:, :query_cols], 1, 1)
             + dot(grad_keyval, w_qkv[:, query_cols:], 1, 1)
         ).astype(BF)
-        grad_normed = scatter_tokens(grad_normed)
+        grad_normed, total = after(scatter_tokens(grad_normed), total)
+        attn_sum = scatter_rows(total)
         grad_resid, grad_gain_attn = norm_backward(grad_normed, resid, inverse_attn, attn_gain)
-        return grad_middle + grad_resid, early, late, grad_gain_attn, others
+        grad_resid = grad_middle + grad_resid
+        return grad_resid, attn_sum, grad_gain_attn, others
 
     def own_width(block):
         block = lax.dynamic_slice_in_dim(block, col * width, width, 1)
@@ -554,7 +604,8 @@
     _, down_part = after(hidden, down_parts[1])
     down_w.append(gather_layers(down_part))
     result = middle + ffn_out(hidden, down_w[0])
-    kept_ffn_0 = (middle, inverse_ffn, normed_ffn, gate, up, hidden)
+    kept_ffn_0 = (middle, inverse_ffn, normed_ffn, gate, up)
+    hidden_0 = hidden
     x_full = gather_tokens(result.astype(BF))
     act_0 = core_swap(0, own_width(x_full))
     normed, inverse = norm(x_full.astype(F32), gains[1, 0])
@@ -567,29 +618,29 @@
     top_branch = gather_width(top.astype(BF))
     top_own = tokens_from_width(top)
     gate, up, hidden = ffn_in(normed_ffn, gate_up_w[1])
+    down_w[1], down_total, top_own = after(down_w[1], down_grad(top_branch, hidden), top_own)
     result = middle + ffn_out(hidden, down_w[1])
-    kept_ffn_1 = (middle, inverse_ffn, normed_ffn, gate, up, hidden)
+    kept_ffn_1 = (middle, inverse_ffn, normed_ffn, gate, up)
     act_1 = core_swap(1, width_from_tokens(result.astype(BF)))
     acts = by_layer(act_0, act_1)
 
     grad_middle, gate_up_1, down_1, gain_ffn_1 = ffn_backward(
-        top_own, top_branch, kept_ffn_1, gains[1, 1], gate_up_w[1], down_w[1]
-    )
-    grad_1, early_1, late_1, gain_attn_1, (acts,) = attn_backward(
+        1, top_own, top_branch, down_total, kept_ffn_1, gains[1, 1], gate_up_w[1], down_w[1]
+    )
+    grad_1, attn_1, gain_attn_1, (acts,) = attn_backward(
         grad_middle, resid_1, inverse_1, kept_attn_1, gains[1, 0], attn_w[1], acts
     )
     grad_1 = grad_1.astype(BF)
-    branch, late_1 = after(gather_tokens(grad_1), late_1)
-    late_1 = scatter_rows(late_1)
+    branch = gather_tokens(grad_1)
     grads_1 = core_swap(1, own_width(branch))
+    branch, down_total = after(branch, down_grad(branch, hidden_0))
     grad_middle, gate_up_0, down_0, gain_ffn_0 = ffn_backward(
-        grad_1.astype(F32), branch, kept_ffn_0, gains[0, 1], gate_up_w[0], down_w[0]
-    )
-    grad_0, early_0, late_0, gain_attn_0, _ = attn_backward(
+        0, grad_1.astype(F32), branch, down_total, kept_ffn_0, gains[0, 1], gate_up_w[0], down_w[0]
+    )
+    grad_0, attn_0, gain_attn_0, _ = attn_backward(
         grad_middle, resid_0, inverse_0, kept_attn_0, gains[0, 0], attn_w[0]
     )
     grads_in = by_layer(core_swap(0, width_from_tokens(grad_0.astype(BF))), grads_1)
-    late_0 = scatter_rows(late_0)
 
     def own_layer(first, second):
         return jax.tree.map(by_section, tuple(first), tuple(second))
@@ -597,13 +648,13 @@
     def final(zero, one):
         return own_layer(to_core(0, zero), to_core(1, one))
 
-    final_query, final_out = final(early_0, early_1)
-    final_key, final_value = final(late_0, late_1)
-    final_keyval = by_key(final_key, final_value).astype(F32) + over_col(
-        by_key(final_value, final_key), 1
-    ).astype(F32)
-    final_gate, final_up = final(gate_up_0, gate_up_1)
-    final_down = jnp.concatenate(final(down_0, down_1), axis=1)[:, :units]
+    final_gate, final_up = [
+        part[None, :, :units].astype(F32) for part in final(gate_up_0, gate_up_1)
+    ]
+    final_down = jnp.concatenate(final(down_0, down_1), axis=1)[:, :units].astype(F32).T[None]
+    attn_0, final_gate, final_up, final_down = after(attn_0, final_gate, final_up, final_down)
+    final_query, final_out = final(attn_0[:, :query_cols], attn_1[:, :query_cols])
+    final_keyval = by_section(attn_0[:, query_cols:], attn_1[:, query_cols:]).astype(F32)
 
     gain_grads_0 = jnp.stack([gain_attn_0, gain_ffn_0])
     gain_grads_1 = jnp.stack([gain_attn_1, gain_ffn_1])
@@ -630,9 +681,9 @@
         final_keyval[None],
         final_out.T[None].astype(F32),
         gain_sums[1:],
-        final_gate[None, :, :units].astype(F32),
-        final_up[None, :, :units].astype(F32),
-        final_down.astype(F32).T[None],
+        final_gate,
+        final_up,
+        final_down,
     )
 
 

time: 1240 us -> 1170 us (0.944)
  waiting for transfers between devices: 737 us -> 682 us
    ppermute x12, waiting for transfers between devices: 134 us -> 76.2 us  [along_row(): return lax.ppermute(block, ROW, route)]
    ppermute x73 -> x77, waiting for transfers between devices: 207 us -> 235 us  [over_col(): return lax.ppermute(block, 'col', [(i, i ^ step) for i in range(count)])]
    all_gather x4, waiting for transfers between devices: 193 us -> 172 us  [gather_layers(): return lax.all_gather(part, ('section', ROW), axis=0, tiled=True)]
    ppermute x73 -> x77, starting transfers between devices: 88.1 us -> 96 us  [over_col(): return lax.ppermute(block, 'col', [(i, i ^ step) for i in range(count)])]
    reduce_scatter x8 -> x6, waiting for transfers between devices: 181 us -> 174 us  [scatter_rows(): return lax.psum_scatter(total, ROW, scatter_dimension=0, tiled=True)]
    unnamed x224 -> x208, local copies, waits for them, and re-layouts: 28.5 us -> 33.9 us
  transfers between devices with their start and end apart: 126 -> 126, of which waited for: 71 -> 75; matrix products, arithmetic and copies ran while one was open for 20% -> 20% of each run, Pallas kernels for 3% -> 3%
where the time goes in v3:
time: 1170 us; the launch traced here: 1160 us
  waiting for transfers between devices  682 us (58%)
  starting transfers between devices  160 us (14%)
  matrix products  152 us (13%)
  other arithmetic  59.1 us (5%)
  local copies, waits for them, and re-layouts  54.5 us (5%)
  Pallas kernels  34 us (3%)
  between operations  16.8 us (1%)
    ppermute x77, waiting for transfers between devices, over_col(): return lax.ppermute(block, 'col', [(i, i ^ step) for i in range(count)])  235 us
    reduce_scatter x6, waiting for transfers between devices, scatter_rows(): return lax.psum_scatter(total, ROW, scatter_dimension=0, tiled=True)  174 us
    all_gather x4, waiting for transfers between devices, gather_layers(): return lax.all_gather(part, ('section', ROW), axis=0, tiled=True)  172 us
    dot_general x38, matrix products, dot(): lax.dot_general(left, right, (((left_dim,), (right_dim,)), ((), ())), pre...  152 us
    ppermute x77, starting transfers between devices, over_col(): return lax.ppermute(block, 'col', [(i, i ^ step) for i in range(count)])  96 us
    ppermute x12, waiting for transfers between devices, along_row(): return lax.ppermute(block, ROW, route)  76.2 us
    unnamed x208, local copies, waits for them, and re-layouts  33.9 us
    ppermute x12, starting transfers between devices, along_row(): return lax.ppermute(block, ROW, route)  24.2 us
  transfers between devices with their start and end apart: 126, of which 75 were waited for; matrix products, arithmetic and copies ran while one was open for 20% of the time, Pallas kernels for 3%

profile of v3, /device:TPU:0, one launch (start us, length us, event | category | flops | bytes accessed | tf_op | source)
XLA Modules:
  0.0 1157.5 jit_solution(5165300011699076256)
XLA Ops:
  106.8 8.0 collective-permute-done.14
  119.5 11.2 all-gather.15.cloned.1.call-start
  147.8 35.8 %all-gather.9.cloned.1.call-done = bf16[3072,2304]{1,0:T(8,128)(2,1)} async-done(((bf16[384,2304]{1,0:T(8,128)(2,1)}), bf16[3072,2304]{1,0:T(8,128)(2,1)}) %all-gather.9.cloned.1.call-update) | async-done | bytes 14155792 | tf_op jit(solution)/shard_map/all_gather | solution.py:456
  198.6 64.2 %all-gather.11.cloned.1.call-done = bf16[3072,1152]{1,0:T(8,128)(2,1)} async-done(((bf16[384,1152]{1,0:T(8,128)(2,1)}), bf16[3072,1152]{1,0:T(8,128)(2,1)}) %all-gather.11.cloned.1.call-update) | async-done | bytes 7077904 | tf_op jit(solution)/shard_map/all_gather | solution.py:456
  273.8 9.4 collective-permute-done.23
  283.3 7.7 collective-permute-done.24
  294.2 8.2 collective-permute-done.26
  337.9 9.6 collective-permute-done.33.refs_4_
  368.7 8.2 collective-permute-done.40
  403.1 28.8 %all-gather.17.cloned.1.call-done = bf16[3072,2304]{1,0:T(8,128)(2,1)} async-done(((bf16[384,2304]{1,0:T(8,128)(2,1)}), bf16[3072,2304]{1,0:T(8,128)(2,1)}) %all-gather.17.cloned.1.call-update) | async-done | bytes 14155792 | tf_op jit(solution)/shard_map/all_gather | solution.py:456
  439.5 8.2 multiply_convert_fusion
  467.5 43.6 %all-gather.15.cloned.1.call-done = bf16[3072,1152]{1,0:T(8,128)(2,1)} async-done(((bf16[384,1152]{1,0:T(8,128)(2,1)}), bf16[3072,1152]{1,0:T(8,128)(2,1)}) %all-gather.15.cloned.1.call-update) | async-done | bytes 7077904 | tf_op jit(solution)/shard_map/all_gather | solution.py:456
  522.6 9.0 convolution_convert_fusion.1
  568.3 8.8 add_convert_fusion.1
  616.9 7.6 attend_back.2
  631.7 9.6 collective-permute-done.58
  646.8 11.2 collective-permute-done.59
  658.0 9.9 collective-permute-done.60
  676.1 9.3 collective-permute-done.71
  698.7 8.1 collective-permute-done.75
  745.5 11.5 collective-permute-done.80
  781.1 9.4 collective-permute-done.81
  802.4 9.0 collective-permute-done.84
  822.0 7.7 attend_back.3
  833.8 8.3 collective-permute-done.88
  846.4 9.9 collective-permute-done.89
  856.3 20.8 %collective-permute-done.90 = bf16[512,128]{1,0:T(8,128)(2,1)S(1)} collective-permute-done((bf16[512,128]{1,0:T(8,128)(2,1)S(1)}, bf16[512,128]{1,0:T(8,128)(2,1)S(1)}, u32[]{:S(2)}, u32[]{:S(2)}) %collective-permute-start.90) | collective-permute-done | bytes 131104 | tf_op jit(solution)/shard_map/ppermute | solution.py:53
  886.9 8.2 collective-permute-done.93
  913.9 11.3 reduce-scatter.11.cloned.1.call-done
  946.5 106.4 %reduce-scatter.9.cloned.1.call-done = bf16[384,2304]{1,0:T(8,128)(2,1)} async-done(((bf16[1536,2304]{1,0:T(8,128)(2,1)}), bf16[384,2304]{1,0:T(8,128)(2,1)}) %reduce-scatter.9.cloned.1.call-update) | async-done | bytes 1769488 | tf_op jit(solution)/shard_map/reduce_scatter | solution.py:512
  1067.1 24.7 %reduce-scatter.7.cloned.1.call-done = bf16[384,512]{1,0:T(8,128)(2,1)} async-done(((bf16[1536,512]{1,0:T(8,128)(2,1)}), bf16[384,512]{1,0:T(8,128)(2,1)}) %reduce-scatter.7.cloned.1.call-update) | async-done | bytes 393232 | tf_op jit(solution)/shard_map/reduce_scatter | solution.py:512
  1097.1 31.1 %reduce-scatter.17.cloned.1.call-done = bf16[384,512]{1,0:T(8,128)(2,1)} async-done(((bf16[1536,512]{1,0:T(8,128)(2,1)}), bf16[384,512]{1,0:T(8,128)(2,1)}) %reduce-scatter.17.cloned.1.call-update) | async-done | bytes 393232 | tf_op jit(solution)/shard_map/reduce_scatter | solution.py:512
  (654 shorter events, 565.7 us)
Async XLA Ops:
  7.2 51.9 %all-gather.7.cloned.1.call-start = ((), (), s32[]{:S(2)}) async-start(), calls=%async_computation.6 | async-start | bytes 3096576 | tf_op jit(solution)/shard_map/all_gather | solution.py:462
  12.3 171.3 %all-gather.9.cloned.1.call-start = ((), (), s32[]{:S(2)}) async-start(), calls=%async_computation.7 | async-start | bytes 15925248 | tf_op jit(solution)/shard_map/all_gather | solution.py:456
  22.9 239.9 %all-gather.11.cloned.1.call-start = ((), (), s32[]{:S(2)}) async-start(), calls=%async_computation.8 | async-start | bytes 7962624 | tf_op jit(solution)/shard_map/all_gather | solution.py:456
  25.2 20.1 %collective-permute-start = (bf16[512,384]{1,0:T(8,128)(2,1)}, bf16[512,384]{1,0:T(8,128)(2,1)}, u32[]{:S(2)}, u32[]{:S(2)}) collective-permute-start(bf16[512,384]{1,0:T(8,128)(2,1)} %get-tuple-element.246), channel_id=1, source_target_pairs={{0,1},{1,0},{2,3},{3,2},{4,5},{5,4},{6,7},{7,6},{8,9},{9,8},{10,11... | collective-permute-start | bytes 1179656 | tf_op jit(solution)/shard_map/ppermute | solution.py:43
  33.9 20.2 %collective-permute-start.22 = (bf16[384,1152]{1,0:T(8,128)(2,1)}, bf16[384,1152]{1,0:T(8,128)(2,1)}, u32[]{:S(2)}, u32[]{:S(2)}) collective-permute-start(bf16[384,1152]{1,0:T(8,128)(2,1)} %broadcast_select_fusion.9), channel_id=1, source_target_pairs={{0,16},{16,0},{1,17},{17,1},{2,18},{18,2},{3,19},{19,3},{4,20},{20... | collective-permute-start | bytes 2654216 | tf_op jit(solution)/shard_map/ppermute | solution.py:47
  56.8 255.8 %all-gather.13.cloned.1.call-start = ((), (), s32[]{:S(2)}) async-start(), calls=%async_computation.9 | async-start | bytes 3096576 | tf_op jit(solution)/shard_map/all_gather | solution.py:462
  100.7 331.2 %all-gather.17.cloned.1.call-start = ((), (), s32[]{:S(2)}) async-start(), calls=%async_computation.11 | async-start | bytes 15925248 | tf_op jit(solution)/shard_map/all_gather | solution.py:456
  119.5 391.6 %all-gather.15.cloned.1.call-start = ((), (), s32[]{:S(2)}) async-start(), calls=%async_computation.10 | async-start | bytes 7962624 | tf_op jit(solution)/shard_map/all_gather | solution.py:456
  324.0 578.5 %reduce-scatter.15.cloned.1.call-start = ((), (), s32[]{:S(2)}) async-start(), calls=%async_computation.16 | async-start | bytes 4423680 | tf_op jit(solution)/shard_map/reduce_scatter | solution.py:512
  360.8 24.5 %collective-permute-start.35 = (bf16[512,384]{1,0:T(8,128)(2,1)S(1)}, bf16[512,384]{1,0:T(8,128)(2,1)S(1)}, u32[]{:S(2)}, u32[]{:S(2)}) collective-permute-start(bf16[512,384]{1,0:T(8,128)(2,1)S(1)} %get-tuple-element.234), channel_id=1, source_target_pairs={{0,1},{1,0},{2,3},{3,2},{4,5},{5,4},{6,7},{7,6},{8,9},{9,8},{10,11... | collective-permute-start | bytes 1179656 | tf_op jit(solution)/shard_map/ppermute | solution.py:43
  531.6 36.7 %collective-permute-start.53 = (bf16[1536,2304]{1,0:T(8,128)(2,1)}, bf16[1536,2304]{1,0:T(8,128)(2,1)}, u32[]{:S(2)}, u32[]{:S(2)}) collective-permute-start(bf16[1536,2304]{1,0:T(8,128)(2,1)} %convolution_convert_fusion.1), channel_id=1, source_target_pairs={{0,16},{16,0},{1,17},{17,1},{2,18},{18,2},{3,19},{19,3},{4,20},{20... | collective-permute-start | bytes 21233672 | tf_op jit(solution)/shard_map/ppermute | solution.py:47
  555.1 22.1 %collective-permute-start.63 = (bf16[128,1536]{1,0:T(8,128)(2,1)}, bf16[128,1536]{1,0:T(8,128)(2,1)}, u32[]{:S(2)}, u32[]{:S(2)}) collective-permute-start(bf16[128,1536]{1,0:T(8,128)(2,1)} %get-tuple-element.179), channel_id=1, source_target_pairs={{0,3},{1,2},{2,1},{3,0},{4,7},{5,6},{6,5},{7,4},{8,11},{9,10},{10,... | collective-permute-start | bytes 1179656 | tf_op jit(solution)/shard_map/ppermute | solution.py:43
  559.1 24.7 %collective-permute-start.64 = (bf16[128,1536]{1,0:T(8,128)(2,1)S(1)}, bf16[128,1536]{1,0:T(8,128)(2,1)}, u32[]{:S(2)}, u32[]{:S(2)}) collective-permute-start(bf16[128,1536]{1,0:T(8,128)(2,1)S(1)} %get-tuple-element.181), channel_id=1, source_target_pairs={{0,1},{1,0},{2,3},{3,2},{4,5},{5,4},{6,7},{7,6},{8,9},{9,8},{10,11... | collective-permute-start | bytes 1179656 | tf_op jit(solution)/shard_map/ppermute | solution.py:43
  593.1 317.0 %reduce-scatter.13.cloned.1.call-start = ((), (), s32[]{:S(2)}) async-start(), calls=%async_computation.15 | async-start | bytes 4423680 | tf_op jit(solution)/shard_map/reduce_scatter | solution.py:512
  610.1 20.5 %collective-permute-start.70 = (bf16[512,384]{1,0:T(8,128)(2,1)S(1)}, bf16[512,384]{1,0:T(8,128)(2,1)}, u32[]{:S(2)}, u32[]{:S(2)}) collective-permute-start(bf16[512,384]{1,0:T(8,128)(2,1)S(1)} %get-tuple-element.223), channel_id=1, source_target_pairs={{16,0},{17,1},{18,2},{19,3},{20,4},{21,5},{22,6},{23,7},{24,8},{25... | collective-permute-start | bytes 1179656 | tf_op jit(solution)/shard_map/ppermute | solution.py:578
  628.9 39.0 %collective-permute-start.62 = (bf16[1536,384]{1,0:T(8,128)(2,1)S(1)}, bf16[1536,384]{1,0:T(8,128)(2,1)S(1)}, u32[]{:S(2)}, u32[]{:S(2)}) collective-permute-start(bf16[1536,384]{1,0:T(8,128)(2,1)S(1)} %get-tuple-element.279), channel_id=1, source_target_pairs={{0,16},{16,0},{1,17},{17,1},{2,18},{18,2},{3,19},{19,3},{4,20},{20... | collective-permute-start | bytes 3538952 | tf_op jit(solution)/shard_map/ppermute | solution.py:47
  642.8 25.1 %collective-permute-start.60 = (bf16[512,128]{1,0:T(8,128)(2,1)S(1)}, bf16[512,128]{1,0:T(8,128)(2,1)S(1)}, u32[]{:S(2)}, u32[]{:S(2)}) collective-permute-start(bf16[512,128]{1,0:T(8,128)(2,1)S(1)} %get-tuple-element.213), channel_id=1, source_target_pairs={{8,0},{12,4},{9,1},{13,5},{10,2},{14,6},{11,3},{15,7},{24,16},{28,... | collective-permute-start | bytes 393224 | tf_op jit(solution)/shard_map/ppermute | solution.py:53
  644.1 23.8 %collective-permute-start.61 = (bf16[512,128]{1,0:T(8,128)(2,1)S(1)}, bf16[512,128]{1,0:T(8,128)(2,1)S(1)}, u32[]{:S(2)}, u32[]{:S(2)}) collective-permute-start(bf16[512,128]{1,0:T(8,128)(2,1)S(1)} %get-tuple-element.212), channel_id=1, source_target_pairs={{12,0},{13,1},{14,2},{15,3},{28,16},{29,17},{30,18},{31,19}} | collective-permute-start | bytes 393224 | tf_op jit(solution)/shard_map/ppermute | solution.py:53
  726.7 198.5 %reduce-scatter.11.cloned.1.call-start = ((), (), s32[]{:S(2)}) async-start(), calls=%async_computation.14 | async-start | bytes 8847360 | tf_op jit(solution)/shard_map/reduce_scatter | solution.py:512
  727.5 325.4 %reduce-scatter.9.cloned.1.call-start = ((), (), s32[]{:S(2)}) async-start(), calls=%async_computation.13 | async-start | bytes 8847360 | tf_op jit(solution)/shard_map/reduce_scatter | solution.py:512
  763.2 328.6 %reduce-scatter.7.cloned.1.call-start = ((), (), s32[]{:S(2)}) async-start(), calls=%async_computation.12 | async-start | bytes 1966080 | tf_op jit(solution)/shard_map/reduce_scatter | solution.py:512
  833.8 43.5 %collective-permute-start.92 = (bf16[1536,384]{1,0:T(8,128)(2,1)S(1)}, bf16[1536,384]{1,0:T(8,128)(2,1)S(1)}, u32[]{:S(2)}, u32[]{:S(2)}) collective-permute-start(bf16[1536,384]{1,0:T(8,128)(2,1)S(1)} %get-tuple-element.281), channel_id=1, source_target_pairs={{0,16},{16,0},{1,17},{17,1},{2,18},{18,2},{3,19},{19,3},{4,20},{20... | collective-permute-start | bytes 3538952 | tf_op jit(solution)/shard_map/ppermute | solution.py:47
  843.6 33.6 %collective-permute-start.90 = (bf16[512,128]{1,0:T(8,128)(2,1)S(1)}, bf16[512,128]{1,0:T(8,128)(2,1)S(1)}, u32[]{:S(2)}, u32[]{:S(2)}) collective-permute-start(bf16[512,128]{1,0:T(8,128)(2,1)S(1)} %get-tuple-element.210), channel_id=1, source_target_pairs={{8,0},{12,4},{9,1},{13,5},{10,2},{14,6},{11,3},{15,7},{24,16},{28,... | collective-permute-start | bytes 393224 | tf_op jit(solution)/shard_map/ppermute | solution.py:53
  845.1 32.0 %collective-permute-start.91 = (bf16[512,128]{1,0:T(8,128)(2,1)S(1)}, bf16[512,128]{1,0:T(8,128)(2,1)S(1)}, u32[]{:S(2)}, u32[]{:S(2)}) collective-permute-start(bf16[512,128]{1,0:T(8,128)(2,1)S(1)} %get-tuple-element.209), channel_id=1, source_target_pairs={{12,0},{13,1},{14,2},{15,3},{28,16},{29,17},{30,18},{31,19}} | collective-permute-start | bytes 393224 | tf_op jit(solution)/shard_map/ppermute | solution.py:53
  902.4 225.9 %reduce-scatter.17.cloned.1.call-start = ((), (), s32[]{:S(2)}) async-start(), calls=%async_computation.17 | async-start | bytes 1966080 | tf_op jit(solution)/shard_map/reduce_scatter | solution.py:512
  910.1 33.1 %collective-permute-start.111 = (bf16[384,1152]{1,0:T(8,128)(2,1)}, bf16[384,1152]{1,0:T(8,128)(2,1)}, u32[]{:S(2)}, u32[]{:S(2)}) collective-permute-start(bf16[384,1152]{1,0:T(8,128)(2,1)} %reduce-scatter.13.cloned.1.call-done), channel_id=1, source_target_pairs={{16,0},{17,1},{18,2},{19,3},{20,4},{21,5},{22,6},{23,7},{24,8},{25... | collective-permute-start | bytes 2654216 | tf_op jit(solution)/shard_map/ppermute | solution.py:586
  925.2 138.0 %collective-permute-start.108 = (bf16[384,2304]{1,0:T(8,128)(2,1)}, bf16[384,2304]{1,0:T(8,128)(2,1)}, u32[]{:S(2)}, u32[]{:S(2)}) collective-permute-start(bf16[384,2304]{1,0:T(8,128)(2,1)} %reduce-scatter.11.cloned.1.call-done), channel_id=1, source_target_pairs={{0,16},{1,17},{2,18},{3,19},{4,20},{5,21},{6,22},{7,23},{8,24},{9,... | collective-permute-start | bytes 5308424 | tf_op jit(solution)/shard_map/ppermute | solution.py:586
  944.4 109.8 %collective-permute-start.98 = (bf16[128,384]{1,0:T(8,128)(2,1)S(1)}, bf16[128,384]{1,0:T(8,128)(2,1)S(1)}, u32[]{:S(2)}, u32[]{:S(2)}) collective-permute-start(bf16[128,384]{1,0:T(8,128)(2,1)S(1)} %get-tuple-element.219), channel_id=1, source_target_pairs={{0,2},{1,3},{2,0},{3,1},{4,6},{5,7},{6,4},{7,5},{8,10},{9,11},{10,... | collective-permute-start | bytes 294920 | tf_op jit(solution)/shard_map/ppermute | solution.py:43
  945.0 109.3 %collective-permute-start.99 = (bf16[128,384]{1,0:T(8,128)(2,1)S(1)}, bf16[128,384]{1,0:T(8,128)(2,1)S(1)}, u32[]{:S(2)}, u32[]{:S(2)}) collective-permute-start(bf16[128,384]{1,0:T(8,128)(2,1)S(1)} %get-tuple-element.218), channel_id=1, source_target_pairs={{0,3},{1,2},{2,1},{3,0},{4,7},{5,6},{6,5},{7,4},{8,11},{9,10},{10,... | collective-permute-start | bytes 294920 | tf_op jit(solution)/shard_map/ppermute | solution.py:43
  946.5 111.4 %collective-permute-start.107 = (f32[2,384]{1,0:T(2,128)S(1)}, f32[2,384]{1,0:T(2,128)S(1)}, u32[]{:S(2)}, u32[]{:S(2)}) collective-permute-start(f32[2,384]{1,0:T(2,128)S(1)} %add.525), channel_id=1, source_target_pairs={{0,8},{4,12},{8,0},{12,4},{1,9},{5,13},{9,1},{13,5},{2,10},{6,14},... | collective-permute-start | bytes 9224 | tf_op jit(solution)/shard_map/ppermute | solution.py:671
  1060.3 35.1 %collective-permute-start.100 = (bf16[512,384]{1,0:T(8,128)(2,1)}, bf16[512,384]{1,0:T(8,128)(2,1)}, u32[]{:S(2)}, u32[]{:S(2)}) collective-permute-start(bf16[512,384]{1,0:T(8,128)(2,1)} %get-tuple-element.216), channel_id=1, source_target_pairs={{0,16},{1,17},{2,18},{3,19},{4,20},{5,21},{6,22},{7,23},{8,24},{9,... | collective-permute-start | bytes 1179656 | tf_op jit(solution)/shard_map/ppermute | solution.py:578
  1093.5 34.8 %collective-permute-start.113 = (bf16[384,384]{1,0:T(8,128)(2,1)}, bf16[384,384]{1,0:T(8,128)(2,1)}, u32[]{:S(2)}, u32[]{:S(2)}) collective-permute-start(bf16[384,384]{1,0:T(8,128)(2,1)} %slice.252), channel_id=1, source_target_pairs={{16,0},{17,1},{18,2},{19,3},{20,4},{21,5},{22,6},{23,7},{24,8},{25... | collective-permute-start | bytes 884744 | tf_op jit(solution)/shard_map/ppermute | solution.py:586
  (185 other events, 2160.1 us)
Sparse Core Ops, SparseCore 0:
  12.4 37.4 all-gather.6
  52.1 131.4 all-gather.8
  185.2 77.5 all-gather.10
  264.9 33.4 all-gather.12
  300.4 131.4 all-gather.16
  433.4 77.6 all-gather.14
  593.2 66.6 reduce-scatter.14
  726.9 63.8 reduce-scatter.12
  793.1 132.1 reduce-scatter.10
  927.4 125.5 reduce-scatter.8
  1055.8 35.9 reduce-scatter.6
  1093.9 34.2 reduce-scatter.16

commit v4 on v3

--- a/solution.py
+++ b/solution.py
@@ -366,6 +366,46 @@
         ),
         name="attend_back",
     )(flags, order[:, None], order[None, :], cosine, signed, queries, grads, lse, keys, values)
+
+
+def settle_kernel(flag_ref, *refs):
+    half, out_ref = len(refs) // 2, refs[-1]
+    blocks = (refs[:half], refs[half:-1])
+    for layer, parts in enumerate(blocks):
+        for i, part in enumerate(parts):
+            mine = flag_ref[0] == layer
+            if len(parts) > 1:
+                low = pl.program_id(0) < pl.num_programs(0) // 2
+                mine = mine & (low if i == 0 else jnp.logical_not(low))
+
+            @pl.when(mine)
+            def _():
+                out_ref[...] = part[...].astype(F32).T
+
+
+def settle(flag, zero, one, units):
+    shard = zero[0].shape[0]
+    tile = 128
+    count = zero[0].shape[1] // tile
+    if len(zero) == 1:
+        maps = [lambda j: (0, j)]
+    else:
+        maps = [
+            lambda j: (0, jnp.minimum(j, count - 1)),
+            lambda j: (0, jnp.maximum(j - count, 0)),
+        ]
+    specs = [pl.BlockSpec((shard, tile), index_map) for index_map in maps]
+    return pl.pallas_call(
+        settle_kernel,
+        grid=(count * len(zero),),
+        in_specs=[pl.BlockSpec(memory_space=pltpu.SMEM), *specs, *specs],
+        out_specs=pl.BlockSpec((tile, shard), lambda j: (j, 0)),
+        out_shape=jax.ShapeDtypeStruct((units, shard), F32),
+        cost_estimate=pl.CostEstimate(
+            flops=units * shard, bytes_accessed=8 * units * shard, transcendentals=0
+        ),
+        name="settle",
+    )(flag, *zero, *one)
 
 
 def step(layer_input, g_out, attn_gain, w_query, w_keyval, w_out, ffn_gain, w_gate, w_up, w_down):
@@ -588,11 +628,10 @@
 
     attn_w = [gather_attn(attn_parts[0])]
     x_full = gather_width(lax.dynamic_index_in_dim(layer_input[:, 0], section, 0, keepdims=False))
-    gate_up_w = [gather_layers(gate_up_parts[0])]
+    ffn_w = gather_layers(jnp.concatenate([gate_up_parts[0], down_parts[0]], axis=1))
+    gate_up_w, down_w = [ffn_w[:, :wide]], [ffn_w[:, wide:]]
     normed, inverse = norm(x_full.astype(F32), gains[0, 0])
     resid_0, inverse_0 = x_full[:own_rows].astype(F32), inverse[:own_rows]
-    _, down_part = after(normed, down_parts[0])
-    down_w = [gather_layers(down_part)]
     attended, kept_attn_0 = attn_forward(normed, attn_w[0])
     _, attn_part = after(attended, attn_parts[1])
     attn_w.append(gather_attn(attn_part))
@@ -648,10 +687,11 @@
     def final(zero, one):
         return own_layer(to_core(0, zero), to_core(1, one))
 
-    final_gate, final_up = [
-        part[None, :, :units].astype(F32) for part in final(gate_up_0, gate_up_1)
-    ]
-    final_down = jnp.concatenate(final(down_0, down_1), axis=1)[:, :units].astype(F32).T[None]
+    flag = jnp.reshape(section, (1,)).astype(jnp.int32)
+    gate_up_0, gate_up_1 = to_core(0, gate_up_0), to_core(1, gate_up_1)
+    final_gate = settle(flag, gate_up_0[:1], gate_up_1[:1], units)
+    final_up = settle(flag, gate_up_0[1:], gate_up_1[1:], units)
+    final_down = settle(flag, to_core(0, down_0), to_core(1, down_1), units)
     attn_0, final_gate, final_up, final_down = after(attn_0, final_gate, final_up, final_down)
     final_query, final_out = final(attn_0[:, :query_cols], attn_1[:, :query_cols])
     final_keyval = by_section(attn_0[:, query_cols:], attn_1[:, query_cols:]).astype(F32)
@@ -681,9 +721,9 @@
         final_keyval[None],
         final_out.T[None].astype(F32),
         gain_sums[1:],
-        final_gate,
-        final_up,
-        final_down,
+        final_gate.T[None],
+        final_up.T[None],
+        final_down[None],
     )
 
 

time: 1170 us -> 1190 us (1.017)
  Pallas kernels: 34 us -> 68.9 us
  local copies, waits for them, and re-layouts: 54.5 us -> 32.2 us
  waiting for transfers between devices: 682 us -> 699 us
  matrix products: 152 us -> 165 us
  other arithmetic: 59.1 us -> 46.2 us
    pallas_call x0 -> x3, Pallas kernels: none -> 35.2 us  [settle(): pl.pallas_call(settle_kernel, grid=(count * len(zero),), in_specs=[pl.Blo...]
    reduce_scatter x6, waiting for transfers between devices: 174 us -> 204 us  [scatter_rows(): return lax.psum_scatter(total, ROW, scatter_dimension=0, tiled=True)]
    unnamed x208 -> x196, local copies, waits for them, and re-layouts: 33.9 us -> 16.5 us
    ppermute x12, waiting for transfers between devices: 76.2 us -> 63.1 us  [along_row(): return lax.ppermute(block, ROW, route)]
    dot_general x38, matrix products: 152 us -> 165 us  [dot(): lax.dot_general(left, right, (((left_dim,), (right_dim,)), ((), ())), pre...]
    all_gather x4 -> x3, waiting for transfers between devices: 172 us -> 165 us  [gather_layers(): return lax.all_gather(part, ('section', ROW), axis=0, tiled=True)]
  transfers between devices with their start and end apart: 126 -> 125, of which waited for: 75 -> 77; matrix products, arithmetic and copies ran while one was open for 20% -> 17% of each run, Pallas kernels for 3% -> 6%
where the time goes in v4:
time: 1190 us; the launch traced here: 1180 us
  waiting for transfers between devices  699 us (59%)
  matrix products  165 us (14%)
  starting transfers between devices  149 us (13%)
  Pallas kernels  68.9 us (6%)
  other arithmetic  46.2 us (4%)
  local copies, waits for them, and re-layouts  32.2 us (3%)
  between operations  16.3 us (1%)
    ppermute x77, waiting for transfers between devices, over_col(): return lax.ppermute(block, 'col', [(i, i ^ step) for i in range(count)])  237 us
    reduce_scatter x6, waiting for transfers between devices, scatter_rows(): return lax.psum_scatter(total, ROW, scatter_dimension=0, tiled=True)  204 us
    all_gather x3, waiting for transfers between devices, gather_layers(): return lax.all_gather(part, ('section', ROW), axis=0, tiled=True)  165 us
    dot_general x38, matrix products, dot(): lax.dot_general(left, right, (((left_dim,), (right_dim,)), ((), ())), pre...  165 us
    ppermute x77, starting transfers between devices, over_col(): return lax.ppermute(block, 'col', [(i, i ^ step) for i in range(count)])  98.3 us
    ppermute x12, waiting for transfers between devices, along_row(): return lax.ppermute(block, ROW, route)  63.1 us
    pallas_call x3, Pallas kernels, settle(): pl.pallas_call(settle_kernel, grid=(count * len(zero),), in_specs=[pl.Blo...  35.2 us
    ppermute x12, starting transfers between devices, along_row(): return lax.ppermute(block, ROW, route)  27.5 us
  transfers between devices with their start and end apart: 125, of which 77 were waited for; matrix products, arithmetic and copies ran while one was open for 17% of the time, Pallas kernels for 6%

profile of v4, /device:TPU:0, one launch (start us, length us, event | category | flops | bytes accessed | tf_op | source)
XLA Modules:
  0.0 1175.6 jit_solution(4293804584839703940)
XLA Ops:
  75.6 8.2 collective-permute-done.12.refs_4_
  95.7 9.4 collective-permute-done.14
  113.6 8.0 collective-permute-done.17
  128.9 109.9 %all-gather.8.cloned.1.call-done = bf16[3072,3456]{0,1:T(8,128)(2,1)} async-done(((bf16[384,3456]{0,1:T(8,128)(2,1)}), bf16[3072,3456]{0,1:T(8,128)(2,1)}) %all-gather.8.cloned.1.call-update) | async-done | bytes 21233680 | tf_op jit(solution)/shard_map/all_gather | solution.py:496
  245.0 10.2 multiply_convert_fusion.1
  268.2 9.4 collective-permute-done.23
  288.5 8.1 collective-permute-done.26
  336.2 9.4 collective-permute-done.33.refs_4_
  367.0 8.1 collective-permute-done.40
  400.0 13.7 %all-gather.14.cloned.1.call-done = bf16[3072,2304]{0,1:T(8,128)(2,1)} async-done(((bf16[384,2304]{0,1:T(8,128)(2,1)}), bf16[3072,2304]{0,1:T(8,128)(2,1)}) %all-gather.14.cloned.1.call-update) | async-done | bytes 14155792 | tf_op jit(solution)/shard_map/all_gather | solution.py:496
  420.6 10.7 multiply_convert_fusion
  450.9 41.6 %all-gather.12.cloned.1.call-done = bf16[3072,1152]{0,1:T(8,128)(2,1)} async-done(((bf16[384,1152]{0,1:T(8,128)(2,1)}), bf16[3072,1152]{0,1:T(8,128)(2,1)}) %all-gather.12.cloned.1.call-update) | async-done | bytes 7077904 | tf_op jit(solution)/shard_map/all_gather | solution.py:496
  504.1 9.2 convolution_convert_fusion.1
  549.8 9.3 add_convert_fusion.1
  609.6 10.0 collective-permute-done.58
  628.0 8.7 collective-permute-done.60
  650.9 8.0 collective-permute-done.71
  671.5 8.7 collective-permute-done.75
  723.0 11.3 collective-permute-done.80
  759.4 9.4 collective-permute-done.81
  781.0 8.7 collective-permute-done.84
  813.3 7.9 collective-permute-done.88
  825.5 10.4 collective-permute-done.89
  835.9 16.1 %collective-permute-done.90 = bf16[512,128]{1,0:T(8,128)(2,1)S(1)} collective-permute-done((bf16[512,128]{1,0:T(8,128)(2,1)S(1)}, bf16[512,128]{1,0:T(8,128)(2,1)S(1)}, u32[]{:S(2)}, u32[]{:S(2)}) %collective-permute-start.90) | collective-permute-done | bytes 131104 | tf_op jit(solution)/shard_map/ppermute | solution.py:53
  862.0 8.3 collective-permute-done.93
  886.6 61.1 %reduce-scatter.9.cloned.1.call-done.refs_0_ = bf16[384,2304]{1,0:T(8,128)(2,1)} async-done(((bf16[1536,2304]{1,0:T(8,128)(2,1)}), bf16[384,2304]{1,0:T(8,128)(2,1)}) %reduce-scatter.9.cloned.1.call-update) | async-done | bytes 1769488 | tf_op jit(solution)/shard_map/reduce_scatter | solution.py:552
  959.9 58.5 %reduce-scatter.15.cloned.1.call-done.refs_3_ = bf16[384,1152]{1,0:T(8,128)(2,1)} async-done(((bf16[1536,1152]{1,0:T(8,128)(2,1)}), bf16[384,1152]{1,0:T(8,128)(2,1)}) %reduce-scatter.15.cloned.1.call-update) | async-done | bytes 884752 | tf_op jit(solution)/shard_map/reduce_scatter | solution.py:552
  1019.9 67.6 %reduce-scatter.13.cloned.1.call-done.refs_0_ = bf16[384,1152]{1,0:T(8,128)(2,1)} async-done(((bf16[1536,1152]{1,0:T(8,128)(2,1)}), bf16[384,1152]{1,0:T(8,128)(2,1)}) %reduce-scatter.13.cloned.1.call-update) | async-done | bytes 884752 | tf_op jit(solution)/shard_map/reduce_scatter | solution.py:552
  1105.7 11.9 %settle.5 = f32[2240,384]{1,0:T(8,128)} custom-call(s32[1]{0:T(128)} %bitcast.35.flag_ref, bf16[384,1152]{1,0:T(8,128)(2,1)} %reduce-scatter.13.cloned.1.call-done.refs_0_, bf16[384,1152]{1,0:T(8,128)(2,1)} %collective-permute-done.110.refs_1_, bf16[384,1152]{1,0:T(8,128)(2,1)} %copy-done.35, bf16[384,1152]{1,0:T(8,128)(2,1)} %reduce-scatter.15.cloned.1.call-done.refs_3_), custom_call_target="tpu_custom_call" | custom-call | flops 860160 | bytes 6881280 | tf_op jit(solution)/shard_map/settle/pallas_call | solution.py:398
  1117.5 11.7 settle.3
  1130.5 11.7 settle.4
  1145.1 16.9 %reduce-scatter.17.cloned.1.call-done = bf16[384,512]{1,0:T(8,128)(2,1)} async-done(((bf16[1536,512]{1,0:T(8,128)(2,1)}), bf16[384,512]{1,0:T(8,128)(2,1)}) %reduce-scatter.17.cloned.1.call-update) | async-done | bytes 393232 | tf_op jit(solution)/shard_map/reduce_scatter | solution.py:552
  (638 shorter events, 547.1 us)
Async XLA Ops:
  7.2 42.9 %all-gather.6.cloned.1.call-start = ((), (), s32[]{:S(2)}) async-start(), calls=%async_computation.6 | async-start | bytes 3096576 | tf_op jit(solution)/shard_map/all_gather | solution.py:502
  12.5 226.3 %all-gather.8.cloned.1.call-start = ((), (), s32[]{:S(2)}) async-start(), calls=%async_computation.7 | async-start | bytes 23887872 | tf_op jit(solution)/shard_map/all_gather | solution.py:496
  23.2 283.7 %all-gather.10.cloned.1.call-start = ((), (), s32[]{:S(2)}) async-start(), calls=%async_computation.8 | async-start | bytes 3096576 | tf_op jit(solution)/shard_map/all_gather | solution.py:502
  89.6 324.1 %all-gather.14.cloned.1.call-start = ((), (), s32[]{:S(2)}) async-start(), calls=%async_computation.10 | async-start | bytes 15925248 | tf_op jit(solution)/shard_map/all_gather | solution.py:496
  110.1 382.4 %all-gather.12.cloned.1.call-start = ((), (), s32[]{:S(2)}) async-start(), calls=%async_computation.9 | async-start | bytes 7962624 | tf_op jit(solution)/shard_map/all_gather | solution.py:496
  323.7 558.5 %reduce-scatter.11.cloned.1.call-start = ((), (), s32[]{:S(2)}) async-start(), calls=%async_computation.13 | async-start | bytes 8847360 | tf_op jit(solution)/shard_map/reduce_scatter | solution.py:552
  355.5 19.6 %collective-permute-start.40 = (bf16[128,1536]{1,0:T(8,128)(2,1)S(1)}, bf16[128,1536]{1,0:T(8,128)(2,1)S(1)}, u32[]{:S(2)}, u32[]{:S(2)}) collective-permute-start(bf16[128,1536]{1,0:T(8,128)(2,1)S(1)} %get-tuple-element.192), channel_id=1, source_target_pairs={{0,1},{1,0},{2,3},{3,2},{4,5},{5,4},{6,7},{7,6},{8,9},{9,8},{10,11... | collective-permute-start | bytes 1179656 | tf_op jit(solution)/shard_map/ppermute | solution.py:43
  359.1 24.4 %collective-permute-start.35 = (bf16[512,384]{1,0:T(8,128)(2,1)S(1)}, bf16[512,384]{1,0:T(8,128)(2,1)S(1)}, u32[]{:S(2)}, u32[]{:S(2)}) collective-permute-start(bf16[512,384]{1,0:T(8,128)(2,1)S(1)} %get-tuple-element.232), channel_id=1, source_target_pairs={{0,1},{1,0},{2,3},{3,2},{4,5},{5,4},{6,7},{7,6},{8,9},{9,8},{10,11... | collective-permute-start | bytes 1179656 | tf_op jit(solution)/shard_map/ppermute | solution.py:43
  360.6 19.8 %collective-permute-start.36 = (bf16[512,384]{1,0:T(8,128)(2,1)S(1)}, bf16[512,384]{1,0:T(8,128)(2,1)S(1)}, u32[]{:S(2)}, u32[]{:S(2)}) collective-permute-start(bf16[512,384]{1,0:T(8,128)(2,1)S(1)} %get-tuple-element.232), channel_id=1, source_target_pairs={{0,2},{1,3},{2,0},{3,1},{4,6},{5,7},{6,4},{7,5},{8,10},{9,11},{10,... | collective-permute-start | bytes 1179656 | tf_op jit(solution)/shard_map/ppermute | solution.py:43
  513.3 36.5 %collective-permute-start.53 = (bf16[1536,2304]{1,0:T(8,128)(2,1)}, bf16[1536,2304]{1,0:T(8,128)(2,1)}, u32[]{:S(2)}, u32[]{:S(2)}) collective-permute-start(bf16[1536,2304]{1,0:T(8,128)(2,1)} %convolution_convert_fusion.1), channel_id=1, source_target_pairs={{0,16},{16,0},{1,17},{17,1},{2,18},{18,2},{3,19},{19,3},{4,20},{20... | collective-permute-start | bytes 21233672 | tf_op jit(solution)/shard_map/ppermute | solution.py:47
  530.0 19.0 %collective-permute-start.51 = (bf16[128,1536]{1,0:T(8,128)(2,1)S(1)}, bf16[128,1536]{1,0:T(8,128)(2,1)S(1)}, u32[]{:S(2)}, u32[]{:S(2)}) collective-permute-start(bf16[128,1536]{1,0:T(8,128)(2,1)S(1)} %get-tuple-element.186), channel_id=1, source_target_pairs={{0,1},{1,0},{2,3},{3,2},{4,5},{5,4},{6,7},{7,6},{8,9},{9,8},{10,11... | collective-permute-start | bytes 1179656 | tf_op jit(solution)/shard_map/ppermute | solution.py:43
  530.6 19.0 %collective-permute-start.52 = (bf16[128,1536]{1,0:T(8,128)(2,1)S(1)}, bf16[128,1536]{1,0:T(8,128)(2,1)S(1)}, u32[]{:S(2)}, u32[]{:S(2)}) collective-permute-start(bf16[128,1536]{1,0:T(8,128)(2,1)S(1)} %get-tuple-element.185), channel_id=1, source_target_pairs={{0,2},{1,3},{2,0},{3,1},{4,6},{5,7},{6,4},{7,5},{8,10},{9,11},{10,... | collective-permute-start | bytes 1179656 | tf_op jit(solution)/shard_map/ppermute | solution.py:43
  537.7 21.4 %collective-permute-start.63 = (bf16[128,1536]{1,0:T(8,128)(2,1)}, bf16[128,1536]{1,0:T(8,128)(2,1)}, u32[]{:S(2)}, u32[]{:S(2)}) collective-permute-start(bf16[128,1536]{1,0:T(8,128)(2,1)} %get-tuple-element.177), channel_id=1, source_target_pairs={{0,3},{1,2},{2,1},{3,0},{4,7},{5,6},{6,5},{7,4},{8,11},{9,10},{10,... | collective-permute-start | bytes 1179656 | tf_op jit(solution)/shard_map/ppermute | solution.py:43
  540.6 24.7 %collective-permute-start.64 = (bf16[128,1536]{1,0:T(8,128)(2,1)S(1)}, bf16[128,1536]{1,0:T(8,128)(2,1)}, u32[]{:S(2)}, u32[]{:S(2)}) collective-permute-start(bf16[128,1536]{1,0:T(8,128)(2,1)S(1)} %get-tuple-element.179), channel_id=1, source_target_pairs={{0,1},{1,0},{2,3},{3,2},{4,5},{5,4},{6,7},{7,6},{8,9},{9,8},{10,11... | collective-permute-start | bytes 1179656 | tf_op jit(solution)/shard_map/ppermute | solution.py:43
  589.0 19.4 %collective-permute-start.70 = (bf16[512,384]{1,0:T(8,128)(2,1)S(1)}, bf16[512,384]{1,0:T(8,128)(2,1)}, u32[]{:S(2)}, u32[]{:S(2)}) collective-permute-start(bf16[512,384]{1,0:T(8,128)(2,1)S(1)} %get-tuple-element.221), channel_id=1, source_target_pairs={{16,0},{17,1},{18,2},{19,3},{20,4},{21,5},{22,6},{23,7},{24,8},{25... | collective-permute-start | bytes 1179656 | tf_op jit(solution)/shard_map/ppermute | solution.py:618
  608.4 31.7 %collective-permute-start.62 = (bf16[1536,384]{1,0:T(8,128)(2,1)S(1)}, bf16[1536,384]{1,0:T(8,128)(2,1)S(1)}, u32[]{:S(2)}, u32[]{:S(2)}) collective-permute-start(bf16[1536,384]{1,0:T(8,128)(2,1)S(1)} %get-tuple-element.277), channel_id=1, source_target_pairs={{0,16},{16,0},{1,17},{17,1},{2,18},{18,2},{3,19},{19,3},{4,20},{20... | collective-permute-start | bytes 3538952 | tf_op jit(solution)/shard_map/ppermute | solution.py:47
  691.5 256.2 %reduce-scatter.9.cloned.1.call-start = ((), (), s32[]{:S(2)}) async-start(), calls=%async_computation.12 | async-start | bytes 8847360 | tf_op jit(solution)/shard_map/reduce_scatter | solution.py:552
  740.6 277.9 %reduce-scatter.15.cloned.1.call-start = ((), (), s32[]{:S(2)}) async-start(), calls=%async_computation.15 | async-start | bytes 4423680 | tf_op jit(solution)/shard_map/reduce_scatter | solution.py:552
  741.3 346.2 %reduce-scatter.13.cloned.1.call-start = ((), (), s32[]{:S(2)}) async-start(), calls=%async_computation.14 | async-start | bytes 4423680 | tf_op jit(solution)/shard_map/reduce_scatter | solution.py:552
  781.0 361.2 %reduce-scatter.7.cloned.1.call-start = ((), (), s32[]{:S(2)}) async-start(), calls=%async_computation.11 | async-start | bytes 1966080 | tf_op jit(solution)/shard_map/reduce_scatter | solution.py:552
  813.3 38.9 %collective-permute-start.92 = (bf16[1536,384]{1,0:T(8,128)(2,1)S(1)}, bf16[1536,384]{1,0:T(8,128)(2,1)S(1)}, u32[]{:S(2)}, u32[]{:S(2)}) collective-permute-start(bf16[1536,384]{1,0:T(8,128)(2,1)S(1)} %get-tuple-element.279), channel_id=1, source_target_pairs={{0,16},{16,0},{1,17},{17,1},{2,18},{18,2},{3,19},{19,3},{4,20},{20... | collective-permute-start | bytes 3538952 | tf_op jit(solution)/shard_map/ppermute | solution.py:47
  822.9 29.2 %collective-permute-start.90 = (bf16[512,128]{1,0:T(8,128)(2,1)S(1)}, bf16[512,128]{1,0:T(8,128)(2,1)S(1)}, u32[]{:S(2)}, u32[]{:S(2)}) collective-permute-start(bf16[512,128]{1,0:T(8,128)(2,1)S(1)} %get-tuple-element.208), channel_id=1, source_target_pairs={{8,0},{12,4},{9,1},{13,5},{10,2},{14,6},{11,3},{15,7},{24,16},{28,... | collective-permute-start | bytes 393224 | tf_op jit(solution)/shard_map/ppermute | solution.py:53
  824.2 27.9 %collective-permute-start.91 = (bf16[512,128]{1,0:T(8,128)(2,1)S(1)}, bf16[512,128]{1,0:T(8,128)(2,1)S(1)}, u32[]{:S(2)}, u32[]{:S(2)}) collective-permute-start(bf16[512,128]{1,0:T(8,128)(2,1)S(1)} %get-tuple-element.207), channel_id=1, source_target_pairs={{12,0},{13,1},{14,2},{15,3},{28,16},{29,17},{30,18},{31,19}} | collective-permute-start | bytes 393224 | tf_op jit(solution)/shard_map/ppermute | solution.py:53
  879.8 282.2 %reduce-scatter.17.cloned.1.call-start = ((), (), s32[]{:S(2)}) async-start(), calls=%async_computation.16 | async-start | bytes 1966080 | tf_op jit(solution)/shard_map/reduce_scatter | solution.py:552
  882.1 235.4 %collective-permute-start.108 = (bf16[384,2304]{1,0:T(8,128)(2,1)}, bf16[384,2304]{1,0:T(8,128)(2,1)}, u32[]{:S(2)}, u32[]{:S(2)}) collective-permute-start(bf16[384,2304]{1,0:T(8,128)(2,1)} %reduce-scatter.11.cloned.1.call-done.refs_1_), channel_id=1, source_target_pairs={{0,16},{1,17},{2,18},{3,19},{4,20},{5,21},{6,22},{7,23},{8,24},{9,... | collective-permute-start | bytes 5308424 | tf_op jit(solution)/shard_map/ppermute | solution.py:626
  885.6 66.5 %collective-permute-start.102 = (f32[2,1536]{1,0:T(2,128)}, f32[2,1536]{1,0:T(2,128)}, u32[]{:S(2)}, u32[]{:S(2)}) collective-permute-start(f32[2,1536]{1,0:T(2,128)} %broadcast_select_fusion.13), channel_id=1, source_target_pairs={{0,16},{16,0},{1,17},{17,1},{2,18},{18,2},{3,19},{19,3},{4,20},{20... | collective-permute-start | bytes 36872 | tf_op jit(solution)/shard_map/ppermute | solution.py:47
  947.7 181.5 %collective-permute-start.109 = (bf16[384,2304]{1,0:T(8,128)(2,1)}, bf16[384,2304]{1,0:T(8,128)(2,1)S(1)}, u32[]{:S(2)}, u32[]{:S(2)}) collective-permute-start(bf16[384,2304]{1,0:T(8,128)(2,1)} %reduce-scatter.9.cloned.1.call-done.refs_0_), channel_id=1, source_target_pairs={{16,0},{17,1},{18,2},{19,3},{20,4},{21,5},{22,6},{23,7},{24,8},{25... | collective-permute-start | bytes 5308424 | tf_op jit(solution)/shard_map/ppermute | solution.py:626
  952.1 136.6 %collective-permute-start.99 = (bf16[128,384]{1,0:T(8,128)(2,1)S(1)}, bf16[128,384]{1,0:T(8,128)(2,1)S(1)}, u32[]{:S(2)}, u32[]{:S(2)}) collective-permute-start(bf16[128,384]{1,0:T(8,128)(2,1)S(1)} %get-tuple-element.216), channel_id=1, source_target_pairs={{0,3},{1,2},{2,1},{3,0},{4,7},{5,6},{6,5},{7,4},{8,11},{9,10},{10,... | collective-permute-start | bytes 294920 | tf_op jit(solution)/shard_map/ppermute | solution.py:43
  954.6 63.9 %collective-permute-start.103 = (f32[2,384]{1,0:T(2,128)S(1)}, f32[2,384]{1,0:T(2,128)S(1)}, u32[]{:S(2)}, u32[]{:S(2)}) collective-permute-start(f32[2,384]{1,0:T(2,128)S(1)} %get-tuple-element.264), channel_id=1, source_target_pairs={{0,1},{1,0},{2,3},{3,2},{4,5},{5,4},{6,7},{7,6},{8,9},{9,8},{10,11... | collective-permute-start | bytes 9224 | tf_op jit(solution)/shard_map/ppermute | solution.py:43
  957.4 130.1 %collective-permute-start.104 = (f32[2,384]{1,0:T(2,128)S(1)}, f32[2,384]{1,0:T(2,128)S(1)}, u32[]{:S(2)}, u32[]{:S(2)}) collective-permute-start(f32[2,384]{1,0:T(2,128)S(1)} %get-tuple-element.262), channel_id=1, source_target_pairs={{0,2},{1,3},{2,0},{3,1},{4,6},{5,7},{6,4},{7,5},{8,10},{9,11},{10,... | collective-permute-start | bytes 9224 | tf_op jit(solution)/shard_map/ppermute | solution.py:43
  1018.5 85.5 %collective-permute-start.111 = (bf16[384,1152]{1,0:T(8,128)(2,1)}, bf16[384,1152]{1,0:T(8,128)(2,1)S(1)}, u32[]{:S(2)}, u32[]{:S(2)}) collective-permute-start(bf16[384,1152]{1,0:T(8,128)(2,1)} %reduce-scatter.15.cloned.1.call-done.refs_3_), channel_id=1, source_target_pairs={{0,16},{1,17},{2,18},{3,19},{4,20},{5,21},{6,22},{7,23},{8,24},{9,... | collective-permute-start | bytes 2654216 | tf_op jit(solution)/shard_map/ppermute | solution.py:626
  1101.0 44.0 %collective-permute-start.100 = (bf16[512,384]{1,0:T(8,128)(2,1)}, bf16[512,384]{1,0:T(8,128)(2,1)}, u32[]{:S(2)}, u32[]{:S(2)}) collective-permute-start(bf16[512,384]{1,0:T(8,128)(2,1)} %get-tuple-element.214), channel_id=1, source_target_pairs={{0,16},{1,17},{2,18},{3,19},{4,20},{5,21},{6,22},{7,23},{8,24},{9,... | collective-permute-start | bytes 1179656 | tf_op jit(solution)/shard_map/ppermute | solution.py:618
  (181 other events, 2108.3 us)
Sparse Core Ops, SparseCore 0:
  12.6 37.4 all-gather.5
  52.2 186.5 all-gather.7
  241.0 39.1 all-gather.9
  282.3 131.4 all-gather.13
  415.2 77.2 all-gather.11
  691.6 121.2 reduce-scatter.10
  815.2 132.4 reduce-scatter.8
  950.0 68.3 reduce-scatter.14
  1020.8 66.6 reduce-scatter.12
  1089.6 35.7 reduce-scatter.6
  1127.7 34.2 reduce-scatter.16

commit v5 on v4

--- a/solution.py
+++ b/solution.py
@@ -97,7 +97,7 @@
             own_ref[...] = z.astype(BF)
 
 
-def project_turn(normed, weight, tables, heads):
+def project_turn(normed, weight, layer, tables, heads):
     rows, depth = normed.shape
     step = rows // 2
     cols = (heads + 1) * HD
@@ -107,7 +107,7 @@
         grid=(2,),
         in_specs=[
             pl.BlockSpec((step, depth), lambda i: (i, 0)),
-            pl.BlockSpec((depth, cols), lambda i: (0, 0)),
+            pl.BlockSpec((depth, cols), lambda i: (0, layer)),
             *[table] * 4,
         ],
         out_specs=[
@@ -385,8 +385,8 @@
 
 def settle(flag, zero, one, units):
     shard = zero[0].shape[0]
-    tile = 128
-    count = zero[0].shape[1] // tile
+    tile = zero[0].shape[1] // 3
+    count = 3
     if len(zero) == 1:
         maps = [lambda j: (0, j)]
     else:
@@ -498,6 +498,10 @@
     def split_layers(both):
         return both[:full], both[full:]
 
+    def split_attn(both, layer):
+        first, out = layer * qkv_cols, 2 * qkv_cols + layer * query_cols
+        return both[:, first : first + qkv_cols], both[:, out : out + query_cols]
+
     def gather_attn(part):
         return lax.all_gather(part, (ROW, "section"), axis=0, tiled=True)
 
@@ -517,7 +521,7 @@
     tables = (cosine, signed, own_cosine, own_signed)
 
     def attn_forward(normed, attn_w):
-        queries, own = project_turn(normed, attn_w, tables, heads)
+        queries, own = project_turn(normed, *attn_w, tables, heads)
         first = over_col(own, 1)
         mine = [own] + [along_row(own, k) for k in range(1, SPAN)]
         later = over_col(jnp.concatenate(mine[1:], axis=0), 1)
@@ -527,7 +531,7 @@
         return attended, (normed, queries, keys, values, lse, attended)
 
     def attn_out(resid, attended, attn_w):
-        return resid + scatter_tokens(dot(attended, attn_w[:, qkv_cols:], 1, 1).astype(BF))
+        return resid + scatter_tokens(dot(attended, split_attn(*attn_w)[1], 1, 1).astype(BF))
 
     def ffn_gather(middle, ffn_gain):
         normed_own, inverse_ffn = norm(middle, ffn_gain)
@@ -579,7 +583,7 @@
 
     def attn_backward(grad_middle, resid, inverse_attn, kept, attn_gain, attn_w, *others):
         normed, queries, keys, values, lse, attended = kept
-        w_qkv, w_o = attn_w[:, :qkv_cols], attn_w[:, qkv_cols:]
+        w_qkv, w_o = split_attn(*attn_w)
         grad_attn_out = gather_tokens(grad_middle.astype(BF))
         grad_attended = dot(grad_attn_out, w_o, 1, 0).astype(BF)
         grad_query_raw, grad_keep, grad_send = attend_back(
@@ -626,15 +630,19 @@
         got = lax.ppermute(block, "section", [(1 - layer, layer)])
         return (block, got) if layer == 0 else (got, block)
 
-    attn_w = [gather_attn(attn_parts[0])]
+    both = gather_attn(
+        jnp.concatenate(
+            [part[:, :qkv_cols] for part in attn_parts] + [part[:, qkv_cols:] for part in attn_parts],
+            axis=1,
+        )
+    )
+    attn_w = [(both, 0), (both, 1)]
     x_full = gather_width(lax.dynamic_index_in_dim(layer_input[:, 0], section, 0, keepdims=False))
     ffn_w = gather_layers(jnp.concatenate([gate_up_parts[0], down_parts[0]], axis=1))
     gate_up_w, down_w = [ffn_w[:, :wide]], [ffn_w[:, wide:]]
     normed, inverse = norm(x_full.astype(F32), gains[0, 0])
     resid_0, inverse_0 = x_full[:own_rows].astype(F32), inverse[:own_rows]
     attended, kept_attn_0 = attn_forward(normed, attn_w[0])
-    _, attn_part = after(attended, attn_parts[1])
-    attn_w.append(gather_attn(attn_part))
     middle = attn_out(resid_0, attended, attn_w[0])
     _, gate_up_part = after(middle, gate_up_parts[1])
     gate_up_w.append(gather_layers(gate_up_part))

time: 1190 us -> 1170 us (0.983)
  Pallas kernels: 68.9 us -> 49.2 us
    all_gather x3, waiting for transfers between devices: 165 us -> 128 us  [gather_layers(): return lax.all_gather(part, ('section', ROW), axis=0, tiled=True)]
    all_gather x2 -> x1, waiting for transfers between devices: 1.81 us -> 24 us  [gather_attn(): return lax.all_gather(part, (ROW, 'section'), axis=0, tiled=True)]
    pallas_call x3, Pallas kernels: 35.2 us -> 15.7 us  [settle(): pl.pallas_call(settle_kernel, grid=(count * len(zero),), in_specs=[pl.Blo...]
    reduce_scatter x6, waiting for transfers between devices: 204 us -> 223 us  [scatter_rows(): return lax.psum_scatter(total, ROW, scatter_dimension=0, tiled=True)]
  transfers between devices with their start and end apart: 125 -> 124, of which waited for: 77 -> 78; matrix products, arithmetic and copies ran while one was open for 17% -> 17% of each run, Pallas kernels for 6% -> 4%
where the time goes in v5:
time: 1170 us; the launch traced here: 1160 us
  waiting for transfers between devices  706 us (60%)
  matrix products  169 us (14%)
  starting transfers between devices  149 us (13%)
  Pallas kernels  49.2 us (4%)
  other arithmetic  44 us (4%)
  local copies, waits for them, and re-layouts  31.1 us (3%)
  between operations  16.6 us (1%)
    ppermute x77, waiting for transfers between devices, over_col(): return lax.ppermute(block, 'col', [(i, i ^ step) for i in range(count)])  239 us
    reduce_scatter x6, waiting for transfers between devices, scatter_rows(): return lax.psum_scatter(total, ROW, scatter_dimension=0, tiled=True)  223 us
    dot_general x38, matrix products, dot(): lax.dot_general(left, right, (((left_dim,), (right_dim,)), ((), ())), pre...  169 us
    all_gather x3, waiting for transfers between devices, gather_layers(): return lax.all_gather(part, ('section', ROW), axis=0, tiled=True)  128 us
    ppermute x77, starting transfers between devices, over_col(): return lax.ppermute(block, 'col', [(i, i ^ step) for i in range(count)])  99.2 us
    ppermute x12, waiting for transfers between devices, along_row(): return lax.ppermute(block, ROW, route)  65 us
    ppermute x12, starting transfers between devices, along_row(): return lax.ppermute(block, ROW, route)  26.3 us
    all_gather x1, waiting for transfers between devices, gather_attn(): return lax.all_gather(part, (ROW, 'section'), axis=0, tiled=True)  24 us
  transfers between devices with their start and end apart: 124, of which 78 were waited for; matrix products, arithmetic and copies ran while one was open for 17% of the time, Pallas kernels for 4%

profile of v5, /device:TPU:0, one launch (start us, length us, event | category | flops | bytes accessed | tf_op | source)
XLA Modules:
  0.0 1164.4 jit_solution(1985214397172990099)
XLA Ops:
  49.4 24.0 %all-gather.5.cloned.1.call-done.w_ref = bf16[1536,1792]{1,0:T(8,128)(2,1)} async-done(((bf16[192,1792]{1,0:T(8,128)(2,1)}), bf16[1536,1792]{1,0:T(8,128)(2,1)}) %all-gather.5.cloned.1.call-update) | async-done | bytes 5505040 | tf_op jit(solution)/shard_map/all_gather | solution.py:506
  98.7 8.2 collective-permute-done.12.refs_4_
  118.8 9.4 collective-permute-done.14
  136.7 8.1 collective-permute-done.17
  152.0 109.8 %all-gather.7.cloned.1.call-done = bf16[3072,3456]{0,1:T(8,128)(2,1)} async-done(((bf16[384,3456]{0,1:T(8,128)(2,1)}), bf16[3072,3456]{0,1:T(8,128)(2,1)}) %all-gather.7.cloned.1.call-update) | async-done | bytes 21233680 | tf_op jit(solution)/shard_map/all_gather | solution.py:496
  268.0 10.2 multiply_convert_fusion.1
  291.5 9.4 collective-permute-done.23
  301.0 7.8 collective-permute-done.24
  312.0 8.1 collective-permute-done.26
  359.6 9.5 collective-permute-done.33.refs_4_
  390.4 8.1 collective-permute-done.40
  430.6 10.8 multiply_convert_fusion
  461.0 18.4 %all-gather.9.cloned.1.call-done = bf16[3072,1152]{0,1:T(8,128)(2,1)} async-done(((bf16[384,1152]{0,1:T(8,128)(2,1)}), bf16[3072,1152]{0,1:T(8,128)(2,1)}) %all-gather.9.cloned.1.call-update) | async-done | bytes 7077904 | tf_op jit(solution)/shard_map/all_gather | solution.py:496
  491.0 9.2 convolution_convert_fusion.1
  536.6 9.2 add_convert_fusion.1
  596.4 10.0 collective-permute-done.58
  614.8 8.8 collective-permute-done.60
  639.1 8.0 collective-permute-done.71
  647.1 8.2 collective-permute-done.72
  660.1 8.7 collective-permute-done.75
  710.8 11.4 collective-permute-done.80
  747.0 9.4 collective-permute-done.81
  768.1 8.6 collective-permute-done.84
  800.5 7.8 collective-permute-done.88
  812.5 11.5 collective-permute-done.89
  824.0 16.2 %collective-permute-done.90 = bf16[512,128]{1,0:T(8,128)(2,1)S(1)} collective-permute-done((bf16[512,128]{1,0:T(8,128)(2,1)S(1)}, bf16[512,128]{1,0:T(8,128)(2,1)S(1)}, u32[]{:S(2)}, u32[]{:S(2)}) %collective-permute-start.90) | collective-permute-done | bytes 131104 | tf_op jit(solution)/shard_map/ppermute | solution.py:53
  851.6 8.2 collective-permute-done.93
  859.8 8.0 collective-permute-done.94
  874.8 61.4 %reduce-scatter.9.cloned.1.call-done.refs_0_ = bf16[384,2304]{1,0:T(8,128)(2,1)} async-done(((bf16[1536,2304]{1,0:T(8,128)(2,1)}), bf16[384,2304]{1,0:T(8,128)(2,1)}) %reduce-scatter.9.cloned.1.call-update) | async-done | bytes 1769488 | tf_op jit(solution)/shard_map/reduce_scatter | solution.py:556
  949.4 57.5 %reduce-scatter.15.cloned.1.call-done.refs_3_ = bf16[384,1152]{1,0:T(8,128)(2,1)} async-done(((bf16[1536,1152]{1,0:T(8,128)(2,1)}), bf16[384,1152]{1,0:T(8,128)(2,1)}) %reduce-scatter.15.cloned.1.call-update) | async-done | bytes 884752 | tf_op jit(solution)/shard_map/reduce_scatter | solution.py:556
  1008.3 67.6 %reduce-scatter.13.cloned.1.call-done.refs_0_ = bf16[384,1152]{1,0:T(8,128)(2,1)} async-done(((bf16[1536,1152]{1,0:T(8,128)(2,1)}), bf16[384,1152]{1,0:T(8,128)(2,1)}) %reduce-scatter.13.cloned.1.call-update) | async-done | bytes 884752 | tf_op jit(solution)/shard_map/reduce_scatter | solution.py:556
  1117.0 33.5 %reduce-scatter.17.cloned.1.call-done = bf16[384,512]{1,0:T(8,128)(2,1)} async-done(((bf16[1536,512]{1,0:T(8,128)(2,1)}), bf16[384,512]{1,0:T(8,128)(2,1)}) %reduce-scatter.17.cloned.1.call-update) | async-done | bytes 393232 | tf_op jit(solution)/shard_map/reduce_scatter | solution.py:556
  (628 shorter events, 542.6 us)
Async XLA Ops:
  7.2 66.2 %all-gather.5.cloned.1.call-start = ((), (), s32[]{:S(2)}) async-start(), calls=%async_computation.6 | async-start | bytes 6193152 | tf_op jit(solution)/shard_map/all_gather | solution.py:506
  12.5 249.3 %all-gather.7.cloned.1.call-start = ((), (), s32[]{:S(2)}) async-start(), calls=%async_computation.7 | async-start | bytes 23887872 | tf_op jit(solution)/shard_map/all_gather | solution.py:496
  24.3 399.4 %all-gather.11.cloned.1.call-start = ((), (), s32[]{:S(2)}) async-start(), calls=%async_computation.9 | async-start | bytes 15925248 | tf_op jit(solution)/shard_map/all_gather | solution.py:496
  133.2 346.2 %all-gather.9.cloned.1.call-start = ((), (), s32[]{:S(2)}) async-start(), calls=%async_computation.8 | async-start | bytes 7962624 | tf_op jit(solution)/shard_map/all_gather | solution.py:496
  347.0 523.2 %reduce-scatter.11.cloned.1.call-start = ((), (), s32[]{:S(2)}) async-start(), calls=%async_computation.12 | async-start | bytes 8847360 | tf_op jit(solution)/shard_map/reduce_scatter | solution.py:556
  378.9 19.6 %collective-permute-start.40 = (bf16[128,1536]{1,0:T(8,128)(2,1)S(1)}, bf16[128,1536]{1,0:T(8,128)(2,1)S(1)}, u32[]{:S(2)}, u32[]{:S(2)}) collective-permute-start(bf16[128,1536]{1,0:T(8,128)(2,1)S(1)} %get-tuple-element.190), channel_id=1, source_target_pairs={{0,1},{1,0},{2,3},{3,2},{4,5},{5,4},{6,7},{7,6},{8,9},{9,8},{10,11... | collective-permute-start | bytes 1179656 | tf_op jit(solution)/shard_map/ppermute | solution.py:43
  382.4 24.4 %collective-permute-start.35 = (bf16[512,384]{1,0:T(8,128)(2,1)S(1)}, bf16[512,384]{1,0:T(8,128)(2,1)S(1)}, u32[]{:S(2)}, u32[]{:S(2)}) collective-permute-start(bf16[512,384]{1,0:T(8,128)(2,1)S(1)} %get-tuple-element.230), channel_id=1, source_target_pairs={{0,1},{1,0},{2,3},{3,2},{4,5},{5,4},{6,7},{7,6},{8,9},{9,8},{10,11... | collective-permute-start | bytes 1179656 | tf_op jit(solution)/shard_map/ppermute | solution.py:43
  384.0 19.9 %collective-permute-start.36 = (bf16[512,384]{1,0:T(8,128)(2,1)S(1)}, bf16[512,384]{1,0:T(8,128)(2,1)S(1)}, u32[]{:S(2)}, u32[]{:S(2)}) collective-permute-start(bf16[512,384]{1,0:T(8,128)(2,1)S(1)} %get-tuple-element.230), channel_id=1, source_target_pairs={{0,2},{1,3},{2,0},{3,1},{4,6},{5,7},{6,4},{7,5},{8,10},{9,11},{10,... | collective-permute-start | bytes 1179656 | tf_op jit(solution)/shard_map/ppermute | solution.py:43
  500.2 36.5 %collective-permute-start.53 = (bf16[1536,2304]{1,0:T(8,128)(2,1)}, bf16[1536,2304]{1,0:T(8,128)(2,1)}, u32[]{:S(2)}, u32[]{:S(2)}) collective-permute-start(bf16[1536,2304]{1,0:T(8,128)(2,1)} %convolution_convert_fusion.1), channel_id=1, source_target_pairs={{0,16},{16,0},{1,17},{17,1},{2,18},{18,2},{3,19},{19,3},{4,20},{20... | collective-permute-start | bytes 21233672 | tf_op jit(solution)/shard_map/ppermute | solution.py:47
  517.4 19.0 %collective-permute-start.52 = (bf16[128,1536]{1,0:T(8,128)(2,1)S(1)}, bf16[128,1536]{1,0:T(8,128)(2,1)S(1)}, u32[]{:S(2)}, u32[]{:S(2)}) collective-permute-start(bf16[128,1536]{1,0:T(8,128)(2,1)S(1)} %get-tuple-element.183), channel_id=1, source_target_pairs={{0,2},{1,3},{2,0},{3,1},{4,6},{5,7},{6,4},{7,5},{8,10},{9,11},{10,... | collective-permute-start | bytes 1179656 | tf_op jit(solution)/shard_map/ppermute | solution.py:43
  524.5 21.4 %collective-permute-start.63 = (bf16[128,1536]{1,0:T(8,128)(2,1)}, bf16[128,1536]{1,0:T(8,128)(2,1)}, u32[]{:S(2)}, u32[]{:S(2)}) collective-permute-start(bf16[128,1536]{1,0:T(8,128)(2,1)} %get-tuple-element.175), channel_id=1, source_target_pairs={{0,3},{1,2},{2,1},{3,0},{4,7},{5,6},{6,5},{7,4},{8,11},{9,10},{10,... | collective-permute-start | bytes 1179656 | tf_op jit(solution)/shard_map/ppermute | solution.py:43
  527.4 24.7 %collective-permute-start.64 = (bf16[128,1536]{1,0:T(8,128)(2,1)S(1)}, bf16[128,1536]{1,0:T(8,128)(2,1)}, u32[]{:S(2)}, u32[]{:S(2)}) collective-permute-start(bf16[128,1536]{1,0:T(8,128)(2,1)S(1)} %get-tuple-element.177), channel_id=1, source_target_pairs={{0,1},{1,0},{2,3},{3,2},{4,5},{5,4},{6,7},{7,6},{8,9},{9,8},{10,11... | collective-permute-start | bytes 1179656 | tf_op jit(solution)/shard_map/ppermute | solution.py:43
  575.9 19.4 %collective-permute-start.70 = (bf16[512,384]{1,0:T(8,128)(2,1)S(1)}, bf16[512,384]{1,0:T(8,128)(2,1)}, u32[]{:S(2)}, u32[]{:S(2)}) collective-permute-start(bf16[512,384]{1,0:T(8,128)(2,1)S(1)} %get-tuple-element.219), channel_id=1, source_target_pairs={{16,0},{17,1},{18,2},{19,3},{20,4},{21,5},{22,6},{23,7},{24,8},{25... | collective-permute-start | bytes 1179656 | tf_op jit(solution)/shard_map/ppermute | solution.py:622
  595.2 31.7 %collective-permute-start.62 = (bf16[1536,384]{1,0:T(8,128)(2,1)S(1)}, bf16[1536,384]{1,0:T(8,128)(2,1)S(1)}, u32[]{:S(2)}, u32[]{:S(2)}) collective-permute-start(bf16[1536,384]{1,0:T(8,128)(2,1)S(1)} %get-tuple-element.275), channel_id=1, source_target_pairs={{0,16},{16,0},{1,17},{17,1},{2,18},{18,2},{3,19},{19,3},{4,20},{20... | collective-permute-start | bytes 3538952 | tf_op jit(solution)/shard_map/ppermute | solution.py:47
  635.6 19.7 %collective-permute-start.72 = (bf16[128,1536]{1,0:T(8,128)(2,1)}, bf16[128,1536]{1,0:T(8,128)(2,1)}, u32[]{:S(2)}, u32[]{:S(2)}) collective-permute-start(bf16[128,1536]{1,0:T(8,128)(2,1)} %get-tuple-element.174), channel_id=1, source_target_pairs={{0,1},{1,0},{2,3},{3,2},{4,5},{5,4},{6,7},{7,6},{8,9},{9,8},{10,11... | collective-permute-start | bytes 1179656 | tf_op jit(solution)/shard_map/ppermute | solution.py:43
  680.1 256.1 %reduce-scatter.9.cloned.1.call-start = ((), (), s32[]{:S(2)}) async-start(), calls=%async_computation.11 | async-start | bytes 8847360 | tf_op jit(solution)/shard_map/reduce_scatter | solution.py:556
  728.4 278.5 %reduce-scatter.15.cloned.1.call-start = ((), (), s32[]{:S(2)}) async-start(), calls=%async_computation.14 | async-start | bytes 4423680 | tf_op jit(solution)/shard_map/reduce_scatter | solution.py:556
  729.2 346.8 %reduce-scatter.13.cloned.1.call-start = ((), (), s32[]{:S(2)}) async-start(), calls=%async_computation.13 | async-start | bytes 4423680 | tf_op jit(solution)/shard_map/reduce_scatter | solution.py:556
  768.1 346.0 %reduce-scatter.7.cloned.1.call-start = ((), (), s32[]{:S(2)}) async-start(), calls=%async_computation.10 | async-start | bytes 1966080 | tf_op jit(solution)/shard_map/reduce_scatter | solution.py:556
  800.4 40.0 %collective-permute-start.92 = (bf16[1536,384]{1,0:T(8,128)(2,1)S(1)}, bf16[1536,384]{1,0:T(8,128)(2,1)S(1)}, u32[]{:S(2)}, u32[]{:S(2)}) collective-permute-start(bf16[1536,384]{1,0:T(8,128)(2,1)S(1)} %get-tuple-element.277), channel_id=1, source_target_pairs={{0,16},{16,0},{1,17},{17,1},{2,18},{18,2},{3,19},{19,3},{4,20},{20... | collective-permute-start | bytes 3538952 | tf_op jit(solution)/shard_map/ppermute | solution.py:47
  809.9 30.4 %collective-permute-start.90 = (bf16[512,128]{1,0:T(8,128)(2,1)S(1)}, bf16[512,128]{1,0:T(8,128)(2,1)S(1)}, u32[]{:S(2)}, u32[]{:S(2)}) collective-permute-start(bf16[512,128]{1,0:T(8,128)(2,1)S(1)} %get-tuple-element.206), channel_id=1, source_target_pairs={{8,0},{12,4},{9,1},{13,5},{10,2},{14,6},{11,3},{15,7},{24,16},{28,... | collective-permute-start | bytes 393224 | tf_op jit(solution)/shard_map/ppermute | solution.py:53
  811.2 29.1 %collective-permute-start.91 = (bf16[512,128]{1,0:T(8,128)(2,1)S(1)}, bf16[512,128]{1,0:T(8,128)(2,1)S(1)}, u32[]{:S(2)}, u32[]{:S(2)}) collective-permute-start(bf16[512,128]{1,0:T(8,128)(2,1)S(1)} %get-tuple-element.205), channel_id=1, source_target_pairs={{12,0},{13,1},{14,2},{15,3},{28,16},{29,17},{30,18},{31,19}} | collective-permute-start | bytes 393224 | tf_op jit(solution)/shard_map/ppermute | solution.py:53
  869.3 281.2 %reduce-scatter.17.cloned.1.call-start = ((), (), s32[]{:S(2)}) async-start(), calls=%async_computation.15 | async-start | bytes 1966080 | tf_op jit(solution)/shard_map/reduce_scatter | solution.py:556
  870.2 230.0 %collective-permute-start.108 = (bf16[384,2304]{1,0:T(8,128)(2,1)}, bf16[384,2304]{1,0:T(8,128)(2,1)}, u32[]{:S(2)}, u32[]{:S(2)}) collective-permute-start(bf16[384,2304]{1,0:T(8,128)(2,1)} %reduce-scatter.11.cloned.1.call-done.refs_1_), channel_id=1, source_target_pairs={{0,16},{1,17},{2,18},{3,19},{4,20},{5,21},{6,22},{7,23},{8,24},{9,... | collective-permute-start | bytes 5308424 | tf_op jit(solution)/shard_map/ppermute | solution.py:630
  873.7 67.9 %collective-permute-start.102 = (f32[2,1536]{1,0:T(2,128)S(1)}, f32[2,1536]{1,0:T(2,128)S(1)}, u32[]{:S(2)}, u32[]{:S(2)}) collective-permute-start(f32[2,1536]{1,0:T(2,128)S(1)} %broadcast_select_fusion.13), channel_id=1, source_target_pairs={{0,16},{16,0},{1,17},{17,1},{2,18},{18,2},{3,19},{19,3},{4,20},{20... | collective-permute-start | bytes 36872 | tf_op jit(solution)/shard_map/ppermute | solution.py:47
  936.2 168.9 %collective-permute-start.109 = (bf16[384,2304]{1,0:T(8,128)(2,1)}, bf16[384,2304]{1,0:T(8,128)(2,1)S(1)}, u32[]{:S(2)}, u32[]{:S(2)}) collective-permute-start(bf16[384,2304]{1,0:T(8,128)(2,1)} %reduce-scatter.9.cloned.1.call-done.refs_0_), channel_id=1, source_target_pairs={{16,0},{17,1},{18,2},{19,3},{20,4},{21,5},{22,6},{23,7},{24,8},{25... | collective-permute-start | bytes 5308424 | tf_op jit(solution)/shard_map/ppermute | solution.py:630
  941.7 135.6 %collective-permute-start.99 = (bf16[128,384]{1,0:T(8,128)(2,1)S(1)}, bf16[128,384]{1,0:T(8,128)(2,1)S(1)}, u32[]{:S(2)}, u32[]{:S(2)}) collective-permute-start(bf16[128,384]{1,0:T(8,128)(2,1)S(1)} %get-tuple-element.214), channel_id=1, source_target_pairs={{0,3},{1,2},{2,1},{3,0},{4,7},{5,6},{6,5},{7,4},{8,11},{9,10},{10,... | collective-permute-start | bytes 294920 | tf_op jit(solution)/shard_map/ppermute | solution.py:43
  944.1 62.8 %collective-permute-start.103 = (f32[2,384]{1,0:T(2,128)S(1)}, f32[2,384]{1,0:T(2,128)S(1)}, u32[]{:S(2)}, u32[]{:S(2)}) collective-permute-start(f32[2,384]{1,0:T(2,128)S(1)} %get-tuple-element.262), channel_id=1, source_target_pairs={{0,1},{1,0},{2,3},{3,2},{4,5},{5,4},{6,7},{7,6},{8,9},{9,8},{10,11... | collective-permute-start | bytes 9224 | tf_op jit(solution)/shard_map/ppermute | solution.py:43
  946.9 129.0 %collective-permute-start.104 = (f32[2,384]{1,0:T(2,128)S(1)}, f32[2,384]{1,0:T(2,128)S(1)}, u32[]{:S(2)}, u32[]{:S(2)}) collective-permute-start(f32[2,384]{1,0:T(2,128)S(1)} %get-tuple-element.260), channel_id=1, source_target_pairs={{0,2},{1,3},{2,0},{3,1},{4,6},{5,7},{6,4},{7,5},{8,10},{9,11},{10,... | collective-permute-start | bytes 9224 | tf_op jit(solution)/shard_map/ppermute | solution.py:43
  1006.9 85.6 %collective-permute-start.111 = (bf16[384,1152]{1,0:T(8,128)(2,1)}, bf16[384,1152]{1,0:T(8,128)(2,1)S(1)}, u32[]{:S(2)}, u32[]{:S(2)}) collective-permute-start(bf16[384,1152]{1,0:T(8,128)(2,1)} %reduce-scatter.15.cloned.1.call-done.refs_3_), channel_id=1, source_target_pairs={{0,16},{1,17},{2,18},{3,19},{4,20},{5,21},{6,22},{7,23},{8,24},{9,... | collective-permute-start | bytes 2654216 | tf_op jit(solution)/shard_map/ppermute | solution.py:630
  1089.7 27.2 %collective-permute-start.100 = (bf16[512,384]{1,0:T(8,128)(2,1)}, bf16[512,384]{1,0:T(8,128)(2,1)}, u32[]{:S(2)}, u32[]{:S(2)}) collective-permute-start(bf16[512,384]{1,0:T(8,128)(2,1)} %get-tuple-element.212), channel_id=1, source_target_pairs={{0,16},{1,17},{2,18},{3,19},{4,20},{5,21},{6,22},{7,23},{8,24},{9,... | collective-permute-start | bytes 1179656 | tf_op jit(solution)/shard_map/ppermute | solution.py:622
  1115.0 35.5 %collective-permute-start.113 = (bf16[384,384]{1,0:T(8,128)(2,1)S(1)}, bf16[384,384]{1,0:T(8,128)(2,1)S(1)}, u32[]{:S(2)}, u32[]{:S(2)}) collective-permute-start(bf16[384,384]{1,0:T(8,128)(2,1)S(1)} %slice.262), channel_id=1, source_target_pairs={{16,0},{17,1},{18,2},{19,3},{20,4},{21,5},{22,6},{23,7},{24,8},{25... | collective-permute-start | bytes 884744 | tf_op jit(solution)/shard_map/ppermute | solution.py:630
  (174 other events, 2212.3 us)
Sparse Core Ops, SparseCore 0:
  12.6 60.7 all-gather.4
  75.6 186.1 all-gather.6
  264.0 136.5 all-gather.10
  402.1 77.2 all-gather.8
  680.3 121.2 reduce-scatter.10
  803.7 132.4 reduce-scatter.8
  938.5 68.3 reduce-scatter.14
  1009.2 66.6 reduce-scatter.12
  1078.3 35.7 reduce-scatter.6
  1116.2 34.2 reduce-scatter.16

commit v6 on v5

--- a/solution.py
+++ b/solution.py
@@ -684,24 +684,25 @@
     grad_middle, gate_up_0, down_0, gain_ffn_0 = ffn_backward(
         0, grad_1.astype(F32), branch, down_total, kept_ffn_0, gains[0, 1], gate_up_w[0], down_w[0]
     )
-    grad_0, attn_0, gain_attn_0, _ = attn_backward(
-        grad_middle, resid_0, inverse_0, kept_attn_0, gains[0, 0], attn_w[0]
-    )
+    flag = jnp.reshape(section, (1,)).astype(jnp.int32)
+    grad_0, attn_0, gain_attn_0, others = attn_backward(
+        grad_middle, resid_0, inverse_0, kept_attn_0, gains[0, 0], attn_w[0],
+        settle(flag, to_core(0, down_0), to_core(1, down_1), units),
+        *to_core(1, gate_up_1),
+        *to_core(1, attn_1[:, :query_cols]),
+        *grads_1,
+    )
+    final_down, gate_up_1, attn_1_out, grads_1 = others[0], others[1:3], others[3:5], others[5:]
     grads_in = by_layer(core_swap(0, width_from_tokens(grad_0.astype(BF))), grads_1)
 
     def own_layer(first, second):
         return jax.tree.map(by_section, tuple(first), tuple(second))
 
-    def final(zero, one):
-        return own_layer(to_core(0, zero), to_core(1, one))
-
-    flag = jnp.reshape(section, (1,)).astype(jnp.int32)
-    gate_up_0, gate_up_1 = to_core(0, gate_up_0), to_core(1, gate_up_1)
+    gate_up_0 = to_core(0, gate_up_0)
     final_gate = settle(flag, gate_up_0[:1], gate_up_1[:1], units)
     final_up = settle(flag, gate_up_0[1:], gate_up_1[1:], units)
-    final_down = settle(flag, to_core(0, down_0), to_core(1, down_1), units)
-    attn_0, final_gate, final_up, final_down = after(attn_0, final_gate, final_up, final_down)
-    final_query, final_out = final(attn_0[:, :query_cols], attn_1[:, :query_cols])
+    attn_0, final_gate, final_up = after(attn_0, final_gate, final_up)
+    final_query, final_out = own_layer(to_core(0, attn_0[:, :query_cols]), attn_1_out)
     final_keyval = by_section(attn_0[:, query_cols:], attn_1[:, query_cols:]).astype(F32)
 
     gain_grads_0 = jnp.stack([gain_attn_0, gain_ffn_0])

time: 1170 us -> 1120 us (0.957)
  waiting for transfers between devices: 706 us -> 631 us
    reduce_scatter x6, waiting for transfers between devices: 223 us -> 160 us  [scatter_rows(): return lax.psum_scatter(total, ROW, scatter_dimension=0, tiled=True)]
    ppermute x77, waiting for transfers between devices: 239 us -> 224 us  [over_col(): return lax.ppermute(block, 'col', [(i, i ^ step) for i in range(count)])]
  transfers between devices with their start and end apart: 124 -> 124, of which waited for: 78 -> 72; matrix products, arithmetic and copies ran while one was open for 17% -> 20% of each run, Pallas kernels for 4% -> 4%
where the time goes in v6:
time: 1120 us; the launch traced here: 1110 us
  waiting for transfers between devices  631 us (56%)
  matrix products  169 us (15%)
  starting transfers between devices  151 us (13%)
  other arithmetic  50.8 us (5%)
  Pallas kernels  49.3 us (4%)
  local copies, waits for them, and re-layouts  39.9 us (4%)
  between operations  16.6 us (1%)
    ppermute x77, waiting for transfers between devices, over_col(): return lax.ppermute(block, 'col', [(i, i ^ step) for i in range(count)])  224 us
    dot_general x38, matrix products, dot(): lax.dot_general(left, right, (((left_dim,), (right_dim,)), ((), ())), pre...  169 us
    reduce_scatter x6, waiting for transfers between devices, scatter_rows(): return lax.psum_scatter(total, ROW, scatter_dimension=0, tiled=True)  160 us
    all_gather x3, waiting for transfers between devices, gather_layers(): return lax.all_gather(part, ('section', ROW), axis=0, tiled=True)  128 us
    ppermute x77, starting transfers between devices, over_col(): return lax.ppermute(block, 'col', [(i, i ^ step) for i in range(count)])  97.5 us
    ppermute x12, waiting for transfers between devices, along_row(): return lax.ppermute(block, ROW, route)  65.2 us
    ppermute x12, starting transfers between devices, along_row(): return lax.ppermute(block, ROW, route)  26.1 us
    all_gather x1, waiting for transfers between devices, gather_attn(): return lax.all_gather(part, (ROW, 'section'), axis=0, tiled=True)  24 us
  transfers between devices with their start and end apart: 124, of which 72 were waited for; matrix products, arithmetic and copies ran while one was open for 20% of the time, Pallas kernels for 4%

profile of v6, /device:TPU:0, one launch (start us, length us, event | category | flops | bytes accessed | tf_op | source)
XLA Modules:
  0.0 1108.4 jit_solution(12414378877971198975)
XLA Ops:
  49.4 24.0 %all-gather.5.cloned.1.call-done.w_ref = bf16[1536,1792]{1,0:T(8,128)(2,1)} async-done(((bf16[192,1792]{1,0:T(8,128)(2,1)}), bf16[1536,1792]{1,0:T(8,128)(2,1)}) %all-gather.5.cloned.1.call-update) | async-done | bytes 5505040 | tf_op jit(solution)/shard_map/all_gather | solution.py:506
  98.7 8.2 collective-permute-done.12.refs_4_
  118.8 9.4 collective-permute-done.14
  136.6 8.0 collective-permute-done.17
  152.0 109.8 %all-gather.7.cloned.1.call-done = bf16[3072,3456]{0,1:T(8,128)(2,1)} async-done(((bf16[384,3456]{0,1:T(8,128)(2,1)}), bf16[3072,3456]{0,1:T(8,128)(2,1)}) %all-gather.7.cloned.1.call-update) | async-done | bytes 21233680 | tf_op jit(solution)/shard_map/all_gather | solution.py:496
  268.0 10.2 multiply_convert_fusion.1
  291.5 9.4 collective-permute-done.23
  301.0 7.8 collective-permute-done.24
  312.0 8.1 collective-permute-done.26
  359.6 9.5 collective-permute-done.33.refs_4_
  390.4 8.1 collective-permute-done.40
  408.1 7.6 collective-permute-done.37
  430.7 10.8 multiply_convert_fusion
  460.9 18.5 %all-gather.9.cloned.1.call-done = bf16[3072,1152]{0,1:T(8,128)(2,1)} async-done(((bf16[384,1152]{0,1:T(8,128)(2,1)}), bf16[3072,1152]{0,1:T(8,128)(2,1)}) %all-gather.9.cloned.1.call-update) | async-done | bytes 7077904 | tf_op jit(solution)/shard_map/all_gather | solution.py:496
  491.0 9.2 convolution_convert_fusion.1
  536.6 9.2 add_convert_fusion.1
  585.3 7.6 attend_back.2
  599.9 9.8 collective-permute-done.58
  614.9 11.8 %collective-permute-done.59 = bf16[512,128]{1,0:T(8,128)(2,1)S(1)} collective-permute-done((bf16[512,128]{1,0:T(8,128)(2,1)S(1)}, bf16[512,128]{1,0:T(8,128)(2,1)S(1)}, u32[]{:S(2)}, u32[]{:S(2)}) %collective-permute-start.59) | collective-permute-done | bytes 131104 | tf_op jit(solution)/shard_map/ppermute | solution.py:53
  626.7 9.5 collective-permute-done.60
  645.9 9.3 collective-permute-done.71
  655.2 7.8 collective-permute-done.72
  668.7 8.1 collective-permute-done.75
  715.5 11.5 %collective-permute-done.80 = bf16[1536,2304]{1,0:T(8,128)(2,1)} collective-permute-done((bf16[1536,2304]{1,0:T(8,128)(2,1)}, bf16[1536,2304]{1,0:T(8,128)(2,1)}, u32[]{:S(2)}, u32[]{:S(2)}) %collective-permute-start.80) | collective-permute-done | bytes 7077920 | tf_op jit(solution)/shard_map/ppermute | solution.py:47
  727.1 10.4 add_convert_fusion
  755.9 9.4 collective-permute-done.81
  765.4 7.8 collective-permute-done.82
  782.8 104.0 %reduce-scatter.11.cloned.1.call-done.refs_1_ = bf16[384,2304]{1,0:T(8,128)(2,1)} async-done(((bf16[1536,2304]{1,0:T(8,128)(2,1)}), bf16[384,2304]{1,0:T(8,128)(2,1)}) %reduce-scatter.11.cloned.1.call-update) | async-done | bytes 1769488 | tf_op jit(solution)/shard_map/reduce_scatter | solution.py:556
  901.1 7.7 attend_back.3
  937.2 21.9 %collective-permute-done.90 = bf16[512,128]{1,0:T(8,128)(2,1)} collective-permute-done((bf16[512,128]{1,0:T(8,128)(2,1)}, bf16[512,128]{1,0:T(8,128)(2,1)}, u32[]{:S(2)}, u32[]{:S(2)}) %collective-permute-start.90) | collective-permute-done | bytes 131104 | tf_op jit(solution)/shard_map/ppermute | solution.py:53
  976.3 15.1 %collective-permute-done.100 = bf16[128,1536]{1,0:T(8,128)(2,1)S(1)} collective-permute-done((bf16[128,1536]{1,0:T(8,128)(2,1)}, bf16[128,1536]{1,0:T(8,128)(2,1)S(1)}, u32[]{:S(2)}, u32[]{:S(2)}) %collective-permute-start.100) | collective-permute-done | bytes 393248 | tf_op jit(solution)/shard_map/ppermute | solution.py:43
  999.0 55.1 %reduce-scatter.17.cloned.1.call-done.refs_0_ = bf16[384,2304]{1,0:T(8,128)(2,1)} async-done(((bf16[1536,2304]{1,0:T(8,128)(2,1)}), bf16[384,2304]{1,0:T(8,128)(2,1)}) %reduce-scatter.17.cloned.1.call-update) | async-done | bytes 1769488 | tf_op jit(solution)/shard_map/reduce_scatter | solution.py:556
  (647 shorter events, 516.9 us)
Async XLA Ops:
  7.2 66.2 %all-gather.5.cloned.1.call-start = ((), (), s32[]{:S(2)}) async-start(), calls=%async_computation.6 | async-start | bytes 6193152 | tf_op jit(solution)/shard_map/all_gather | solution.py:506
  12.5 249.3 %all-gather.7.cloned.1.call-start = ((), (), s32[]{:S(2)}) async-start(), calls=%async_computation.7 | async-start | bytes 23887872 | tf_op jit(solution)/shard_map/all_gather | solution.py:496
  24.3 399.4 %all-gather.11.cloned.1.call-start = ((), (), s32[]{:S(2)}) async-start(), calls=%async_computation.9 | async-start | bytes 15925248 | tf_op jit(solution)/shard_map/all_gather | solution.py:496
  133.2 346.2 %all-gather.9.cloned.1.call-start = ((), (), s32[]{:S(2)}) async-start(), calls=%async_computation.8 | async-start | bytes 7962624 | tf_op jit(solution)/shard_map/all_gather | solution.py:496
  347.0 431.5 %reduce-scatter.9.cloned.1.call-start = ((), (), s32[]{:S(2)}) async-start(), calls=%async_computation.11 | async-start | bytes 4423680 | tf_op jit(solution)/shard_map/reduce_scatter | solution.py:556
  382.5 24.4 %collective-permute-start.35 = (bf16[512,384]{1,0:T(8,128)(2,1)S(1)}, bf16[512,384]{1,0:T(8,128)(2,1)S(1)}, u32[]{:S(2)}, u32[]{:S(2)}) collective-permute-start(bf16[512,384]{1,0:T(8,128)(2,1)S(1)} %get-tuple-element.240), channel_id=1, source_target_pairs={{0,1},{1,0},{2,3},{3,2},{4,5},{5,4},{6,7},{7,6},{8,9},{9,8},{10,11... | collective-permute-start | bytes 1179656 | tf_op jit(solution)/shard_map/ppermute | solution.py:43
  384.0 19.9 %collective-permute-start.36 = (bf16[512,384]{1,0:T(8,128)(2,1)S(1)}, bf16[512,384]{1,0:T(8,128)(2,1)S(1)}, u32[]{:S(2)}, u32[]{:S(2)}) collective-permute-start(bf16[512,384]{1,0:T(8,128)(2,1)S(1)} %get-tuple-element.240), channel_id=1, source_target_pairs={{0,2},{1,3},{2,0},{3,1},{4,6},{5,7},{6,4},{7,5},{8,10},{9,11},{10,... | collective-permute-start | bytes 1179656 | tf_op jit(solution)/shard_map/ppermute | solution.py:43
  500.1 36.5 %collective-permute-start.53 = (bf16[1536,2304]{1,0:T(8,128)(2,1)}, bf16[1536,2304]{1,0:T(8,128)(2,1)}, u32[]{:S(2)}, u32[]{:S(2)}) collective-permute-start(bf16[1536,2304]{1,0:T(8,128)(2,1)} %convolution_convert_fusion.1), channel_id=1, source_target_pairs={{0,16},{16,0},{1,17},{17,1},{2,18},{18,2},{3,19},{19,3},{4,20},{20... | collective-permute-start | bytes 21233672 | tf_op jit(solution)/shard_map/ppermute | solution.py:47
  524.5 21.4 %collective-permute-start.63 = (bf16[128,1536]{1,0:T(8,128)(2,1)}, bf16[128,1536]{1,0:T(8,128)(2,1)}, u32[]{:S(2)}, u32[]{:S(2)}) collective-permute-start(bf16[128,1536]{1,0:T(8,128)(2,1)} %get-tuple-element.187), channel_id=1, source_target_pairs={{0,3},{1,2},{2,1},{3,0},{4,7},{5,6},{6,5},{7,4},{8,11},{9,10},{10,... | collective-permute-start | bytes 1179656 | tf_op jit(solution)/shard_map/ppermute | solution.py:43
  527.4 24.8 %collective-permute-start.64 = (bf16[128,1536]{1,0:T(8,128)(2,1)S(1)}, bf16[128,1536]{1,0:T(8,128)(2,1)}, u32[]{:S(2)}, u32[]{:S(2)}) collective-permute-start(bf16[128,1536]{1,0:T(8,128)(2,1)S(1)} %get-tuple-element.189), channel_id=1, source_target_pairs={{0,1},{1,0},{2,3},{3,2},{4,5},{5,4},{6,7},{7,6},{8,9},{9,8},{10,11... | collective-permute-start | bytes 1179656 | tf_op jit(solution)/shard_map/ppermute | solution.py:43
  561.4 220.0 %reduce-scatter.7.cloned.1.call-start = ((), (), s32[]{:S(2)}) async-start(), calls=%async_computation.10 | async-start | bytes 4423680 | tf_op jit(solution)/shard_map/reduce_scatter | solution.py:556
  578.5 20.3 %collective-permute-start.70 = (bf16[512,384]{1,0:T(8,128)(2,1)}, bf16[512,384]{1,0:T(8,128)(2,1)}, u32[]{:S(2)}, u32[]{:S(2)}) collective-permute-start(bf16[512,384]{1,0:T(8,128)(2,1)} %get-tuple-element.229), channel_id=1, source_target_pairs={{16,0},{17,1},{18,2},{19,3},{20,4},{21,5},{22,6},{23,7},{24,8},{25... | collective-permute-start | bytes 1179656 | tf_op jit(solution)/shard_map/ppermute | solution.py:622
  597.2 39.1 %collective-permute-start.62 = (bf16[1536,384]{1,0:T(8,128)(2,1)S(1)}, bf16[1536,384]{1,0:T(8,128)(2,1)S(1)}, u32[]{:S(2)}, u32[]{:S(2)}) collective-permute-start(bf16[1536,384]{1,0:T(8,128)(2,1)S(1)} %get-tuple-element.285), channel_id=1, source_target_pairs={{0,16},{16,0},{1,17},{17,1},{2,18},{18,2},{3,19},{19,3},{4,20},{20... | collective-permute-start | bytes 3538952 | tf_op jit(solution)/shard_map/ppermute | solution.py:47
  611.2 25.0 %collective-permute-start.60 = (bf16[512,128]{1,0:T(8,128)(2,1)S(1)}, bf16[512,128]{1,0:T(8,128)(2,1)S(1)}, u32[]{:S(2)}, u32[]{:S(2)}) collective-permute-start(bf16[512,128]{1,0:T(8,128)(2,1)S(1)} %get-tuple-element.221), channel_id=1, source_target_pairs={{8,0},{12,4},{9,1},{13,5},{10,2},{14,6},{11,3},{15,7},{24,16},{28,... | collective-permute-start | bytes 393224 | tf_op jit(solution)/shard_map/ppermute | solution.py:53
  612.5 23.7 %collective-permute-start.61 = (bf16[512,128]{1,0:T(8,128)(2,1)S(1)}, bf16[512,128]{1,0:T(8,128)(2,1)S(1)}, u32[]{:S(2)}, u32[]{:S(2)}) collective-permute-start(bf16[512,128]{1,0:T(8,128)(2,1)S(1)} %get-tuple-element.220), channel_id=1, source_target_pairs={{12,0},{13,1},{14,2},{15,3},{28,16},{29,17},{30,18},{31,19}} | collective-permute-start | bytes 393224 | tf_op jit(solution)/shard_map/ppermute | solution.py:53
  696.8 190.0 %reduce-scatter.11.cloned.1.call-start = ((), (), s32[]{:S(2)}) async-start(), calls=%async_computation.12 | async-start | bytes 8847360 | tf_op jit(solution)/shard_map/reduce_scatter | solution.py:556
  697.5 229.9 %reduce-scatter.13.cloned.1.call-start = ((), (), s32[]{:S(2)}) async-start(), calls=%async_computation.13 | async-start | bytes 1966080 | tf_op jit(solution)/shard_map/reduce_scatter | solution.py:556
  715.5 338.7 %reduce-scatter.17.cloned.1.call-start = ((), (), s32[]{:S(2)}) async-start(), calls=%async_computation.15 | async-start | bytes 8847360 | tf_op jit(solution)/shard_map/reduce_scatter | solution.py:556
  737.5 357.0 %reduce-scatter.15.cloned.1.call-start = ((), (), s32[]{:S(2)}) async-start(), calls=%async_computation.14 | async-start | bytes 1966080 | tf_op jit(solution)/shard_map/reduce_scatter | solution.py:556
  775.3 114.4 %collective-permute-start.84 = (bf16[128,1536]{1,0:T(8,128)(2,1)S(1)}, bf16[128,1536]{1,0:T(8,128)(2,1)S(1)}, u32[]{:S(2)}, u32[]{:S(2)}) collective-permute-start(bf16[128,1536]{1,0:T(8,128)(2,1)S(1)} %get-tuple-element.145), channel_id=1, source_target_pairs={{0,1},{1,0},{2,3},{3,2},{4,5},{5,4},{6,7},{7,6},{8,9},{9,8},{10,11... | collective-permute-start | bytes 1179656 | tf_op jit(solution)/shard_map/ppermute | solution.py:43
  776.7 114.6 %collective-permute-start.85 = (bf16[128,1536]{1,0:T(8,128)(2,1)S(1)}, bf16[128,1536]{1,0:T(8,128)(2,1)S(1)}, u32[]{:S(2)}, u32[]{:S(2)}) collective-permute-start(bf16[128,1536]{1,0:T(8,128)(2,1)S(1)} %get-tuple-element.145), channel_id=1, source_target_pairs={{0,2},{1,3},{2,0},{3,1},{4,6},{5,7},{6,4},{7,5},{8,10},{9,11},{10,... | collective-permute-start | bytes 1179656 | tf_op jit(solution)/shard_map/ppermute | solution.py:43
  778.5 144.9 %collective-permute-start.94 = (bf16[384,1152]{1,0:T(8,128)(2,1)}, bf16[384,1152]{1,0:T(8,128)(2,1)}, u32[]{:S(2)}, u32[]{:S(2)}) collective-permute-start(bf16[384,1152]{1,0:T(8,128)(2,1)} %reduce-scatter.9.cloned.1.call-done.refs_3_), channel_id=1, source_target_pairs={{0,16},{1,17},{2,18},{3,19},{4,20},{5,21},{6,22},{7,23},{8,24},{9,... | collective-permute-start | bytes 2654216 | tf_op jit(solution)/shard_map/ppermute | solution.py:630
  781.5 143.2 %collective-permute-start.93 = (bf16[384,1152]{1,0:T(8,128)(2,1)}, bf16[384,1152]{1,0:T(8,128)(2,1)}, u32[]{:S(2)}, u32[]{:S(2)}) collective-permute-start(bf16[384,1152]{1,0:T(8,128)(2,1)} %reduce-scatter.7.cloned.1.call-done.refs_0_), channel_id=1, source_target_pairs={{16,0},{17,1},{18,2},{19,3},{20,4},{21,5},{22,6},{23,7},{24,8},{25... | collective-permute-start | bytes 2654216 | tf_op jit(solution)/shard_map/ppermute | solution.py:630
  886.8 78.5 %collective-permute-start.95 = (bf16[384,2304]{1,0:T(8,128)(2,1)}, bf16[384,2304]{1,0:T(8,128)(2,1)}, u32[]{:S(2)}, u32[]{:S(2)}) collective-permute-start(bf16[384,2304]{1,0:T(8,128)(2,1)} %reduce-scatter.11.cloned.1.call-done.refs_1_), channel_id=1, source_target_pairs={{0,16},{1,17},{2,18},{3,19},{4,20},{5,21},{6,22},{7,23},{8,24},{9,... | collective-permute-start | bytes 5308424 | tf_op jit(solution)/shard_map/ppermute | solution.py:630
  915.0 46.8 %collective-permute-start.92 = (bf16[1536,384]{1,0:T(8,128)(2,1)}, bf16[1536,384]{1,0:T(8,128)(2,1)}, u32[]{:S(2)}, u32[]{:S(2)}) collective-permute-start(bf16[1536,384]{1,0:T(8,128)(2,1)} %get-tuple-element.287), channel_id=1, source_target_pairs={{0,16},{16,0},{1,17},{17,1},{2,18},{18,2},{3,19},{19,3},{4,20},{20... | collective-permute-start | bytes 3538952 | tf_op jit(solution)/shard_map/ppermute | solution.py:47
  923.4 35.7 %collective-permute-start.90 = (bf16[512,128]{1,0:T(8,128)(2,1)}, bf16[512,128]{1,0:T(8,128)(2,1)}, u32[]{:S(2)}, u32[]{:S(2)}) collective-permute-start(bf16[512,128]{1,0:T(8,128)(2,1)} %get-tuple-element.218), channel_id=1, source_target_pairs={{8,0},{12,4},{9,1},{13,5},{10,2},{14,6},{11,3},{15,7},{24,16},{28,... | collective-permute-start | bytes 393224 | tf_op jit(solution)/shard_map/ppermute | solution.py:53
  924.7 35.9 %collective-permute-start.91 = (bf16[512,128]{1,0:T(8,128)(2,1)}, bf16[512,128]{1,0:T(8,128)(2,1)}, u32[]{:S(2)}, u32[]{:S(2)}) collective-permute-start(bf16[512,128]{1,0:T(8,128)(2,1)} %get-tuple-element.217), channel_id=1, source_target_pairs={{12,0},{13,1},{14,2},{15,3},{28,16},{29,17},{30,18},{31,19}} | collective-permute-start | bytes 393224 | tf_op jit(solution)/shard_map/ppermute | solution.py:53
  935.8 28.0 %collective-permute-start.97 = (bf16[512,384]{1,0:T(8,128)(2,1)S(1)}, bf16[512,384]{1,0:T(8,128)(2,1)S(1)}, u32[]{:S(2)}, u32[]{:S(2)}) collective-permute-start(bf16[512,384]{1,0:T(8,128)(2,1)S(1)} %pad_maximum_fusion.13), channel_id=1, source_target_pairs={{0,16},{1,17},{2,18},{3,19},{4,20},{5,21},{6,22},{7,23},{8,24},{9,... | collective-permute-start | bytes 1179656 | tf_op jit(solution)/shard_map/ppermute | solution.py:622
  971.4 20.1 %collective-permute-start.100 = (bf16[128,1536]{1,0:T(8,128)(2,1)}, bf16[128,1536]{1,0:T(8,128)(2,1)S(1)}, u32[]{:S(2)}, u32[]{:S(2)}) collective-permute-start(bf16[128,1536]{1,0:T(8,128)(2,1)} %get-tuple-element.175), channel_id=1, source_target_pairs={{0,2},{1,3},{2,0},{3,1},{4,6},{5,7},{6,4},{7,5},{8,10},{9,11},{10,... | collective-permute-start | bytes 1179656 | tf_op jit(solution)/shard_map/ppermute | solution.py:43
  971.5 20.0 %collective-permute-start.98 = (bf16[128,1536]{1,0:T(8,128)(2,1)}, bf16[128,1536]{1,0:T(8,128)(2,1)}, u32[]{:S(2)}, u32[]{:S(2)}) collective-permute-start(bf16[128,1536]{1,0:T(8,128)(2,1)} %get-tuple-element.174), channel_id=1, source_target_pairs={{0,3},{1,2},{2,1},{3,0},{4,7},{5,6},{6,5},{7,4},{8,11},{9,10},{10,... | collective-permute-start | bytes 1179656 | tf_op jit(solution)/shard_map/ppermute | solution.py:43
  997.3 58.1 %collective-permute-start.106 = (f32[2,1536]{1,0:T(2,128)}, f32[2,1536]{1,0:T(2,128)}, u32[]{:S(2)}, u32[]{:S(2)}) collective-permute-start(f32[2,1536]{1,0:T(2,128)} %broadcast_select_fusion.13), channel_id=1, source_target_pairs={{0,16},{16,0},{1,17},{17,1},{2,18},{18,2},{3,19},{19,3},{4,20},{20... | collective-permute-start | bytes 36872 | tf_op jit(solution)/shard_map/ppermute | solution.py:47
  1054.1 33.3 %collective-permute-start.112 = (bf16[384,2304]{1,0:T(8,128)(2,1)}, bf16[384,2304]{1,0:T(8,128)(2,1)S(1)}, u32[]{:S(2)}, u32[]{:S(2)}) collective-permute-start(bf16[384,2304]{1,0:T(8,128)(2,1)} %reduce-scatter.17.cloned.1.call-done.refs_0_), channel_id=1, source_target_pairs={{16,0},{17,1},{18,2},{19,3},{20,4},{21,5},{22,6},{23,7},{24,8},{25... | collective-permute-start | bytes 5308424 | tf_op jit(solution)/shard_map/ppermute | solution.py:630
  (183 other events, 2283.4 us)
Sparse Core Ops, SparseCore 0:
  12.6 60.7 all-gather.4
  75.6 186.1 all-gather.6
  264.0 136.5 all-gather.10
  402.1 77.2 all-gather.8
  561.6 66.5 reduce-scatter.8
  696.9 63.8 reduce-scatter.6
  763.1 123.6 reduce-scatter.10
  889.1 35.9 reduce-scatter.12
  927.4 126.7 reduce-scatter.16
  1056.3 38.1 reduce-scatter.14
